TPU v7x, 32 devices: a whole 2x2x4 slice. The times are simulated.
32 devices in a mesh: seg: 4 (over y, x), doc: 8 (over z, core).
Axes of the slice: x: 2, y: 2, z: 4, core: 2. Of those that a mesh axis runs over, the one named last changes fastest.
Arguments:
- tokens: bfloat16 [16, 512, 768], P('doc', 'seg'), may hold values from -6 to 6
- new_doc: int32 [16], P('doc'), may hold values from 0 to 1, as said below
- valid_len: int32 [16], P('doc'), may hold values from 1 to 512, as said below
- mem_init: bfloat16 [16, 768], replicated, may hold values from -6 to 6
- query_proj: bfloat16 [768, 768], replicated, may hold values from -0.21875 to 0.21875
- query_bias: float32 [768], replicated, may hold values from -3 to 3
- key_proj: bfloat16 [768, 768], replicated, may hold values from -0.21875 to 0.21875
- value_proj: bfloat16 [768, 768], replicated, may hold values from -0.21875 to 0.21875
- value_bias: float32 [768], replicated, may hold values from -3 to 3
- output_proj: bfloat16 [768, 768], replicated, may hold values from -1.75 to 1.75
- output_bias: float32 [768], replicated, may hold values from -2 to 2
- attn_gain: float32 [768], replicated, may hold values from 0.5 to 1.5
- attn_shift: float32 [768], replicated, may hold values from -2 to 2
- expand_proj: bfloat16 [768, 3072], replicated, may hold values from -0.21875 to 0.21875
- expand_bias: float32 [3072], replicated, may hold values from -2 to 2
- reduce_proj: bfloat16 [3072, 768], replicated, may hold values from -0.109375 to 0.109375
- reduce_bias: float32 [768], replicated, may hold values from -2 to 2
- final_gain: float32 [768], replicated, may hold values from 0.5 to 1.5
- final_shift: float32 [768], replicated, may hold values from -2 to 2
- d_out: bfloat16 [16, 512, 768], P('doc', 'seg'), may hold values from -6 to 6
Outputs:
- layer_out: bfloat16 [16, 512, 768], P('doc', 'seg')
- grad_tokens: bfloat16 [16, 512, 768], P('doc', 'seg')
- grad_mem: float32 [16, 768], P(None, ('seg', 'doc'))
- grad_query_proj: float32 [768, 768], P(('seg', 'doc'))
- grad_query_bias: float32 [768], P(('seg', 'doc'))
- grad_key_proj: float32 [768, 768], P(('seg', 'doc'))
- grad_value_proj: float32 [768, 768], P(('seg', 'doc'))
- grad_value_bias: float32 [768], P(('seg', 'doc'))
- grad_output_proj: float32 [768, 768], P(('seg', 'doc'))
- grad_output_bias: float32 [768], P(('seg', 'doc'))
- grad_attn_gain: float32 [768], P(('seg', 'doc'))
- grad_attn_shift: float32 [768], P(('seg', 'doc'))
- grad_expand_proj: float32 [768, 3072], P(('seg', 'doc'))
- grad_expand_bias: float32 [3072], P(('seg', 'doc'))
- grad_reduce_proj: float32 [3072, 768], P(('seg', 'doc'))
- grad_reduce_bias: float32 [768], P(('seg', 'doc'))
- grad_final_gain: float32 [768], P(('seg', 'doc'))
- grad_final_shift: float32 [768], P(('seg', 'doc'))
Inputs may be any that keep to these rules, and one draw needn't show every extreme that they name: `new_doc`: the first of every 2 consecutive segments starts a document. `valid_len`: 512 for every segment that is not the last of its document.
All inputs are finite; a program needn't handle non-finite values.
Results may differ from a plain program's by a relative error of at most 0.02.
Values may be sent and summed in bfloat16 or wider, within the bound.
No kernel may reach another device: no remote copies, remote signals or barrier semaphores. Data moves between devices by JAX's collectives and lax.ppermute only.
A program may use at most 192 MiB of HBM per device.

v0:
```python
import functools

import jax
import jax.numpy as jnp
from jax import lax
from jax.experimental import pallas as pl
from jax.experimental.pallas import tpu as pltpu
from jax.sharding import PartitionSpec as P

HEADS = 12


EPS = 1e-12
NEG_FILL = -1e30
F32 = jnp.float32
BF16 = jnp.bfloat16
NN = (((1,), (0,)), ((), ()))
NT = (((1,), (1,)), ((), ()))
TN = (((0,), (0,)), ((), ()))

Q_B, V_B, OUT_B, ATTN_G, ATTN_S, RED_B, FIN_G, FIN_S, EXP_B = range(9)
FRESH, VALID = 1, 2
N_VEC = 16
N_SMALL = 32


def mm(left, right, dims=NN):
    return lax.dot_general(left, right, dims, preferred_element_type=F32)


def swap(block, axis, mask):
    return lax.ppermute(block, axis, [(i, i ^ mask) for i in range(lax.axis_size(axis))])


def seg_here():
    return lax.axis_index("seg")


def core_here():
    return lax.axis_index("doc") & 1


def pair_here():
    return lax.axis_index("doc") >> 1


def shape_of(*dims, dtype=BF16):
    return jax.ShapeDtypeStruct(dims, dtype)


def call(kernel, out_shape, args, micros, far_in=(), far_out=(), scratch=()):
    vmem, far = pl.BlockSpec(memory_space=pltpu.VMEM), pl.BlockSpec(memory_space=pltpu.HBM)
    near = [
        x if i == 0 else pltpu.with_memory_space_constraint(x, pltpu.HBM if i in far_in else pltpu.VMEM)
        for i, x in enumerate(args)
    ]
    return pl.pallas_call(
        kernel,
        out_shape=[o if i in far_out else pltpu.VMEM(o.shape, o.dtype) for i, o in enumerate(out_shape)],
        in_specs=[pl.BlockSpec(memory_space=pltpu.SMEM)]
        + [far if i in far_in else vmem for i in range(1, len(args))],
        out_specs=[vmem] * len(out_shape),
        scratch_shapes=scratch,
        compiler_params=pltpu.CompilerParams(vmem_limit_bytes=8 << 20),
        cost_estimate=pl.CostEstimate(flops=0, transcendentals=0, bytes_accessed=int(micros * 3e6)),
    )(*near)


def reorder(x, seg, n_seg):
    width = x.shape[1] // n_seg
    bit = 1
    while bit < n_seg:
        moved = jnp.concatenate([x[:, (b ^ bit) * width : ((b ^ bit) + 1) * width] for b in range(n_seg)], axis=1)
        x = jnp.where((seg & bit) != 0, moved, x)
        bit *= 2
    return x


def in_loop(count, together, step):
    def some(j, carry):
        for k in range(together):
            step(j * together + k)
        return carry

    lax.fori_loop(0, count // together, some, 0)


def own_columns(x, seg, n_seg):
    width = x.shape[1] // n_seg
    out = x[:, :width]
    for b in range(1, n_seg):
        out = jnp.where(seg == b, x[:, b * width : (b + 1) * width], out)
    return out


def prep_kernel(meta_ref, wq_ref, wk_ref, wv_ref, *refs, n_seg, chunks):
    vec_refs, (w_ref, b_ref, out_ref, line_ref, sems) = refs[: EXP_B + 1], refs[EXP_B + 1 :]
    copies = [pltpu.make_async_copy(r, out_ref.at[i], sems.at[i]) for i, r in enumerate(vec_refs[:EXP_B])]
    copies.append(pltpu.make_async_copy(vec_refs[EXP_B], line_ref.at[0], sems.at[EXP_B]))
    for c in copies:
        c.start()
    seg = seg_here()
    rows = w_ref.shape[0] // 8

    def some_rows(i):
        these = pl.ds(pl.multiple_of(i * rows, rows), rows)
        w_ref[these] = jnp.concatenate([own_columns(r[these], seg, n_seg) for r in (wq_ref, wk_ref, wv_ref)], axis=1)

    in_loop(8, 1, some_rows)
    for c in copies:
        c.wait()
    wide = out_ref.shape[1]
    for q in range(chunks):
        out_ref[EXP_B + q : EXP_B + q + 1] = line_ref[:, q * wide : (q + 1) * wide]
    q_b = own_columns(out_ref[Q_B : Q_B + 1], seg, n_seg)
    v_b = own_columns(out_ref[V_B : V_B + 1], seg, n_seg)
    b_ref[...] = jnp.concatenate([q_b, jnp.zeros_like(q_b), v_b], axis=1)


def qkv_kernel(meta_ref, w_ref, b_ref, *refs):
    rows, out_ref = refs[:-1], refs[-1]
    size = rows[0].shape[0]
    for b, r in enumerate(rows):
        out_ref[b * size : (b + 1) * size, :] = (mm(r[...], w_ref[...]) + b_ref[...]).astype(BF16)


def mask_block(meta_ref, slot, blocks, size, mem, width):
    total = blocks * size + 2 * mem
    row = lax.broadcasted_iota(jnp.int32, (total, width), 0)
    col = lax.broadcasted_iota(jnp.int32, (total, width), 1)
    place = row
    for b in range(blocks):
        inside = (row >= b * size) & (row < (b + 1) * size)
        place = jnp.where(inside, ((seg_here() ^ b) - b) * size + row, place)
    out = (place >= meta_ref[VALID + slot]) & (row < blocks * size) & (col == 0)
    return jnp.where(out, NEG_FILL, 0.0).astype(BF16)


def ones_block(rows, width):
    col = lax.broadcasted_iota(jnp.int32, (rows, width), 1)
    return jnp.where(col == 0, 1.0, 0.0).astype(BF16)


def with_memory(rows, memory):
    return jnp.concatenate([rows, memory, memory], axis=0)


SCALE = 0.125 * 1.4426950408889634


def attn_fwd_kernel(meta_ref, qkv_ref, mem_ref, w_ref, b_ref, *outs, slot, blocks, heads, mem_queries):
    if mem_queries:
        memory = mem_ref[...]
    else:
        written_ref, outs = outs[0], outs[1:]
        memory = jnp.where(meta_ref[FRESH] == 1, mem_ref[...], written_ref[...].astype(BF16))
        outs[-1][...] = memory
    mix_refs, lse_ref, mem_out_ref = outs[:blocks], outs[blocks], outs[blocks + 1]
    size = qkv_ref.shape[0] // blocks
    mem = mem_ref.shape[0]
    width = qkv_ref.shape[1] // 3
    head_dim = width // heads
    mem_out_ref[...] = (mm(memory, w_ref[...]) + b_ref[...]).astype(BF16)
    mask = mask_block(meta_ref, slot, blocks, size, mem, head_dim)
    ones = ones_block(size, head_dim)
    value_t = with_memory(qkv_ref[:, 2 * width :], mem_out_ref[:, 2 * width :]).T
    keys = []
    for h in range(heads):
        cols = slice(width + h * head_dim, width + (h + 1) * head_dim)
        keys.append(jnp.concatenate([with_memory(qkv_ref[:, cols], mem_out_ref[:, cols]), mask], axis=1))

    def mixed_of(queries, ones, first):
        out = []
        for h in range(heads):
            lo, hi = h * head_dim, (h + 1) * head_dim
            scores = mm(keys[h], jnp.concatenate([queries[:, lo:hi], ones], axis=1), NT)
            highest = jnp.max(scores, axis=0, keepdims=True)
            weights = jnp.exp2((scores - highest) * SCALE)
            total = jnp.sum(weights, axis=0, keepdims=True)
            out.append(mm(value_t[lo:hi], weights.astype(BF16)) * (1.0 / total))
            lse_ref[h : h + 1, first : first + queries.shape[0]] = highest * SCALE + jnp.log(total) * 1.4426950408889634
        return jnp.concatenate(out, axis=0).T.astype(BF16)

    for b in range(blocks):
        mix_refs[b][:size] = mixed_of(qkv_ref[b * size : (b + 1) * size, :width], ones, b * size)
    if mem_queries:
        mixed = mixed_of(mem_out_ref[:, :width], ones[:mem], blocks * size)
        for b in range(blocks):
            mix_refs[b][size:] = mixed


def attn_bwd_kernel(meta_ref, qkv_ref, mem_ref, lse_ref, *refs, slot, blocks, heads, mem_queries):
    n_grad = blocks + (1 if mem_queries else 0)
    grad_refs, refs = refs[:n_grad], refs[n_grad:]
    more_refs, out_refs, mem_out_ref = refs[: -blocks - 1], refs[-blocks - 1 : -1], refs[-1]
    for more_ref, out_ref in zip(more_refs, out_refs):
        out_ref[out_ref.shape[0] - more_ref.shape[0] :, :] = more_ref[...]
    size = qkv_ref.shape[0] // blocks
    mem = mem_ref.shape[0]
    width = qkv_ref.shape[1] // 3
    first = slot * width
    head_dim = width // heads
    own = blocks * size + mem
    mask = mask_block(meta_ref, slot, blocks, size, mem, head_dim)
    ones = ones_block(size, head_dim)
    key_t = with_memory(qkv_ref[:, width : 2 * width], mem_ref[:, width : 2 * width]).T
    grad_q = [[] for _ in range(n_grad)]
    for h in range(heads):
        lo, hi = h * head_dim, (h + 1) * head_dim
        key = with_memory(qkv_ref[:, width + lo : width + hi], mem_ref[:, width + lo : width + hi])
        key = jnp.concatenate([key, mask], axis=1)
        value = with_memory(qkv_ref[:, 2 * width + lo : 2 * width + hi], mem_ref[:, 2 * width + lo : 2 * width + hi])

        def one(query, ones, grad, lse):
            scores = mm(key, jnp.concatenate([query, ones], axis=1), NT)
            probs = jnp.exp2(scores * SCALE - lse)
            grad_probs = mm(value, grad, NT)
            inner = jnp.sum(grad_probs * probs, axis=0, keepdims=True)
            return (probs * (grad_probs - inner)).astype(BF16), probs.astype(BF16)

        queries, grads, scores_g, probs = [], [], [], []
        for b in range(blocks):
            queries.append(qkv_ref[b * size : (b + 1) * size, lo:hi])
            grads.append(grad_refs[b][:, first + lo : first + hi])
            g, p = one(queries[b], ones, grads[b], lse_ref[h : h + 1, b * size : (b + 1) * size])
            scores_g.append(g)
            probs.append(p)
            grad_q[b].append(mm(key_t[lo:hi], g) * 0.125)
        grad_key = mm(jnp.concatenate([g[:own] for g in scores_g], axis=1), jnp.concatenate(queries, axis=0))
        grad_value = mm(jnp.concatenate([p[:own] for p in probs], axis=1), jnp.concatenate(grads, axis=0))
        if mem_queries:
            query, grad = mem_ref[:, lo:hi], grad_refs[blocks][:, lo:hi]
            g, p = one(query, ones[:mem], grad, lse_ref[h : h + 1, blocks * size : own])
            grad_q[blocks].append(mm(key_t[lo:hi], g) * 0.125)
            grad_key = grad_key + mm(g[:own], query)
            grad_value = grad_value + mm(p[:own], grad)
        grad_key = (grad_key * 0.125).astype(BF16)
        grad_value = grad_value.astype(BF16)
        for b in range(blocks):
            out_refs[b][:size, width + lo : width + hi] = grad_key[b * size : (b + 1) * size]
            out_refs[b][:size, 2 * width + lo : 2 * width + hi] = grad_value[b * size : (b + 1) * size]
        mem_out_ref[:, width + lo : width + hi] = grad_key[blocks * size :]
        mem_out_ref[:, 2 * width + lo : 2 * width + hi] = grad_value[blocks * size :]
    for b in range(blocks):
        out_refs[b][:size, :width] = jnp.concatenate(grad_q[b], axis=0).T.astype(BF16)
    if mem_queries:
        mem_out_ref[:, :width] = jnp.concatenate(grad_q[blocks], axis=0).T.astype(BF16)
    else:
        mem_out_ref[:, :width] = jnp.zeros((mem, width), BF16)


def norm_parts(hidden):
    center = hidden - jnp.mean(hidden, axis=-1, keepdims=True)
    inverse = lax.rsqrt(jnp.mean(center * center, axis=-1, keepdims=True) + EPS)
    return center * inverse, inverse


def norm_back(grad, gain, unit, inverse):
    scaled = grad * gain
    mean_scaled = jnp.mean(scaled, axis=-1, keepdims=True)
    mean_product = jnp.mean(scaled * unit, axis=-1, keepdims=True)
    return inverse * (scaled - mean_scaled - unit * mean_product)


def gelu_and_slope(pre):
    cdf = 0.5 * (1.0 + lax.erf(pre * (2.0**-0.5)))
    density = jnp.exp(-0.5 * pre * pre) * 0.3989422804014327
    return pre * cdf, cdf + pre * density


N_KEPT = 4


def rows_fwd_kernel(meta_ref, *refs, n_seg, n_pair, n_hidden):
    mix_refs, hid_refs = refs[:n_seg], refs[n_seg : n_seg + n_hidden]
    vec_ref, out_ref, exp_ref, red_ref = refs[n_seg + n_hidden : n_seg + n_hidden + 4]
    outs = refs[n_seg + n_hidden + 4 :]
    unit_a_ref, inv_ref, slope_ref, unit_f_ref = outs[:N_KEPT]
    result_refs, left_refs, acc_ref = outs[N_KEPT : N_KEPT + n_hidden], outs[N_KEPT + n_hidden : -1], outs[-1]
    wide = out_ref.shape[0]
    size = hid_refs[0].shape[0]

    def vec(i):
        return vec_ref[i : i + 1]

    def keep_left(x, at, first, blocks):
        left_factors(meta_ref, x, left_refs, at, first, blocks, n_seg, n_pair, size)

    each = wide // (n_seg * n_pair * 2)
    mixed = reorder(jnp.concatenate([r[...] for r in mix_refs], axis=1), seg_here(), n_seg)
    hidden = jnp.concatenate([r[...].astype(F32) for r in hid_refs], axis=0)
    unit, inverse = norm_parts(hidden + (mm(mixed, out_ref[...]) + vec(OUT_B)))
    unit_a_ref[...] = unit
    inv_ref[:, 0:1] = inverse
    normed = unit * vec(ATTN_G) + vec(ATTN_S)
    low = normed.astype(BF16)
    chunks = exp_ref.shape[1] // wide
    acc_ref[...] = normed + vec(RED_B)

    def chunk(q):
        cols = pl.ds(pl.multiple_of(q * wide, wide), wide)
        active, slope = gelu_and_slope(mm(low, exp_ref[:, cols]) + vec_ref[pl.ds(EXP_B + q, 1)])
        slope_ref[:, cols] = slope
        active = active.astype(BF16)
        acc_ref[...] += mm(active, red_ref[cols])
        keep_left(active, each, q * (n_seg // chunks), n_seg // chunks)

    in_loop(chunks, 2, chunk)
    unit, inverse = norm_parts(acc_ref[...])
    unit_f_ref[...] = unit
    inv_ref[:, 1:2] = inverse
    result = unit * vec(FIN_G) + vec(FIN_S)
    at = 0
    for r in result_refs:
        r[...] = result[at : at + r.shape[0]].astype(r.dtype)
        at += r.shape[0]
    keep_left(low, 0, 0, n_seg)
    keep_left(mixed, (chunks + 1) * each, 0, n_seg)


def left_factors(meta_ref, x, left_refs, at, first, blocks, n_seg, n_pair, size):
    seg, core, pair = seg_here(), core_here(), pair_here()
    rows = x.shape[1] // (blocks * n_pair * 2)
    keep_ref, send_ref = left_refs[:2]
    keep, send = core_halves(x[:size].astype(F32).T, core, n_pair, rows)
    for s in range(blocks):
        for z in range(n_pair):
            keep_ref[(first + s) ^ seg, z ^ pair, at : at + rows] = keep[s * n_pair + z]
            send_ref[(first + s) ^ seg, z ^ pair, at : at + rows] = send[s * n_pair + z]
    if left_refs[2:]:
        keep_ref, send_ref = left_refs[2:]
        mine = x[size:].astype(F32)
        if blocks > 1:
            assert blocks == n_seg
            mine = own_columns(mine, seg, n_seg)
        keep, send = core_halves(mine.T, core, n_pair, rows)

        @pl.when((seg == first) | (blocks > 1))
        def _():
            for z in range(n_pair):
                keep_ref[z ^ pair, at : at + rows] = keep[z]
                send_ref[z ^ pair, at : at + rows] = send[z]


def core_halves(x, core, pairs, rows):
    x = x.reshape(x.shape[0] // (2 * rows), 2, rows, x.shape[1])
    even, odd = x[:, 0], x[:, 1]
    return jnp.where(core == 0, even, odd).astype(BF16), jnp.where(core == 0, odd, even).astype(BF16)


def rows_back(seg, n_seg, grad, kept, vec_ref, out_ref, exp_ref, red_ref, outs, acc_ref, together):
    right_ref, hidden_ref, small_ref = outs
    wide = hidden_ref.shape[1]
    chunks = exp_ref.shape[1] // wide

    def vec(i):
        return vec_ref[i : i + 1]

    def total(x):
        return jnp.sum(x, axis=0, keepdims=True)

    unit = kept(3)
    grad_sum = norm_back(grad, vec(FIN_G), unit, kept(1)[:, 1:2])
    low = grad_sum.astype(BF16)
    right_ref[:, chunks * wide : (chunks + 1) * wide] = low
    small_ref[...] = jnp.zeros_like(small_ref)
    small_ref[FIN_G : FIN_G + 1] = total(grad * unit)
    small_ref[FIN_S : FIN_S + 1] = total(grad)
    small_ref[RED_B : RED_B + 1] = total(low.astype(F32))
    acc_ref[...] = grad_sum

    def chunk(q):
        cols = pl.ds(pl.multiple_of(q * wide, wide), wide)
        grad_pre = (mm(low, red_ref[cols], NT) * kept(2, cols)).astype(BF16)
        right_ref[:, cols] = grad_pre
        small_ref[pl.ds(EXP_B + q, 1)] = total(grad_pre.astype(F32))
        acc_ref[...] += mm(grad_pre, exp_ref[:, cols], NT)

    in_loop(chunks, together, chunk)
    acc = acc_ref[...]
    unit = kept(0)
    small_ref[ATTN_G : ATTN_G + 1] = total(acc * unit)
    small_ref[ATTN_S : ATTN_S + 1] = total(acc)
    grad_hidden = norm_back(acc, vec(ATTN_G), unit, kept(1)[:, 0:1])
    hidden_ref[...] = grad_hidden
    low = grad_hidden.astype(BF16)
    right_ref[:, (chunks + 1) * wide :] = low
    small_ref[OUT_B : OUT_B + 1] = total(low.astype(F32))
    return reorder(mm(low, out_ref[...], NT).astype(BF16), seg, n_seg)


def token_rows_back_kernel(meta_ref, grad_ref, *refs, slots, n_seg):
    kept_refs = [refs[t * N_KEPT : (t + 1) * N_KEPT] for t in range(slots)]
    refs = refs[slots * N_KEPT :]
    (vec_ref, out_ref, exp_ref, red_ref), outs, mix_refs, acc_ref = refs[:4], refs[4:7], refs[7:-1], refs[-1]
    size = grad_ref.shape[1]

    def kept(i, cols=slice(None)):
        return jnp.concatenate([kept_refs[t][i][:size, cols] for t in range(slots)], axis=0)

    grad = jnp.concatenate([grad_ref[t].astype(F32) for t in range(slots)], axis=0)
    mixed = rows_back(seg_here(), n_seg, grad, kept, vec_ref, out_ref, exp_ref, red_ref, outs, acc_ref, 2)
    width = mixed.shape[1] // n_seg
    for m in range(n_seg):
        for t in range(slots):
            mix_refs[m][:, t * width : (t + 1) * width] = mixed[t * size : (t + 1) * size, m * width : (m + 1) * width]


def memory_rows_back_kernel(meta_ref, *refs, n_seg, size):
    d_refs, refs = refs[:n_seg], refs[n_seg:]
    (wk_ref, wv_ref), kept_refs, refs = refs[:2], refs[2 : 2 + N_KEPT], refs[2 + N_KEPT :]
    (vec_ref, out_ref, exp_ref, red_ref), outs, (memory_ref, own_ref, acc_ref) = refs[:4], refs[4:7], refs[7:]
    seg = seg_here()
    width = d_refs[0].shape[1] // 2
    d_key = reorder(jnp.concatenate([r[:, :width] for r in d_refs], axis=1), seg, n_seg)
    d_value = reorder(jnp.concatenate([r[:, width:] for r in d_refs], axis=1), seg, n_seg)
    grad = 2.0 * (mm(d_key, wk_ref[...], NT) + mm(d_value, wv_ref[...], NT))
    memory_ref[...] = grad
    grad = jnp.where(meta_ref[FRESH] == 1, jnp.zeros_like(grad), grad)

    def kept(i, cols=slice(None)):
        return kept_refs[i][size:, cols]

    mixed = rows_back(seg, n_seg, grad, kept, vec_ref, out_ref, exp_ref, red_ref, outs, acc_ref, 1)
    own_ref[...] = mixed[:, : own_ref.shape[1]]


def tokens_grad_kernel(meta_ref, hidden_ref, wq_ref, wk_ref, wv_ref, *refs, slots, n_seg):
    d_refs, out_ref = refs[:-1], refs[-1]
    size = out_ref.shape[1]
    width = d_refs[0].shape[1] // 3
    seg = seg_here()
    for t in range(slots):
        grad = hidden_ref[t * size : (t + 1) * size]
        for i, w_ref in enumerate((wq_ref, wk_ref, wv_ref)):
            part = jnp.concatenate([r[t * size : (t + 1) * size, i * width : (i + 1) * width] for r in d_refs], 1)
            grad = grad + mm(reorder(part, seg, n_seg), w_ref[...], NT)
        out_ref[t] = grad.astype(BF16)


def row_parts(stream, chunks, each):
    if stream == 0:
        return [(0, each, q, q * each) for q in range(chunks)]
    return [(each, chunks * each, chunks, 0), ((chunks + 1) * each, each, chunks + 1, chunks * each)]


def rows_weights_kernel(meta_ref, *refs, stream, n_seg, n_pair, each):
    left_refs, (right_ref, other_ref), outs = refs[:-6], refs[-6:-4], refs[-4:]
    wide = outs[0].shape[3]
    half = n_pair // 2
    for lo, rows, q, row in row_parts(stream, right_ref.shape[1] // wide - 2, each):
        left = jnp.concatenate(
            [r[:, :, lo : lo + rows].reshape(n_seg * n_pair * rows, r.shape[3]) for r in left_refs], axis=1
        )
        right = jnp.concatenate([r[:, q * wide : (q + 1) * wide] for r in (right_ref, other_ref)], axis=0)
        full = mm(left, right).reshape(n_seg, n_pair, rows, wide).astype(BF16)
        for s in range(n_seg):
            low, high = s & 1, s >> 1
            outs[low][high, :, row : row + rows] = full[s, :half]
            outs[2 + high][low, :, row : row + rows] = full[s, half:]


def quarter_kernel(meta_ref, left_ref, left2_ref, right_ref, right2_ref, *refs, stream, each):
    half_refs, outs = (refs[:2], refs[2:4]), refs[4:]
    wide = outs[0].shape[2]
    pairs = left_ref.shape[0]
    half = pairs // 2
    for lo, rows, q, row in row_parts(stream, right_ref.shape[1] // wide - 2, each):

        def rows_of(r):
            return jnp.concatenate([r[z].astype(F32)[lo : lo + rows] for z in range(pairs)], axis=0)

        left = jnp.concatenate([rows_of(left_ref), rows_of(left2_ref)], axis=1).astype(BF16)
        right = jnp.concatenate([r[:, q * wide : (q + 1) * wide] for r in (right_ref, right2_ref)], axis=0)
        part = mm(left, right).reshape(pairs, rows, wide)
        for z in range(pairs):
            total = part[z]
            for r in half_refs[z // half]:
                total = total + r[z % half, row : row + rows].astype(F32)
            outs[z & 1][z >> 1, row : row + rows] = total.astype(BF16)


def heads_weights_kernel(meta_ref, small_ref, small_m_ref, hid_ref, memory_ref, w_ref, *refs, slots, n_seg):
    rows, refs = refs[: slots * n_seg], refs[slots * n_seg :]
    grads, (mem0_ref, mem1_ref, dm0_ref, dm1_ref, keep_ref, send_ref) = refs[:n_seg], refs[n_seg:]
    seg, core, pair, fresh1 = seg_here(), core_here(), pair_here(), meta_ref[FRESH]
    wide = rows[0].shape[1]
    width = wide // n_seg
    each = keep_ref.shape[2]
    col = lax.broadcasted_iota(jnp.int32, (1, 3 * width), 1)
    twice = jnp.where(col < width, 1.0, 2.0)
    dm0 = (dm0_ref[...].astype(F32) * twice).astype(BF16)
    dm1 = (dm1_ref[...].astype(F32) * twice).astype(BF16)
    full = mm(mem0_ref[...], dm0, TN) + mm(mem1_ref[...], dm1, TN)
    sums = jnp.sum(dm0.astype(F32), axis=0, keepdims=True) + jnp.sum(dm1.astype(F32), axis=0, keepdims=True)
    for m, g in enumerate(grads):
        x = jnp.concatenate([r[...] for r in rows[m::n_seg]], axis=0)
        full = full + mm(x, g[...], TN)
        sums = sums + jnp.sum(g[...].astype(F32), axis=0, keepdims=True)
    grad_mem = mm(dm0, w_ref[...], NT)
    whole = hid_ref[...] + jnp.where(fresh1 == 1, memory_ref[...], 0.0)
    grad_mem = grad_mem + jnp.where(seg == 0, whole, 0.0)

    def placed(v):
        return reorder(jnp.concatenate([v, jnp.zeros((1, wide - width), F32)], axis=1), seg, n_seg)

    n_pair = keep_ref.shape[0]
    chunks = 4
    head = EXP_B + chunks
    given = small_ref[...] + jnp.where(seg == 0, small_m_ref[...], 0.0)
    small = jnp.concatenate(
        [
            placed(sums[:, :width]),
            placed(sums[:, 2 * width :]),
            given[2:head],
            grad_mem,
            jnp.zeros((N_SMALL - head - grad_mem.shape[0], wide), F32),
        ],
        axis=0,
    ).T
    turned = small.reshape(wide // (chunks * each), chunks, each, N_SMALL)
    spread = [
        jnp.concatenate(
            [turned[:, k, :, EXP_B + q : EXP_B + q + 1].reshape(wide // chunks, 1) for k in range(chunks)], axis=1
        )
        for q in range(chunks)
    ]
    small = jnp.concatenate([small[:, :EXP_B], jnp.concatenate(spread, axis=0), small[:, head:]], axis=1)
    high = small.astype(BF16)
    rest = (small - high.astype(F32)).astype(BF16)
    full = jnp.concatenate([full, high.astype(F32), rest.astype(F32)], axis=1)
    keep, send = core_halves(full, core, n_pair, each)
    for s in range(n_seg):
        for z in range(n_pair):
            keep_ref[z ^ pair, s ^ seg] = keep[s * n_pair + z]
            send_ref[z ^ pair, s ^ seg] = send[s * n_pair + z]


def late_sum(*parts, at):
    total = sum(p.astype(F32) for p in parts)
    small = total[..., at : at + N_SMALL] + total[..., at + N_SMALL :]
    high = small.astype(BF16)
    rest = (small - high.astype(F32)).astype(BF16)
    return jnp.concatenate([total[..., :at].astype(BF16), high, rest], axis=-1)


def heads_final_kernel(meta_ref, *refs, n_seg, mem):
    ins, outs = refs[:n_seg], refs[n_seg:]
    seg = seg_here()
    width = outs[0].shape[1] // n_seg
    total = [r[...].astype(F32) for r in ins]
    for i in range(3):
        outs[i][...] = reorder(
            jnp.concatenate([total[m][:, i * width : (i + 1) * width] for m in range(n_seg)], axis=1), seg, n_seg
        )
    at = 3 * width
    small = sum(t[:, at : at + N_SMALL] + t[:, at + N_SMALL : at + 2 * N_SMALL] for t in total).T
    vec_refs, exp_ref, mem_ref = outs[3 : 3 + EXP_B], outs[3 + EXP_B], outs[4 + EXP_B]
    for i, r in enumerate(vec_refs):
        r[...] = small[i : i + 1]
    exp_ref[...] = jnp.concatenate([small[EXP_B + q : EXP_B + q + 1] for q in range(4)], axis=1)
    mem_ref[...] = small[EXP_B + 4 : EXP_B + 4 + mem]


def rows_final_kernel(meta_ref, first_ref, second_ref, *outs):
    total = first_ref[...].astype(F32) + second_ref[...].astype(F32)
    wide = total.shape[1]
    at = 0
    for r in outs:
        for q in range(r.shape[1] // wide):
            r[:, q * wide : (q + 1) * wide] = total[at : at + r.shape[0]]
            at += r.shape[0]


def shards(
    tokens,
    new_doc,
    valid_len,
    mem_init,
    query_proj,
    query_bias,
    key_proj,
    value_proj,
    value_bias,
    output_proj,
    output_bias,
    attn_gain,
    attn_shift,
    expand_proj,
    expand_bias,
    reduce_proj,
    reduce_bias,
    final_gain,
    final_shift,
    d_out,
):
    slots, size, wide = tokens.shape
    assert slots == 2
    n_seg, n_doc = lax.axis_size("seg"), lax.axis_size("doc")
    n_pair = n_doc // 2
    hidden_units = expand_proj.shape[1]
    chunks = hidden_units // wide
    assert chunks == 4
    mem = mem_init.shape[0]
    width = wide // n_seg
    heads = HEADS // n_seg
    others = range(1, n_seg)
    all_rows = n_seg * size

    rows0 = [tokens[0]] + [swap(tokens[0], "seg", m) for m in others]
    place = jnp.concatenate([new_doc, valid_len])
    w_own, b_own, vecs = call(
        functools.partial(prep_kernel, n_seg=n_seg, chunks=chunks),
        [shape_of(wide, 3 * width), shape_of(1, 3 * width, dtype=F32), shape_of(N_VEC, wide, dtype=F32)],
        (
            place,
            query_proj,
            key_proj,
            value_proj,
            query_bias,
            value_bias,
            output_bias,
            attn_gain,
            attn_shift,
            reduce_bias,
            final_gain,
            final_shift,
            expand_bias,
        ),
        4,
        far_in=range(4, 5 + EXP_B),
        scratch=[pltpu.VMEM((1, hidden_units), F32), pltpu.SemaphoreType.DMA((EXP_B + 1,))],
    )

    second, w_own, *rows0 = lax.optimization_barrier((tokens[1], w_own, *rows0))
    rows = [rows0, [second] + [swap(second, "seg", m) for m in others]]

    def project(t):
        (out,) = call(qkv_kernel, [shape_of(all_rows, 3 * width)], (place, w_own, b_own, *rows[t]), 3)
        return out

    def attend(t, qkv, written=()):
        mem_queries = not written
        got = call(
            functools.partial(attn_fwd_kernel, slot=t, blocks=n_seg, heads=heads, mem_queries=mem_queries),
            [shape_of(size + (mem if mem_queries else 0), width)] * n_seg
            + [shape_of(8, all_rows + 128, dtype=F32), shape_of(mem, 3 * width)]
            + [shape_of(mem, wide)] * len(written),
            (place, qkv, mem_init, w_own, b_own, *written),
            8,
        )
        return list(got[:n_seg]), *got[n_seg:]

    def attend_back(t, qkv, qkv_mem, lse, grads, more=()):
        got = call(
            functools.partial(attn_bwd_kernel, slot=t, blocks=n_seg, heads=heads, mem_queries=len(grads) > n_seg),
            [shape_of(size * (2 if more else 1), 3 * width)] * n_seg + [shape_of(mem, 3 * width)],
            (place, qkv, qkv_mem, lse, *grads, *more),
            8,
        )
        return list(got[:n_seg]), got[n_seg]

    def trade(blocks):
        return [blocks[0]] + [swap(blocks[m], "seg", m) for m in others]

    weights = (vecs, output_proj, expand_proj, reduce_proj)
    each = wide // (n_seg * n_doc)

    def rows_forward(mixed, hidden, result_shapes):
        n_rows = sum(h.shape[0] for h in hidden)
        left = [shape_of(n_seg, n_pair, (chunks + 2) * each, size)] * 2
        if len(hidden) > 1:
            left += [shape_of(n_pair, (chunks + 2) * each, mem)] * 2
        got = call(
            functools.partial(rows_fwd_kernel, n_seg=n_seg, n_pair=n_pair, n_hidden=len(hidden)),
            [
                shape_of(n_rows, wide, dtype=F32),
                shape_of(n_rows, 128, dtype=F32),
                shape_of(n_rows, hidden_units, dtype=F32),
                shape_of(n_rows, wide, dtype=F32),
                *result_shapes,
                *left,
            ],
            (place, *mixed, *hidden, *weights),
            8,
            scratch=[pltpu.VMEM((n_rows, wide), F32)],
        )
        return got[:N_KEPT], got[N_KEPT : N_KEPT + len(hidden)], got[N_KEPT + len(hidden) :]

    qkv0 = project(0)
    mixed0, lse0, qkv_mem0 = attend(0, qkv0)
    mixed0[0], *rows[1] = lax.optimization_barrier((mixed0[0], *rows[1]))
    qkv1 = project(1)
    mixed0 = trade(mixed0)
    qkv1, mixed0[0] = lax.optimization_barrier((qkv1, mixed0[0]))
    kept0, (layer0, written), (left0, left0_send, left_m, left_m_send) = rows_forward(
        mixed0, (tokens[0], mem_init), [shape_of(size, wide), shape_of(mem, wide, dtype=F32)]
    )
    mixed1, lse1, qkv_mem1, memory1 = attend(1, qkv1, (written,))
    left0_other, left_m_other = swap(left0_send, "doc", 1), swap(left_m_send, "doc", 1)
    mixed1[0], left0_other, left_m_other = lax.optimization_barrier((mixed1[0], left0_other, left_m_other))
    kept1, (layer1,), (left1, left1_send) = rows_forward(trade(mixed1), (tokens[1],), [shape_of(size, wide)])
    left1_other = swap(left1_send, "doc", 1)
    layer_out = jnp.stack([layer0, layer1])

    def back_shapes(n_rows):
        return [
            shape_of(n_rows, hidden_units + 2 * wide),
            shape_of(n_rows, wide, dtype=F32),
            shape_of(N_VEC, wide, dtype=F32),
        ]

    n_rows = slots * size
    got = call(
        functools.partial(token_rows_back_kernel, slots=slots, n_seg=n_seg),
        back_shapes(n_rows) + [shape_of(size, slots * width)] * n_seg,
        (place, d_out, *kept0, *kept1, *weights),
        10,
        scratch=[pltpu.VMEM((n_rows, wide), F32)],
    )
    right, hidden, small = got[:3]
    grads = trade(got[3:])
    right_other = swap(right, "doc", 1)
    right, left1_other = lax.optimization_barrier((right, left1_other))

    def plain_sum(*parts):
        return sum(p.astype(F32) for p in parts).astype(BF16)

    share = [chunks * each, (chunks + 1) * each]

    def row_weights(stream, right_other):
        return call(
            functools.partial(rows_weights_kernel, stream=stream, n_seg=n_seg, n_pair=n_pair, each=each),
            [shape_of(n_seg // 2, n_pair // 2, share[stream], wide)] * 4,
            (place, left0, left1, left0_other, left1_other, right, right_other),
            2,
        )

    def both_sums(keep_a, came_a, keep_b, came_b):
        return [plain_sum(k[i], c[i]) for k, c in ((keep_a, came_a), (keep_b, came_b)) for i in range(2)]

    keep_a, send_a, keep_b, send_b = row_weights(0, right_other)
    send_a, send_b, *grads = lax.optimization_barrier((send_a, send_b, *grads))
    came_a, came_b = swap(send_a, "seg", 1), swap(send_b, "seg", 2)
    d_qkv1, d_mem1 = attend_back(1, qkv1, qkv_mem1, lse1, grads)
    d_mem1_all = trade([d_mem1[:, width:]] * n_seg)

    right_other, d_mem1_all[0] = lax.optimization_barrier((right_other, d_mem1_all[0]))
    keep_c, send_c, keep_d, send_d = row_weights(1, right_other)
    send_c, send_d, came_a, came_b, *d_mem1_all = lax.optimization_barrier(
        (send_c, send_d, came_a, came_b, *d_mem1_all)
    )
    keep_a, send_a, keep_b, send_b = both_sums(keep_a, came_a, keep_b, came_b)
    send_a, send_b, d_mem1_all[0] = lax.optimization_barrier((send_a, send_b, d_mem1_all[0]))
    came_a, came_b = swap(send_a, "seg", 2), swap(send_b, "seg", 1)

    got = call(
        functools.partial(memory_rows_back_kernel, n_seg=n_seg, size=size),
        back_shapes(mem) + [shape_of(mem, wide, dtype=F32), shape_of(mem, width)],
        (place, *d_mem1_all, key_proj, value_proj, *kept0, *weights),
        6,
        scratch=[pltpu.VMEM((mem, wide), F32)],
    )
    right_m, hidden_m, small_m, memory1_grad, mixed_m = got
    right_m_other = swap(right_m, "doc", 1)
    def pair_sum(keep, came, add):
        bit = 2
        while keep.shape[0] > 1:
            bit *= 2
            if keep.shape[0] == 2:
                (keep, send) = [add(keep[i : i + 1], came[i : i + 1]) for i in range(2)]
            else:
                both = add(keep, came)
                keep, send = both[0::2], both[1::2]
            came = swap(send, "doc", bit)
        return [keep[0], came[0]]

    def quarter(stream, *halves):
        keep, send = call(
            functools.partial(quarter_kernel, stream=stream, each=each),
            [shape_of(n_pair // 2, share[stream], wide)] * 2,
            (place, left_m, left_m_other, right_m, right_m_other, *halves),
            1,
        )
        return keep, send

    right_m, came_a, came_b, send_c, send_d = lax.optimization_barrier((right_m, came_a, came_b, send_c, send_d))
    came_c, came_d = swap(send_c, "seg", 1), swap(send_d, "seg", 2)
    keep_x, send_x = quarter(0, keep_a, came_a, keep_b, came_b)
    send_x, mixed_m = lax.optimization_barrier((send_x, mixed_m))
    came_x = swap(send_x, "doc", 2)
    d_qkv, d_mem0 = attend_back(0, qkv0, qkv_mem0, lse0, [*grads, mixed_m], d_qkv1)

    came_x, d_mem0 = lax.optimization_barrier((came_x, d_mem0))
    parts_exp = pair_sum(keep_x, came_x, plain_sum)

    columns = 3 * width + 2 * N_SMALL
    keep, send = call(
        functools.partial(heads_weights_kernel, slots=slots, n_seg=n_seg),
        [shape_of(n_pair, n_seg, each, columns)] * 2,
        (
            place,
            small,
            small_m,
            hidden_m,
            memory1_grad,
            w_own,
            *rows[0],
            *rows[1],
            *d_qkv,
            mem_init,
            memory1,
            d_mem0,
            d_mem1,
        ),
        6,
    )

    def rows_final(parts, *shapes):
        return call(
            rows_final_kernel,
            [shape_of(*dims, dtype=F32) for dims in shapes],
            (place, *parts),
            1,
            far_out=range(len(shapes)),
        )

    add = functools.partial(late_sum, at=3 * width)
    came = swap(send, "doc", 1)
    came_c, came_d, keep = lax.optimization_barrier((came_c, came_d, keep))
    keep_c, send_c, keep_d, send_d = both_sums(keep_c, came_c, keep_d, came_d)
    came_c, came_d = swap(send_c, "seg", 2), swap(send_d, "seg", 1)
    _, came, parts_exp[1] = lax.optimization_barrier((send_c, came, parts_exp[1]))
    mine = add(keep, came)
    came_l = swap(mine[1::2], "doc", 2)
    keep_y, send_y = quarter(1, keep_c, came_c, keep_d, came_d)
    _, came_l, *d_qkv = lax.optimization_barrier((send_y, came_l, *d_qkv))
    late = pair_sum(mine[0::2], came_l, add)
    parts_rest = pair_sum(keep_y, swap(send_y, "doc", 2), plain_sum)
    (grad_exp,) = rows_final(parts_exp, (each, hidden_units))

    back = trade(d_qkv)
    (grad_tokens,) = call(
        functools.partial(tokens_grad_kernel, slots=slots, n_seg=n_seg),
        [shape_of(slots, size, wide)],
        (place, hidden, query_proj, key_proj, value_proj, *back),
        3,
        far_out=(0,),
    )

    late[1], grad_exp, layer_out = lax.optimization_barrier((late[1], grad_exp, layer_out))
    mine = add(*late)
    parts = trade([mine[m] for m in range(n_seg)])
    grad_tokens, *parts = lax.optimization_barrier((grad_tokens, *parts))
    got = call(
        functools.partial(heads_final_kernel, n_seg=n_seg, mem=mem),
        [shape_of(each, wide, dtype=F32)] * 3
        + [shape_of(1, each, dtype=F32)] * EXP_B
        + [shape_of(1, chunks * each, dtype=F32), shape_of(mem, each, dtype=F32)],
        (place, *parts),
        1,
        far_out=range(5 + EXP_B),
    )
    grad_red, grad_out = rows_final(parts_rest, (chunks * each, wide), (each, wide))
    grad_q, grad_k, grad_v = got[:3]
    flat = [v.reshape(-1) for v in got[3:-1]]

    return (
        layer_out,
        grad_tokens,
        got[-1],
        grad_q,
        flat[Q_B],
        grad_k,
        grad_v,
        flat[V_B],
        grad_out,
        flat[OUT_B],
        flat[ATTN_G],
        flat[ATTN_S],
        grad_exp,
        flat[EXP_B],
        grad_red,
        flat[RED_B],
        flat[FIN_G],
        flat[FIN_S],
    )


def solution(mesh):
    both = ("seg", "doc")
    data = P("doc", "seg", None)
    placed = (data, P("doc"), P("doc")) + (P(),) * 16 + (data,)
    vec, mat = P(both), P(both, None)
    return jax.shard_map(
        shards,
        mesh=mesh,
        in_specs=placed,
        out_specs=(
            data,
            data,
            P(None, both),
            mat,
            vec,
            mat,
            mat,
            vec,
            mat,
            vec,
            vec,
            vec,
            mat,
            vec,
            mat,
            vec,
            vec,
            vec,
        ),
        check_vma=False,
    )
```

profile of v0, /device:TPU:0, one launch (start us, length us, event | category | flops | bytes accessed | tf_op | source)
XLA Modules:
  0.0 149.8 jit_solution(1039972534151189993)
XLA Ops:
  1.8 4.0 %collective-permute-start.2 = (bf16[128,768]{1,0:T(8,128)(2,1)S(1)}, bf16[128,768]{1,0:T(8,128)(2,1)S(1)}, u32[]{:S(2)}, u32[]{:S(2)}) collective-permute-start(bf16[128,768]{1,0:T(8,128)(2,1)S(1)} %get-tuple-element.169.refs_0_.refs_4_), channel_id=1, source_target_pairs={{0,24},{8,16},{16,8},{24,0},{1,25},{9,17},{17,9},{25,1},{2,26},{10... | collective-permute-start | bytes 589832 | tf_op jit(solution)/shard_map/ppermute | solution.py:32
  7.2 1.3 copy-done.3
  8.4 1.3 copy-done.5
  11.0 2.9 %shard_map.331 = (bf16[768,576]{1,0:T(8,128)(2,1)S(1)}, f32[1,576]{1,0:T(1,128)S(1)}, f32[16,768]{1,0:T(8,128)S(1)}) custom-call(s32[4]{0:T(128)S(1)} %pad_add_fusion.meta_ref, bf16[768,768]{1,0:T(8,128)(2,1)S(1)} %copy-done.7, bf16[768,768]{1,0:T(8,128)(2,1)S(1)} %copy-done.3, bf16[768,768]{1,0:T(8,128)(2,1)S(1)} %copy-done.5, f32[768]{0:T(1024)} %refs_0_.1, ...), custom_call_target="tpu_custom_call" | custom-call | bytes 12000000 | tf_op jit(solution)/shard_map/pallas_call | solution.py:57
  15.2 1.7 %collective-permute-start.5 = (bf16[128,768]{1,0:T(8,128)(2,1)S(1)}, bf16[128,768]{1,0:T(8,128)(2,1)S(1)}, u32[]{:S(2)}, u32[]{:S(2)}) collective-permute-start(bf16[128,768]{1,0:T(8,128)(2,1)S(1)} %get-tuple-element.175.refs_0_.refs_4_), channel_id=1, source_target_pairs={{0,24},{8,16},{16,8},{24,0},{1,25},{9,17},{17,9},{25,1},{2,26},{10... | collective-permute-start | bytes 589832 | tf_op jit(solution)/shard_map/ppermute | solution.py:32
  16.9 1.3 collective-permute-start.4
  18.7 1.3 shard_map.332.qkv_ref
  20.0 4.3 %shard_map.333 = (bf16[144,192]{1,0:T(8,128)(2,1)S(1)}, bf16[144,192]{1,0:T(8,128)(2,1)S(1)}, bf16[144,192]{1,0:T(8,128)(2,1)S(1)}, bf16[144,192]{1,0:T(8,128)(2...) custom-call(s32[4]{0:T(128)S(1)} %pad_add_fusion.meta_ref, bf16[512,576]{1,0:T(8,128)(2,1)S(1)} %shard_map.332.qkv_ref, ...), custom_call_target="tpu_custom_call" | custom-call | bytes 24000000 | tf_op jit(solution)/shard_map/pallas_call | solution.py:57
  24.3 1.5 %collective-permute-start.6 = (bf16[144,192]{1,0:T(8,128)(2,1)S(1)}, bf16[144,192]{1,0:T(8,128)(2,1)S(1)}, u32[]{:S(2)}, u32[]{:S(2)}) collective-permute-start(bf16[144,192]{1,0:T(8,128)(2,1)S(1)} %get-tuple-element.181), channel_id=1, source_target_pairs={{0,8},{8,0},{16,24},{24,16},{1,9},{9,1},{17,25},{25,17},{2,10},{10... | collective-permute-start | bytes 165896 | tf_op jit(solution)/shard_map/ppermute | solution.py:32
  27.9 1.3 shard_map.334.qkv_ref
  30.2 1.7 %collective-permute-done.8.refs_3_ = bf16[144,192]{1,0:T(8,128)(2,1)S(1)} collective-permute-done((bf16[144,192]{1,0:T(8,128)(2,1)S(1)}, bf16[144,192]{1,0:T(8,128)(2,1)S(1)}, u32[]{:S(2)}, u32[]{:S(2)}) %collective-permute-start.8) | collective-permute-done | bytes 55328 | tf_op jit(solution)/shard_map/ppermute | solution.py:32
  31.9 4.8 %shard_map.335 = (f32[144,768]{1,0:T(8,128)S(1)}, f32[144,128]{1,0:T(8,128)S(1)}, f32[144,3072]{1,0:T(8,128)S(1)}, f32[144,768]{1,0:T(8,128)S(1)}, bf16[128,768]...) custom-call(s32[4]{0:T(128)S(1)} %pad_add_fusion.meta_ref, ...), custom_call_target="tpu_custom_call" | custom-call | bytes 24000000 | tf_op jit(solution)/shard_map/pallas_call | solution.py:57
  36.7 3.5 %shard_map.336 = (bf16[128,192]{1,0:T(8,128)(2,1)S(1)}, bf16[128,192]{1,0:T(8,128)(2,1)S(1)}, bf16[128,192]{1,0:T(8,128)(2,1)S(1)}, bf16[128,192]{1,0:T(8,128)(2...) custom-call(s32[4]{0:T(128)S(1)} %pad_add_fusion.meta_ref, ...), custom_call_target="tpu_custom_call" | custom-call | bytes 24000000 | tf_op jit(solution)/shard_map/pallas_call | solution.py:57
  40.2 1.3 collective-permute-start.11
  42.1 1.7 %collective-permute-start.13 = (bf16[128,192]{1,0:T(8,128)(2,1)S(1)}, bf16[128,192]{1,0:T(8,128)(2,1)S(1)}, u32[]{:S(2)}, u32[]{:S(2)}) collective-permute-start(bf16[128,192]{1,0:T(8,128)(2,1)S(1)} %get-tuple-element.194), channel_id=1, source_target_pairs={{0,24},{8,16},{16,8},{24,0},{1,25},{9,17},{17,9},{25,1},{2,26},{10... | collective-permute-start | bytes 147464 | tf_op jit(solution)/shard_map/ppermute | solution.py:32
  43.8 1.4 collective-permute-done.10.left2_ref
  45.2 1.3 collective-permute-done.12.refs_2_
  47.3 4.1 %shard_map.337 = (f32[128,768]{1,0:T(8,128)S(1)}, f32[128,128]{1,0:T(8,128)S(1)}, f32[128,3072]{1,0:T(8,128)S(1)}, f32[128,768]{1,0:T(8,128)S(1)}, bf16[128,768]...) custom-call(s32[4]{0:T(128)S(1)} %pad_add_fusion.meta_ref, ...), custom_call_target="tpu_custom_call" | custom-call | bytes 24000000 | tf_op jit(solution)/shard_map/pallas_call | solution.py:57
  51.4 5.4 %shard_map.338 = (bf16[256,4608]{1,0:T(8,128)(2,1)S(1)}, f32[256,768]{1,0:T(8,128)S(1)}, f32[16,768]{1,0:T(8,128)S(1)}, bf16[128,384]{1,0:T(8,128)(2,1)S(1)}, bf...) custom-call(s32[4]{0:T(128)S(1)} %pad_add_fusion.meta_ref, ...), custom_call_target="tpu_custom_call" | custom-call | bytes 30000000 | tf_op jit(solution)/shard_map/pallas_call | solution.py:57
  57.4 1.5 collective-permute-start.16
  60.9 1.4 collective-permute-done.14.refs_3_
  62.3 1.9 %shard_map.339 = (bf16[2,2,96,768]{3,2,1,0:T(8,128)(2,1)S(1)}, bf16[2,2,96,768]{3,2,1,0:T(8,128)(2,1)S(1)}, bf16[2,2,96,768]{3,2,1,0:T(8,128)(2,1)S(1)}, bf16[2,2,96,768]{3,2,1,0:T(8,128)(2,1)S(1)}) custom-call(s32[4]{0:T(128)S(1)} %pad_add_fusion.meta_ref, bf16[4,4,144,128]{3,2,1,0:T(8,128)(2,1)S(1)} %get-tuple-element.185.refs_0_, ...), custom_call_target="tpu_custom_call" | custom-call | bytes 6000000 | tf_op jit(solution)/shard_map/pallas_call | solution.py:57
  64.2 1.4 collective-permute-done.17.refs_2_
  67.6 5.2 %shard_map.340 = (bf16[128,576]{1,0:T(8,128)(2,1)S(1)}, bf16[128,576]{1,0:T(8,128)(2,1)S(1)}, bf16[128,576]{1,0:T(8,128)(2,1)S(1)}, bf16[128,576]{1,0:T(8,128)(2,1)S(1)}, bf16[16,576]{1,0:T(8,128)(2,1)S(1)}) custom-call(s32[4]{0:T(128)S(1)} %pad_add_fusion.meta_ref, bf16[512,576]{1,0:T(8,128)(2,1)S(1)} %shard_map.334.qkv_ref, ...), custom_call_target="tpu_custom_call" | custom-call | bytes 24000000 | tf_op jit(solution)/shard_map/pallas_call | solution.py:57
  72.9 1.5 %collective-permute-start.23 = (bf16[16,384]{1,0:T(8,128)(2,1)S(1)}, bf16[16,384]{1,0:T(8,128)(2,1)S(1)}, u32[]{:S(2)}, u32[]{:S(2)}) collective-permute-start(bf16[16,384]{1,0:T(8,128)(2,1)S(1)} %slice.159.refs_0_), channel_id=1, source_target_pairs={{0,24},{8,16},{16,8},{24,0},{1,25},{9,17},{17,9},{25,1},{2,26},{10... | collective-permute-start | bytes 36872 | tf_op jit(solution)/shard_map/ppermute | solution.py:32
  76.4 2.3 %shard_map.341 = (bf16[2,2,120,768]{3,2,1,0:T(8,128)(2,1)S(1)}, bf16[2,2,120,768]{3,2,1,0:T(8,128)(2,1)S(1)}, bf16[2,2,120,768]{3,2,1,0:T(8,128)(2,1)S(1)}, bf16[2,2,120,768]{3,2,1,0:T(8,128)(2,1)S(1)}) custom-call(s32[4]{0:T(128)S(1)} %pad_add_fusion.meta_ref, bf16[4,4,144,128]{3,2,1,0:T(8,128)(2,1)S(1)} %get-tuple-element.185.refs_0_, ...), custom_call_target="tpu_custom_call" | custom-call | bytes 6000000 | tf_op jit(solution)/shard_map/pallas_call | solution.py:57
  78.7 2.4 %collective-permute-done.23.refs_3_ = bf16[16,384]{1,0:T(8,128)(2,1)S(1)} collective-permute-done((bf16[16,384]{1,0:T(8,128)(2,1)S(1)}, bf16[16,384]{1,0:T(8,128)(2,1)S(1)}, u32[]{:S(2)}, u32[]{:S(2)}) %collective-permute-start.23) | collective-permute-done | bytes 12320 | tf_op jit(solution)/shard_map/ppermute | solution.py:32
  83.8 5.5 %shard_map.342 = (bf16[16,4608]{1,0:T(8,128)(2,1)S(1)}, f32[16,768]{1,0:T(8,128)S(1)}, f32[16,768]{1,0:T(8,128)S(1)}, f32[16,768]{1,0:T(8,128)S(1)}, bf16[16,192]{1,0:T(8,128)(2,1)S(1)}) custom-call(s32[4]{0:T(128)S(1)} %pad_add_fusion.meta_ref, bf16[16,384]{1,0:T(8,128)(2,1)S(1)} %slice.159.refs_0_, bf16[16,384]{1,0:T(8,128)(2,1)S(1)} %collective-permute-done.21.refs_1_, ...), custom_call_target="tpu_custom_call" | custom-call | bytes 18000000 | tf_op jit(solution)/shard_map/pallas_call | solution.py:57
  89.3 1.5 collective-permute-start.26
  91.5 1.4 collective-permute-done.28.right2_ref
  93.8 1.7 %collective-permute-start.29 = (bf16[2,96,768]{2,1,0:T(8,128)(2,1)S(1)}, bf16[2,96,768]{2,1,0:T(8,128)(2,1)S(1)}, u32[]{:S(2)}, u32[]{:S(2)}) collective-permute-start(bf16[2,96,768]{2,1,0:T(8,128)(2,1)S(1)} %get-tuple-element.267), channel_id=1, source_target_pairs={{0,2},{1,3},{2,0},{3,1},{4,6},{5,7},{6,4},{7,5},{8,10},{9,11},{10,... | collective-permute-start | bytes 884744 | tf_op jit(solution)/shard_map/ppermute | solution.py:32
  95.4 6.4 %shard_map.344 = (bf16[256,576]{1,0:T(8,128)(2,1)S(1)}, bf16[256,576]{1,0:T(8,128)(2,1)S(1)}, bf16[256,576]{1,0:T(8,128)(2,1)S(1)}, bf16[256,576]{1,0:T(8,128)(2,1)S(1)}, bf16[16,576]{1,0:T(8,128)(2,1)S(1)}) custom-call(s32[4]{0:T(128)S(1)} %pad_add_fusion.meta_ref, bf16[512,576]{1,0:T(8,128)(2,1)S(1)} %shard_map.332.qkv_ref, ...), custom_call_target="tpu_custom_call" | custom-call | bytes 24000000 | tf_op jit(solution)/shard_map/pallas_call | solution.py:57
  103.0 2.6 %collective-permute-start.31 = (bf16[1,96,768]{2,1,0:T(8,128)(2,1)S(1)}, bf16[1,96,768]{2,1,0:T(8,128)(2,1)S(1)}, u32[]{:S(2)}, u32[]{:S(2)}) collective-permute-start(bf16[1,96,768]{2,1,0:T(8,128)(2,1)S(1)} %get-tuple-element.333), channel_id=1, source_target_pairs={{0,4},{1,5},{2,6},{3,7},{4,0},{5,1},{6,2},{7,3},{8,12},{9,13},{10,... | collective-permute-start | bytes 442376 | tf_op jit(solution)/shard_map/ppermute | solution.py:32
  105.6 3.5 %shard_map.345 = (bf16[4,4,24,640]{3,2,1,0:T(8,128)(2,1)S(1)}, bf16[4,4,24,640]{3,2,1,0:T(8,128)(2,1)S(1)}) custom-call(s32[4]{0:T(128)S(1)} %pad_add_fusion.meta_ref, f32[16,768]{1,0:T(8,128)S(1)} %get-tuple-element.244.small_ref, f32[16,768]{1,0:T(8,128)S(1)} %get-tuple-element.245.small_m_ref, f32[16,768]{1,0:T(8,128)S(1)} %get-tuple-element.246.hid_ref, ...), custom_call_target="tpu_custom_call" | custom-call | bytes 18000000 | tf_op jit(solution)/shard_map/pallas_call | solution.py:57
  109.4 1.6 %collective-permute-start.33 = (bf16[2,120,768]{2,1,0:T(8,128)(2,1)S(1)}, bf16[2,120,768]{2,1,0:T(8,128)(2,1)S(1)}, u32[]{:S(2)}, u32[]{:S(2)}) collective-permute-start(bf16[2,120,768]{2,1,0:T(8,128)(2,1)S(1)} %get-tuple-element.322), channel_id=1, source_target_pairs={{0,8},{8,0},{16,24},{24,16},{1,9},{9,1},{17,25},{25,17},{2,10},{10... | collective-permute-start | bytes 1105928 | tf_op jit(solution)/shard_map/ppermute | solution.py:32
  114.7 1.3 shard_map.347
  116.0 4.5 %collective-permute-done.33.refs_3_ = bf16[2,120,768]{2,1,0:T(8,128)(2,1)S(1)} collective-permute-done((bf16[2,120,768]{2,1,0:T(8,128)(2,1)S(1)}, bf16[2,120,768]{2,1,0:T(8,128)(2,1)S(1)}, u32[]{:S(2)}, u32[]{:S(2)}) %collective-permute-start.33) | collective-permute-done | bytes 368672 | tf_op jit(solution)/shard_map/ppermute | solution.py:32
  120.4 1.5 collective-permute-done.32.refs_1_
  123.1 1.6 %collective-permute-start.42 = (bf16[2,120,768]{2,1,0:T(8,128)(2,1)S(1)}, bf16[2,120,768]{2,1,0:T(8,128)(2,1)S(1)}, u32[]{:S(2)}, u32[]{:S(2)}) collective-permute-start(bf16[2,120,768]{2,1,0:T(8,128)(2,1)S(1)} %get-tuple-element.280), channel_id=1, source_target_pairs={{0,2},{1,3},{2,0},{3,1},{4,6},{5,7},{6,4},{7,5},{8,10},{9,11},{10,... | collective-permute-start | bytes 1105928 | tf_op jit(solution)/shard_map/ppermute | solution.py:32
  125.3 1.3 collective-permute-start.36
  127.2 1.6 %collective-permute-start.38 = (bf16[256,576]{1,0:T(8,128)(2,1)S(1)}, bf16[256,576]{1,0:T(8,128)(2,1)S(1)}, u32[]{:S(2)}, u32[]{:S(2)}) collective-permute-start(bf16[256,576]{1,0:T(8,128)(2,1)S(1)} %get-tuple-element.290.refs_11_), channel_id=1, source_target_pairs={{0,24},{8,16},{16,8},{24,0},{1,25},{9,17},{17,9},{25,1},{2,26},{10... | collective-permute-start | bytes 884744 | tf_op jit(solution)/shard_map/ppermute | solution.py:32
  128.9 5.9 %collective-permute-done.35 = bf16[1,4,24,640]{3,2,1,0:T(8,128)(2,1)S(1)} collective-permute-done((bf16[1,4,24,640]{3,2,1,0:T(8,128)(2,1)S(1)}, bf16[1,4,24,640]{3,2,1,0:T(8,128)(2,1)S(1)}, u32[]{:S(2)}, u32[]{:S(2)}) %collective-permute-start.35) | collective-permute-done | bytes 122912 | tf_op jit(solution)/shard_map/ppermute | solution.py:32
  135.8 2.9 %collective-permute-start.43 = (bf16[1,120,768]{2,1,0:T(8,128)(2,1)S(1)}, bf16[1,120,768]{2,1,0:T(8,128)(2,1)S(1)}, u32[]{:S(2)}, u32[]{:S(2)}) collective-permute-start(bf16[1,120,768]{2,1,0:T(8,128)(2,1)S(1)} %get-tuple-element.330), channel_id=1, source_target_pairs={{0,4},{1,5},{2,6},{3,7},{4,0},{5,1},{6,2},{7,3},{8,12},{9,13},{10,... | collective-permute-start | bytes 552968 | tf_op jit(solution)/shard_map/ppermute | solution.py:32
  138.7 1.4 collective-permute-start.41
  140.7 1.4 collective-permute-done.37.refs_2_
  143.1 3.9 %shard_map.348 = bf16[2,128,768]{2,1,0:T(8,128)(2,1)} custom-call(s32[4]{0:T(128)S(1)} %pad_add_fusion.meta_ref, f32[256,768]{1,0:T(8,128)S(1)} %get-tuple-element.286.hidden_ref, bf16[768,768]{1,0:T(8,128)(2,1)S(1)} %copy-done.8, bf16[768,768]{1,0:T(8,128)(2,1)S(1)} %copy-done.4, bf16[768,768]{1,0:T(8,128)(2,1)S(1)} %copy-done.6, ...), custom_call_target="tpu_custom_call" | custom-call | bytes 9000000 | tf_op jit(solution)/shard_map/pallas_call | solution.py:57
  147.0 1.5 %shard_map.349 = (f32[24,768]{1,0:T(8,128)}, f32[24,768]{1,0:T(8,128)}, f32[24,768]{1,0:T(8,128)}, f32[1,24]{1,0:T(1,128)}, f32[1,24]{1,0:T(1,128)}, /*index=5*/...) custom-call(s32[4]{0:T(128)S(1)} %pad_add_fusion.meta_ref, ...), custom_call_target="tpu_custom_call" | custom-call | bytes 3000000 | tf_op jit(solution)/shard_map/pallas_call | solution.py:57
  148.5 1.3 shard_map.350
  (107 shorter events, 31.0 us)
Async XLA Ops:
  0.7 31.2 %copy-start.2 = (bf16[768,768]{1,0:T(8,128)(2,1)S(1)}, bf16[768,768]{1,0:T(8,128)(2,1)}, u32[]{:S(2)}) copy-start(bf16[768,768]{1,0:T(8,128)(2,1)} %refs_11_.3) | copy-start | bytes 3538948
  1.8 12.1 %collective-permute-start.2 = (bf16[128,768]{1,0:T(8,128)(2,1)S(1)}, bf16[128,768]{1,0:T(8,128)(2,1)S(1)}, u32[]{:S(2)}, u32[]{:S(2)}) collective-permute-start(bf16[128,768]{1,0:T(8,128)(2,1)S(1)} %get-tuple-element.169.refs_0_.refs_4_), channel_id=1, source_target_pairs={{0,24},{8,16},{16,8},{24,0},{1,25},{9,17},{17,9},{25,1},{2,26},{10... | collective-permute-start | bytes 589832 | tf_op jit(solution)/shard_map/ppermute | solution.py:32
  5.8 9.1 %collective-permute-start.1 = (bf16[128,768]{1,0:T(8,128)(2,1)S(1)}, bf16[128,768]{1,0:T(8,128)(2,1)S(1)}, u32[]{:S(2)}, u32[]{:S(2)}) collective-permute-start(bf16[128,768]{1,0:T(8,128)(2,1)S(1)} %get-tuple-element.169.refs_0_.refs_4_), channel_id=1, source_target_pairs={{0,16},{8,24},{16,0},{24,8},{1,17},{9,25},{17,1},{25,9},{2,18},{10... | collective-permute-start | bytes 589832 | tf_op jit(solution)/shard_map/ppermute | solution.py:32
  6.3 8.9 %collective-permute-start = (bf16[128,768]{1,0:T(8,128)(2,1)S(1)}, bf16[128,768]{1,0:T(8,128)(2,1)S(1)}, u32[]{:S(2)}, u32[]{:S(2)}) collective-permute-start(bf16[128,768]{1,0:T(8,128)(2,1)S(1)} %get-tuple-element.169.refs_0_.refs_4_), channel_id=1, source_target_pairs={{0,8},{8,0},{16,24},{24,16},{1,9},{9,1},{17,25},{25,17},{2,10},{10... | collective-permute-start | bytes 589832 | tf_op jit(solution)/shard_map/ppermute | solution.py:32
  11.0 20.9 %copy-start.1 = (bf16[3072,768]{1,0:T(8,128)(2,1)S(1)}, bf16[3072,768]{1,0:T(8,128)(2,1)}, u32[]{:S(2)}) copy-start(bf16[3072,768]{1,0:T(8,128)(2,1)} %refs_13_.1) | copy-start | bytes 14155780
  15.2 11.4 %collective-permute-start.5 = (bf16[128,768]{1,0:T(8,128)(2,1)S(1)}, bf16[128,768]{1,0:T(8,128)(2,1)S(1)}, u32[]{:S(2)}, u32[]{:S(2)}) collective-permute-start(bf16[128,768]{1,0:T(8,128)(2,1)S(1)} %get-tuple-element.175.refs_0_.refs_4_), channel_id=1, source_target_pairs={{0,24},{8,16},{16,8},{24,0},{1,25},{9,17},{17,9},{25,1},{2,26},{10... | collective-permute-start | bytes 589832 | tf_op jit(solution)/shard_map/ppermute | solution.py:32
  16.9 11.0 %collective-permute-start.4 = (bf16[128,768]{1,0:T(8,128)(2,1)S(1)}, bf16[128,768]{1,0:T(8,128)(2,1)S(1)}, u32[]{:S(2)}, u32[]{:S(2)}) collective-permute-start(bf16[128,768]{1,0:T(8,128)(2,1)S(1)} %get-tuple-element.175.refs_0_.refs_4_), channel_id=1, source_target_pairs={{0,16},{8,24},{16,0},{24,8},{1,17},{9,25},{17,1},{25,9},{2,18},{10... | collective-permute-start | bytes 589832 | tf_op jit(solution)/shard_map/ppermute | solution.py:32
  18.1 9.8 %collective-permute-start.3 = (bf16[128,768]{1,0:T(8,128)(2,1)S(1)}, bf16[128,768]{1,0:T(8,128)(2,1)S(1)}, u32[]{:S(2)}, u32[]{:S(2)}) collective-permute-start(bf16[128,768]{1,0:T(8,128)(2,1)S(1)} %get-tuple-element.175.refs_0_.refs_4_), channel_id=1, source_target_pairs={{0,8},{8,0},{16,24},{24,16},{1,9},{9,1},{17,25},{25,17},{2,10},{10... | collective-permute-start | bytes 589832 | tf_op jit(solution)/shard_map/ppermute | solution.py:32
  18.7 13.2 %copy-start = (bf16[768,3072]{1,0:T(8,128)(2,1)S(1)}, bf16[768,3072]{1,0:T(8,128)(2,1)}, u32[]{:S(2)}) copy-start(bf16[768,3072]{1,0:T(8,128)(2,1)} %refs_12_.2) | copy-start | bytes 14155780
  24.3 4.9 %collective-permute-start.6 = (bf16[144,192]{1,0:T(8,128)(2,1)S(1)}, bf16[144,192]{1,0:T(8,128)(2,1)S(1)}, u32[]{:S(2)}, u32[]{:S(2)}) collective-permute-start(bf16[144,192]{1,0:T(8,128)(2,1)S(1)} %get-tuple-element.181), channel_id=1, source_target_pairs={{0,8},{8,0},{16,24},{24,16},{1,9},{9,1},{17,25},{25,17},{2,10},{10... | collective-permute-start | bytes 165896 | tf_op jit(solution)/shard_map/ppermute | solution.py:32
  25.8 4.4 %collective-permute-start.7 = (bf16[144,192]{1,0:T(8,128)(2,1)S(1)}, bf16[144,192]{1,0:T(8,128)(2,1)S(1)}, u32[]{:S(2)}, u32[]{:S(2)}) collective-permute-start(bf16[144,192]{1,0:T(8,128)(2,1)S(1)} %get-tuple-element.182), channel_id=1, source_target_pairs={{0,16},{8,24},{16,0},{24,8},{1,17},{9,25},{17,1},{25,9},{2,18},{10... | collective-permute-start | bytes 165896 | tf_op jit(solution)/shard_map/ppermute | solution.py:32
  26.6 5.3 %collective-permute-start.8 = (bf16[144,192]{1,0:T(8,128)(2,1)S(1)}, bf16[144,192]{1,0:T(8,128)(2,1)S(1)}, u32[]{:S(2)}, u32[]{:S(2)}) collective-permute-start(bf16[144,192]{1,0:T(8,128)(2,1)S(1)} %get-tuple-element.183), channel_id=1, source_target_pairs={{0,24},{8,16},{16,8},{24,0},{1,25},{9,17},{17,9},{25,1},{2,26},{10... | collective-permute-start | bytes 165896 | tf_op jit(solution)/shard_map/ppermute | solution.py:32
  36.6 8.5 %collective-permute-start.9 = (bf16[4,4,144,128]{3,2,1,0:T(8,128)(2,1)S(1)}, bf16[4,4,144,128]{3,2,1,0:T(8,128)(2,1)S(1)}, u32[]{:S(2)}, u32[]{:S(2)}) collective-permute-start(bf16[4,4,144,128]{3,2,1,0:T(8,128)(2,1)S(1)} %get-tuple-element.189), channel_id=1, source_target_pairs={{0,1},{1,0},{2,3},{3,2},{4,5},{5,4},{6,7},{7,6},{8,9},{9,8},{10,11... | collective-permute-start | bytes 1769480 | tf_op jit(solution)/shard_map/ppermute | solution.py:32
  40.2 4.9 %collective-permute-start.11 = (bf16[128,192]{1,0:T(8,128)(2,1)S(1)}, bf16[128,192]{1,0:T(8,128)(2,1)S(1)}, u32[]{:S(2)}, u32[]{:S(2)}) collective-permute-start(bf16[128,192]{1,0:T(8,128)(2,1)S(1)} %get-tuple-element.192), channel_id=1, source_target_pairs={{0,8},{8,0},{16,24},{24,16},{1,9},{9,1},{17,25},{25,17},{2,10},{10... | collective-permute-start | bytes 147464 | tf_op jit(solution)/shard_map/ppermute | solution.py:32
  41.5 5.0 %collective-permute-start.12 = (bf16[128,192]{1,0:T(8,128)(2,1)S(1)}, bf16[128,192]{1,0:T(8,128)(2,1)S(1)}, u32[]{:S(2)}, u32[]{:S(2)}) collective-permute-start(bf16[128,192]{1,0:T(8,128)(2,1)S(1)} %get-tuple-element.193), channel_id=1, source_target_pairs={{0,16},{8,24},{16,0},{24,8},{1,17},{9,25},{17,1},{25,9},{2,18},{10... | collective-permute-start | bytes 147464 | tf_op jit(solution)/shard_map/ppermute | solution.py:32
  42.1 5.2 %collective-permute-start.13 = (bf16[128,192]{1,0:T(8,128)(2,1)S(1)}, bf16[128,192]{1,0:T(8,128)(2,1)S(1)}, u32[]{:S(2)}, u32[]{:S(2)}) collective-permute-start(bf16[128,192]{1,0:T(8,128)(2,1)S(1)} %get-tuple-element.194), channel_id=1, source_target_pairs={{0,24},{8,16},{16,8},{24,0},{1,25},{9,17},{17,9},{25,1},{2,26},{10... | collective-permute-start | bytes 147464 | tf_op jit(solution)/shard_map/ppermute | solution.py:32
  43.8 1.4 collective-permute-start.10
  56.8 5.4 %collective-permute-start.15 = (bf16[256,4608]{1,0:T(8,128)(2,1)S(1)}, bf16[256,4608]{1,0:T(8,128)(2,1)S(1)}, u32[]{:S(2)}, u32[]{:S(2)}) collective-permute-start(bf16[256,4608]{1,0:T(8,128)(2,1)S(1)} %get-tuple-element.208.refs_4_), channel_id=1, source_target_pairs={{0,1},{1,0},{2,3},{3,2},{4,5},{5,4},{6,7},{7,6},{8,9},{9,8},{10,11... | collective-permute-start | bytes 7077896 | tf_op jit(solution)/shard_map/ppermute | solution.py:32
  56.9 5.4 %collective-permute-start.14 = (bf16[4,4,144,128]{3,2,1,0:T(8,128)(2,1)S(1)}, bf16[4,4,144,128]{3,2,1,0:T(8,128)(2,1)S(1)}, u32[]{:S(2)}, u32[]{:S(2)}) collective-permute-start(bf16[4,4,144,128]{3,2,1,0:T(8,128)(2,1)S(1)} %get-tuple-element.206), channel_id=1, source_target_pairs={{0,1},{1,0},{2,3},{3,2},{4,5},{5,4},{6,7},{7,6},{8,9},{9,8},{10,11... | collective-permute-start | bytes 1769480 | tf_op jit(solution)/shard_map/ppermute | solution.py:32
  57.4 6.8 %collective-permute-start.16 = (bf16[128,384]{1,0:T(8,128)(2,1)S(1)}, bf16[128,384]{1,0:T(8,128)(2,1)S(1)}, u32[]{:S(2)}, u32[]{:S(2)}) collective-permute-start(bf16[128,384]{1,0:T(8,128)(2,1)S(1)} %get-tuple-element.215), channel_id=1, source_target_pairs={{0,8},{8,0},{16,24},{24,16},{1,9},{9,1},{17,25},{25,17},{2,10},{10... | collective-permute-start | bytes 294920 | tf_op jit(solution)/shard_map/ppermute | solution.py:32
  58.9 6.7 %collective-permute-start.17 = (bf16[128,384]{1,0:T(8,128)(2,1)S(1)}, bf16[128,384]{1,0:T(8,128)(2,1)S(1)}, u32[]{:S(2)}, u32[]{:S(2)}) collective-permute-start(bf16[128,384]{1,0:T(8,128)(2,1)S(1)} %get-tuple-element.216), channel_id=1, source_target_pairs={{0,16},{8,24},{16,0},{24,8},{1,17},{9,25},{17,1},{25,9},{2,18},{10... | collective-permute-start | bytes 294920 | tf_op jit(solution)/shard_map/ppermute | solution.py:32
  59.6 6.0 %collective-permute-start.18 = (bf16[128,384]{1,0:T(8,128)(2,1)S(1)}, bf16[128,384]{1,0:T(8,128)(2,1)S(1)}, u32[]{:S(2)}, u32[]{:S(2)}) collective-permute-start(bf16[128,384]{1,0:T(8,128)(2,1)S(1)} %get-tuple-element.217), channel_id=1, source_target_pairs={{0,24},{8,16},{16,8},{24,0},{1,25},{9,17},{17,9},{25,1},{2,26},{10... | collective-permute-start | bytes 294920 | tf_op jit(solution)/shard_map/ppermute | solution.py:32
  65.6 15.8 %collective-permute-start.19 = (bf16[2,2,96,768]{3,2,1,0:T(8,128)(2,1)S(1)}, bf16[2,2,96,768]{3,2,1,0:T(8,128)(2,1)S(1)}, u32[]{:S(2)}, u32[]{:S(2)}) collective-permute-start(bf16[2,2,96,768]{3,2,1,0:T(8,128)(2,1)S(1)} %get-tuple-element.226), channel_id=1, source_target_pairs={{0,8},{8,0},{16,24},{24,16},{1,9},{9,1},{17,25},{25,17},{2,10},{10... | collective-permute-start | bytes 1769480 | tf_op jit(solution)/shard_map/ppermute | solution.py:32
  66.4 15.0 %collective-permute-start.20 = (bf16[2,2,96,768]{3,2,1,0:T(8,128)(2,1)S(1)}, bf16[2,2,96,768]{3,2,1,0:T(8,128)(2,1)S(1)}, u32[]{:S(2)}, u32[]{:S(2)}) collective-permute-start(bf16[2,2,96,768]{3,2,1,0:T(8,128)(2,1)S(1)} %get-tuple-element.227), channel_id=1, source_target_pairs={{0,16},{8,24},{16,0},{24,8},{1,17},{9,25},{17,1},{25,9},{2,18},{10... | collective-permute-start | bytes 1769480 | tf_op jit(solution)/shard_map/ppermute | solution.py:32
  72.9 8.1 %collective-permute-start.23 = (bf16[16,384]{1,0:T(8,128)(2,1)S(1)}, bf16[16,384]{1,0:T(8,128)(2,1)S(1)}, u32[]{:S(2)}, u32[]{:S(2)}) collective-permute-start(bf16[16,384]{1,0:T(8,128)(2,1)S(1)} %slice.159.refs_0_), channel_id=1, source_target_pairs={{0,24},{8,16},{16,8},{24,0},{1,25},{9,17},{17,9},{25,1},{2,26},{10... | collective-permute-start | bytes 36872 | tf_op jit(solution)/shard_map/ppermute | solution.py:32
  74.4 7.0 %collective-permute-start.22 = (bf16[16,384]{1,0:T(8,128)(2,1)S(1)}, bf16[16,384]{1,0:T(8,128)(2,1)S(1)}, u32[]{:S(2)}, u32[]{:S(2)}) collective-permute-start(bf16[16,384]{1,0:T(8,128)(2,1)S(1)} %slice.159.refs_0_), channel_id=1, source_target_pairs={{0,16},{8,24},{16,0},{24,8},{1,17},{9,25},{17,1},{25,9},{2,18},{10... | collective-permute-start | bytes 36872 | tf_op jit(solution)/shard_map/ppermute | solution.py:32
  75.2 6.2 %collective-permute-start.21 = (bf16[16,384]{1,0:T(8,128)(2,1)S(1)}, bf16[16,384]{1,0:T(8,128)(2,1)S(1)}, u32[]{:S(2)}, u32[]{:S(2)}) collective-permute-start(bf16[16,384]{1,0:T(8,128)(2,1)S(1)} %slice.159.refs_0_), channel_id=1, source_target_pairs={{0,8},{8,0},{16,24},{24,16},{1,9},{9,1},{17,25},{25,17},{2,10},{10... | collective-permute-start | bytes 36872 | tf_op jit(solution)/shard_map/ppermute | solution.py:32
  81.8 7.5 %collective-permute-start.24 = (bf16[2,96,768]{2,1,0:T(8,128)(2,1)S(1)}, bf16[2,96,768]{2,1,0:T(8,128)(2,1)S(1)}, u32[]{:S(2)}, u32[]{:S(2)}) collective-permute-start(bf16[2,96,768]{2,1,0:T(8,128)(2,1)S(1)} %get-tuple-element.238), channel_id=1, source_target_pairs={{0,16},{8,24},{16,0},{24,8},{1,17},{9,25},{17,1},{25,9},{2,18},{10... | collective-permute-start | bytes 884744 | tf_op jit(solution)/shard_map/ppermute | solution.py:32
  82.6 6.7 %collective-permute-start.25 = (bf16[2,96,768]{2,1,0:T(8,128)(2,1)S(1)}, bf16[2,96,768]{2,1,0:T(8,128)(2,1)S(1)}, u32[]{:S(2)}, u32[]{:S(2)}) collective-permute-start(bf16[2,96,768]{2,1,0:T(8,128)(2,1)S(1)} %get-tuple-element.239), channel_id=1, source_target_pairs={{0,8},{8,0},{16,24},{24,16},{1,9},{9,1},{17,25},{25,17},{2,10},{10... | collective-permute-start | bytes 884744 | tf_op jit(solution)/shard_map/ppermute | solution.py:32
  89.3 19.9 %collective-permute-start.26 = (bf16[2,2,120,768]{3,2,1,0:T(8,128)(2,1)S(1)}, bf16[2,2,120,768]{3,2,1,0:T(8,128)(2,1)S(1)}, u32[]{:S(2)}, u32[]{:S(2)}) collective-permute-start(bf16[2,2,120,768]{3,2,1,0:T(8,128)(2,1)S(1)} %get-tuple-element.242), channel_id=1, source_target_pairs={{0,8},{8,0},{16,24},{24,16},{1,9},{9,1},{17,25},{25,17},{2,10},{10... | collective-permute-start | bytes 2211848 | tf_op jit(solution)/shard_map/ppermute | solution.py:32
  90.8 18.4 %collective-permute-start.27 = (bf16[2,2,120,768]{3,2,1,0:T(8,128)(2,1)S(1)}, bf16[2,2,120,768]{3,2,1,0:T(8,128)(2,1)S(1)}, u32[]{:S(2)}, u32[]{:S(2)}) collective-permute-start(bf16[2,2,120,768]{3,2,1,0:T(8,128)(2,1)S(1)} %get-tuple-element.243), channel_id=1, source_target_pairs={{0,16},{8,24},{16,0},{24,8},{1,17},{9,25},{17,1},{25,9},{2,18},{10... | collective-permute-start | bytes 2211848 | tf_op jit(solution)/shard_map/ppermute | solution.py:32
  91.5 1.4 collective-permute-start.28
  93.8 9.1 %collective-permute-start.29 = (bf16[2,96,768]{2,1,0:T(8,128)(2,1)S(1)}, bf16[2,96,768]{2,1,0:T(8,128)(2,1)S(1)}, u32[]{:S(2)}, u32[]{:S(2)}) collective-permute-start(bf16[2,96,768]{2,1,0:T(8,128)(2,1)S(1)} %get-tuple-element.267), channel_id=1, source_target_pairs={{0,2},{1,3},{2,0},{3,1},{4,6},{5,7},{6,4},{7,5},{8,10},{9,11},{10,... | collective-permute-start | bytes 884744 | tf_op jit(solution)/shard_map/ppermute | solution.py:32
  103.0 9.2 %collective-permute-start.31 = (bf16[1,96,768]{2,1,0:T(8,128)(2,1)S(1)}, bf16[1,96,768]{2,1,0:T(8,128)(2,1)S(1)}, u32[]{:S(2)}, u32[]{:S(2)}) collective-permute-start(bf16[1,96,768]{2,1,0:T(8,128)(2,1)S(1)} %get-tuple-element.333), channel_id=1, source_target_pairs={{0,4},{1,5},{2,6},{3,7},{4,0},{5,1},{6,2},{7,3},{8,12},{9,13},{10,... | collective-permute-start | bytes 442376 | tf_op jit(solution)/shard_map/ppermute | solution.py:32
  109.1 3.1 %collective-permute-start.30 = (bf16[4,4,24,640]{3,2,1,0:T(8,128)(2,1)S(1)}, bf16[4,4,24,640]{3,2,1,0:T(8,128)(2,1)S(1)}, u32[]{:S(2)}, u32[]{:S(2)}) collective-permute-start(bf16[4,4,24,640]{3,2,1,0:T(8,128)(2,1)S(1)} %get-tuple-element.274), channel_id=1, source_target_pairs={{0,1},{1,0},{2,3},{3,2},{4,5},{5,4},{6,7},{7,6},{8,9},{9,8},{10,11... | collective-permute-start | bytes 1474568 | tf_op jit(solution)/shard_map/ppermute | solution.py:32
  109.4 11.0 %collective-permute-start.33 = (bf16[2,120,768]{2,1,0:T(8,128)(2,1)S(1)}, bf16[2,120,768]{2,1,0:T(8,128)(2,1)S(1)}, u32[]{:S(2)}, u32[]{:S(2)}) collective-permute-start(bf16[2,120,768]{2,1,0:T(8,128)(2,1)S(1)} %get-tuple-element.322), channel_id=1, source_target_pairs={{0,8},{8,0},{16,24},{24,16},{1,9},{9,1},{17,25},{25,17},{2,10},{10... | collective-permute-start | bytes 1105928 | tf_op jit(solution)/shard_map/ppermute | solution.py:32
  111.2 10.8 %collective-permute-start.32 = (bf16[2,120,768]{2,1,0:T(8,128)(2,1)S(1)}, bf16[2,120,768]{2,1,0:T(8,128)(2,1)S(1)}, u32[]{:S(2)}, u32[]{:S(2)}) collective-permute-start(bf16[2,120,768]{2,1,0:T(8,128)(2,1)S(1)} %get-tuple-element.325), channel_id=1, source_target_pairs={{0,16},{8,24},{16,0},{24,8},{1,17},{9,25},{17,1},{25,9},{2,18},{10... | collective-permute-start | bytes 1105928 | tf_op jit(solution)/shard_map/ppermute | solution.py:32
  112.7 10.2 %collective-permute-start.34 = (bf16[2,4,24,640]{3,2,1,0:T(8,128)(2,1)S(1)}, bf16[2,4,24,640]{3,2,1,0:T(8,128)(2,1)S(1)}, u32[]{:S(2)}, u32[]{:S(2)}) collective-permute-start(bf16[2,4,24,640]{3,2,1,0:T(8,128)(2,1)S(1)} %get-tuple-element.336), channel_id=1, source_target_pairs={{0,2},{1,3},{2,0},{3,1},{4,6},{5,7},{6,4},{7,5},{8,10},{9,11},{10,... | collective-permute-start | bytes 737288 | tf_op jit(solution)/shard_map/ppermute | solution.py:32
  123.1 20.0 %copy-start.8 = (bf16[768,768]{1,0:T(8,128)(2,1)S(1)}, bf16[768,768]{1,0:T(8,128)(2,1)}, u32[]{:S(2)}) copy-start(bf16[768,768]{1,0:T(8,128)(2,1)} %wq_ref.3) | copy-start | bytes 3538948
  123.1 12.6 %collective-permute-start.42 = (bf16[2,120,768]{2,1,0:T(8,128)(2,1)S(1)}, bf16[2,120,768]{2,1,0:T(8,128)(2,1)S(1)}, u32[]{:S(2)}, u32[]{:S(2)}) collective-permute-start(bf16[2,120,768]{2,1,0:T(8,128)(2,1)S(1)} %get-tuple-element.280), channel_id=1, source_target_pairs={{0,2},{1,3},{2,0},{3,1},{4,6},{5,7},{6,4},{7,5},{8,10},{9,11},{10,... | collective-permute-start | bytes 1105928 | tf_op jit(solution)/shard_map/ppermute | solution.py:32
  124.9 9.9 %collective-permute-start.35 = (bf16[1,4,24,640]{3,2,1,0:T(8,128)(2,1)S(1)}, bf16[1,4,24,640]{3,2,1,0:T(8,128)(2,1)S(1)}, u32[]{:S(2)}, u32[]{:S(2)}) collective-permute-start(bf16[1,4,24,640]{3,2,1,0:T(8,128)(2,1)S(1)} %pad_maximum_fusion.2), channel_id=1, source_target_pairs={{0,4},{1,5},{2,6},{3,7},{4,0},{5,1},{6,2},{7,3},{8,12},{9,13},{10,... | collective-permute-start | bytes 368648 | tf_op jit(solution)/shard_map/ppermute | solution.py:32
  125.3 14.8 %collective-permute-start.36 = (bf16[256,576]{1,0:T(8,128)(2,1)S(1)}, bf16[256,576]{1,0:T(8,128)(2,1)S(1)}, u32[]{:S(2)}, u32[]{:S(2)}) collective-permute-start(bf16[256,576]{1,0:T(8,128)(2,1)S(1)} %get-tuple-element.288.refs_9_), channel_id=1, source_target_pairs={{0,8},{8,0},{16,24},{24,16},{1,9},{9,1},{17,25},{25,17},{2,10},{10... | collective-permute-start | bytes 884744 | tf_op jit(solution)/shard_map/ppermute | solution.py:32
  126.6 15.5 %collective-permute-start.37 = (bf16[256,576]{1,0:T(8,128)(2,1)S(1)}, bf16[256,576]{1,0:T(8,128)(2,1)S(1)}, u32[]{:S(2)}, u32[]{:S(2)}) collective-permute-start(bf16[256,576]{1,0:T(8,128)(2,1)S(1)} %get-tuple-element.289.refs_10_), channel_id=1, source_target_pairs={{0,16},{8,24},{16,0},{24,8},{1,17},{9,25},{17,1},{25,9},{2,18},{10... | collective-permute-start | bytes 884744 | tf_op jit(solution)/shard_map/ppermute | solution.py:32
  127.2 15.9 %collective-permute-start.38 = (bf16[256,576]{1,0:T(8,128)(2,1)S(1)}, bf16[256,576]{1,0:T(8,128)(2,1)S(1)}, u32[]{:S(2)}, u32[]{:S(2)}) collective-permute-start(bf16[256,576]{1,0:T(8,128)(2,1)S(1)} %get-tuple-element.290.refs_11_), channel_id=1, source_target_pairs={{0,24},{8,16},{16,8},{24,0},{1,25},{9,17},{17,9},{25,1},{2,26},{10... | collective-permute-start | bytes 884744 | tf_op jit(solution)/shard_map/ppermute | solution.py:32
  135.8 12.7 %collective-permute-start.43 = (bf16[1,120,768]{2,1,0:T(8,128)(2,1)S(1)}, bf16[1,120,768]{2,1,0:T(8,128)(2,1)S(1)}, u32[]{:S(2)}, u32[]{:S(2)}) collective-permute-start(bf16[1,120,768]{2,1,0:T(8,128)(2,1)S(1)} %get-tuple-element.330), channel_id=1, source_target_pairs={{0,4},{1,5},{2,6},{3,7},{4,0},{5,1},{6,2},{7,3},{8,12},{9,13},{10,... | collective-permute-start | bytes 552968 | tf_op jit(solution)/shard_map/ppermute | solution.py:32
  138.7 8.3 %collective-permute-start.41 = (bf16[24,640]{1,0:T(8,128)(2,1)S(1)}, bf16[24,640]{1,0:T(8,128)(2,1)S(1)}, u32[]{:S(2)}, u32[]{:S(2)}) collective-permute-start(bf16[24,640]{1,0:T(8,128)(2,1)S(1)} %get-tuple-element.340), channel_id=1, source_target_pairs={{0,24},{8,16},{16,8},{24,0},{1,25},{9,17},{17,9},{25,1},{2,26},{10... | collective-permute-start | bytes 92168 | tf_op jit(solution)/shard_map/ppermute | solution.py:32
  140.1 6.9 %collective-permute-start.40 = (bf16[24,640]{1,0:T(8,128)(2,1)S(1)}, bf16[24,640]{1,0:T(8,128)(2,1)S(1)}, u32[]{:S(2)}, u32[]{:S(2)}) collective-permute-start(bf16[24,640]{1,0:T(8,128)(2,1)S(1)} %get-tuple-element.341), channel_id=1, source_target_pairs={{0,16},{8,24},{16,0},{24,8},{1,17},{9,25},{17,1},{25,9},{2,18},{10... | collective-permute-start | bytes 92168 | tf_op jit(solution)/shard_map/ppermute | solution.py:32
  142.2 4.8 %collective-permute-start.39 = (bf16[24,640]{1,0:T(8,128)(2,1)S(1)}, bf16[24,640]{1,0:T(8,128)(2,1)S(1)}, u32[]{:S(2)}, u32[]{:S(2)}) collective-permute-start(bf16[24,640]{1,0:T(8,128)(2,1)S(1)} %get-tuple-element.342), channel_id=1, source_target_pairs={{0,8},{8,0},{16,24},{24,16},{1,9},{9,1},{17,25},{25,17},{2,10},{10... | collective-permute-start | bytes 92168 | tf_op jit(solution)/shard_map/ppermute | solution.py:32
  (7 other events, 21.0 us)
where the time goes:
time: 150 us
  Pallas kernels  62.4 us (42%)
  starting transfers between devices  48 us (32%)
  waiting for transfers between devices  29.7 us (20%)
  local copies, waits for them, and re-layouts  5.23 us (3%)
  other arithmetic  3.37 us (2%)
    pallas_call x20, Pallas kernels, call(): pl.pallas_call(kernel, out_shape=[o if i in far_out else pltpu.VMEM(o.sha...  62.4 us
    ppermute x44, starting transfers between devices, swap(): lax.ppermute(block, axis, [(i, i ^ mask) for i in range(lax.axis_size(axi...  48 us
    ppermute x44, waiting for transfers between devices, swap(): lax.ppermute(block, axis, [(i, i ^ mask) for i in range(lax.axis_size(axi...  29.7 us
    unnamed x22, local copies, waits for them, and re-layouts  3.85 us
  transfers between devices with their start and end apart: 44, of which 20 were waited for; matrix products, arithmetic and copies ran while one was open for 2% of the time, Pallas kernels for 31%

commit v1 on v0

--- a/solution.py
+++ b/solution.py
@@ -19,7 +19,6 @@
 TN = (((0,), (0,)), ((), ()))
 
 Q_B, V_B, OUT_B, ATTN_G, ATTN_S, RED_B, FIN_G, FIN_S, EXP_B = range(9)
-FRESH, VALID = 1, 2
 N_VEC = 16
 N_SMALL = 32
 
@@ -32,6 +31,21 @@
     return lax.ppermute(block, axis, [(i, i ^ mask) for i in range(lax.axis_size(axis))])
 
 
+FRESH, VALID = 0, 1
+
+
+def flags_kernel(meta_ref, out_ref):
+    new_ref, valid_ref = meta_ref
+    out_ref[...] = jnp.zeros_like(out_ref)
+    out_ref[FRESH : FRESH + 1] = jnp.full((1, out_ref.shape[1]), new_ref[1], jnp.int32)
+    for t in range(2):
+        out_ref[VALID + t : VALID + t + 1] = jnp.full((1, out_ref.shape[1]), valid_ref[t], jnp.int32)
+
+
+def flag(flags_ref, i):
+    return flags_ref[i : i + 1, 0:1]
+
+
 def seg_here():
     return lax.axis_index("seg")
 
@@ -50,20 +64,24 @@
 
 def call(kernel, out_shape, args, micros, far_in=(), far_out=(), scratch=()):
     vmem, far = pl.BlockSpec(memory_space=pltpu.VMEM), pl.BlockSpec(memory_space=pltpu.HBM)
+    integers, *rest = args
     near = [
-        x if i == 0 else pltpu.with_memory_space_constraint(x, pltpu.HBM if i in far_in else pltpu.VMEM)
-        for i, x in enumerate(args)
+        pltpu.with_memory_space_constraint(x, pltpu.HBM if i in far_in else pltpu.VMEM) for i, x in enumerate(rest, 1)
     ]
+
+    def body(*refs):
+        kernel(refs[: len(integers)], *refs[len(integers) :])
+
     return pl.pallas_call(
-        kernel,
+        body,
         out_shape=[o if i in far_out else pltpu.VMEM(o.shape, o.dtype) for i, o in enumerate(out_shape)],
-        in_specs=[pl.BlockSpec(memory_space=pltpu.SMEM)]
+        in_specs=[pl.BlockSpec(memory_space=pltpu.SMEM)] * len(integers)
         + [far if i in far_in else vmem for i in range(1, len(args))],
         out_specs=[vmem] * len(out_shape),
         scratch_shapes=scratch,
         compiler_params=pltpu.CompilerParams(vmem_limit_bytes=8 << 20),
         cost_estimate=pl.CostEstimate(flops=0, transcendentals=0, bytes_accessed=int(micros * 3e6)),
-    )(*near)
+    )(*integers, *near)
 
 
 def reorder(x, seg, n_seg):
@@ -94,17 +112,24 @@
 
 
 def prep_kernel(meta_ref, wq_ref, wk_ref, wv_ref, *refs, n_seg, chunks):
-    vec_refs, (w_ref, b_ref, out_ref, line_ref, sems) = refs[: EXP_B + 1], refs[EXP_B + 1 :]
+    vec_refs, (w_ref, b_ref, out_ref, line_ref, near_ref, sems) = refs[: EXP_B + 1], refs[EXP_B + 1 :]
+    weights = [
+        pltpu.make_async_copy(r, near_ref.at[i], sems.at[EXP_B + 1 + i]) for i, r in enumerate((wq_ref, wk_ref, wv_ref))
+    ]
+    for c in weights:
+        c.start()
     copies = [pltpu.make_async_copy(r, out_ref.at[i], sems.at[i]) for i, r in enumerate(vec_refs[:EXP_B])]
     copies.append(pltpu.make_async_copy(vec_refs[EXP_B], line_ref.at[0], sems.at[EXP_B]))
     for c in copies:
         c.start()
     seg = seg_here()
     rows = w_ref.shape[0] // 8
+    for c in weights:
+        c.wait()
 
     def some_rows(i):
         these = pl.ds(pl.multiple_of(i * rows, rows), rows)
-        w_ref[these] = jnp.concatenate([own_columns(r[these], seg, n_seg) for r in (wq_ref, wk_ref, wv_ref)], axis=1)
+        w_ref[these] = jnp.concatenate([own_columns(near_ref[k, these], seg, n_seg) for k in range(3)], axis=1)
 
     in_loop(8, 1, some_rows)
     for c in copies:
@@ -132,7 +157,7 @@
     for b in range(blocks):
         inside = (row >= b * size) & (row < (b + 1) * size)
         place = jnp.where(inside, ((seg_here() ^ b) - b) * size + row, place)
-    out = (place >= meta_ref[VALID + slot]) & (row < blocks * size) & (col == 0)
+    out = (place >= flag(meta_ref, VALID + slot)) & (row < blocks * size) & (col == 0)
     return jnp.where(out, NEG_FILL, 0.0).astype(BF16)
 
 
@@ -148,12 +173,12 @@
 SCALE = 0.125 * 1.4426950408889634
 
 
-def attn_fwd_kernel(meta_ref, qkv_ref, mem_ref, w_ref, b_ref, *outs, slot, blocks, heads, mem_queries):
+def attn_fwd_kernel(_, meta_ref, qkv_ref, mem_ref, w_ref, b_ref, *outs, slot, blocks, heads, mem_queries):
     if mem_queries:
         memory = mem_ref[...]
     else:
         written_ref, outs = outs[0], outs[1:]
-        memory = jnp.where(meta_ref[FRESH] == 1, mem_ref[...], written_ref[...].astype(BF16))
+        memory = jnp.where(flag(meta_ref, FRESH) == 1, mem_ref[...], written_ref[...].astype(BF16))
         outs[-1][...] = memory
     mix_refs, lse_ref, mem_out_ref = outs[:blocks], outs[blocks], outs[blocks + 1]
     size = qkv_ref.shape[0] // blocks
@@ -181,15 +206,23 @@
             lse_ref[h : h + 1, first : first + queries.shape[0]] = highest * SCALE + jnp.log(total) * 1.4426950408889634
         return jnp.concatenate(out, axis=0).T.astype(BF16)
 
+    def put(b, row, rows):
+        half = mix_refs[b].shape[0]
+        cut = max(0, min(rows.shape[0], half - row))
+        if cut:
+            mix_refs[b][row : row + cut, :width] = rows[:cut]
+        if cut < rows.shape[0]:
+            mix_refs[b][row + cut - half : row + rows.shape[0] - half, width:] = rows[cut:]
+
     for b in range(blocks):
-        mix_refs[b][:size] = mixed_of(qkv_ref[b * size : (b + 1) * size, :width], ones, b * size)
+        put(b, 0, mixed_of(qkv_ref[b * size : (b + 1) * size, :width], ones, b * size))
     if mem_queries:
         mixed = mixed_of(mem_out_ref[:, :width], ones[:mem], blocks * size)
         for b in range(blocks):
-            mix_refs[b][size:] = mixed
-
-
-def attn_bwd_kernel(meta_ref, qkv_ref, mem_ref, lse_ref, *refs, slot, blocks, heads, mem_queries):
+            put(b, size, mixed)
+
+
+def attn_bwd_kernel(_, meta_ref, qkv_ref, mem_ref, lse_ref, *refs, slot, blocks, heads, mem_queries):
     n_grad = blocks + (1 if mem_queries else 0)
     grad_refs, refs = refs[:n_grad], refs[n_grad:]
     more_refs, out_refs, mem_out_ref = refs[: -blocks - 1], refs[-blocks - 1 : -1], refs[-1]
@@ -271,7 +304,7 @@
 N_KEPT = 4
 
 
-def rows_fwd_kernel(meta_ref, *refs, n_seg, n_pair, n_hidden):
+def rows_fwd_kernel(meta_ref, *refs, n_seg, n_pair, n_hidden, together):
     mix_refs, hid_refs = refs[:n_seg], refs[n_seg : n_seg + n_hidden]
     vec_ref, out_ref, exp_ref, red_ref = refs[n_seg + n_hidden : n_seg + n_hidden + 4]
     outs = refs[n_seg + n_hidden + 4 :]
@@ -287,7 +320,11 @@
         left_factors(meta_ref, x, left_refs, at, first, blocks, n_seg, n_pair, size)
 
     each = wide // (n_seg * n_pair * 2)
-    mixed = reorder(jnp.concatenate([r[...] for r in mix_refs], axis=1), seg_here(), n_seg)
+    width = mix_refs[0].shape[1] // 2
+    halves = [
+        jnp.concatenate([r[:, i * width : (i + 1) * width] for r in mix_refs], axis=1).astype(F32) for i in range(2)
+    ]
+    mixed = reorder(jnp.concatenate(halves, axis=0).astype(BF16), seg_here(), n_seg)
     hidden = jnp.concatenate([r[...].astype(F32) for r in hid_refs], axis=0)
     unit, inverse = norm_parts(hidden + (mm(mixed, out_ref[...]) + vec(OUT_B)))
     unit_a_ref[...] = unit
@@ -305,7 +342,7 @@
         acc_ref[...] += mm(active, red_ref[cols])
         keep_left(active, each, q * (n_seg // chunks), n_seg // chunks)
 
-    in_loop(chunks, 2, chunk)
+    in_loop(chunks, together, chunk)
     unit, inverse = norm_parts(acc_ref[...])
     unit_f_ref[...] = unit
     inv_ref[:, 1:2] = inverse
@@ -399,14 +436,14 @@
         return jnp.concatenate([kept_refs[t][i][:size, cols] for t in range(slots)], axis=0)
 
     grad = jnp.concatenate([grad_ref[t].astype(F32) for t in range(slots)], axis=0)
-    mixed = rows_back(seg_here(), n_seg, grad, kept, vec_ref, out_ref, exp_ref, red_ref, outs, acc_ref, 2)
+    mixed = rows_back(seg_here(), n_seg, grad, kept, vec_ref, out_ref, exp_ref, red_ref, outs, acc_ref, 4)
     width = mixed.shape[1] // n_seg
     for m in range(n_seg):
         for t in range(slots):
             mix_refs[m][:, t * width : (t + 1) * width] = mixed[t * size : (t + 1) * size, m * width : (m + 1) * width]
 
 
-def memory_rows_back_kernel(meta_ref, *refs, n_seg, size):
+def memory_rows_back_kernel(_, meta_ref, *refs, n_seg, size):
     d_refs, refs = refs[:n_seg], refs[n_seg:]
     (wk_ref, wv_ref), kept_refs, refs = refs[:2], refs[2 : 2 + N_KEPT], refs[2 + N_KEPT :]
     (vec_ref, out_ref, exp_ref, red_ref), outs, (memory_ref, own_ref, acc_ref) = refs[:4], refs[4:7], refs[7:]
@@ -416,7 +453,7 @@
     d_value = reorder(jnp.concatenate([r[:, width:] for r in d_refs], axis=1), seg, n_seg)
     grad = 2.0 * (mm(d_key, wk_ref[...], NT) + mm(d_value, wv_ref[...], NT))
     memory_ref[...] = grad
-    grad = jnp.where(meta_ref[FRESH] == 1, jnp.zeros_like(grad), grad)
+    grad = jnp.where(flag(meta_ref, FRESH) == 1, jnp.zeros_like(grad), grad)
 
     def kept(i, cols=slice(None)):
         return kept_refs[i][size:, cols]
@@ -430,16 +467,20 @@
     size = out_ref.shape[1]
     width = d_refs[0].shape[1] // 3
     seg = seg_here()
-    for t in range(slots):
-        grad = hidden_ref[t * size : (t + 1) * size]
+
+    def slot(t):
+        these = pl.ds(pl.multiple_of(t * size, size), size)
+        grad = hidden_ref[these]
         for i, w_ref in enumerate((wq_ref, wk_ref, wv_ref)):
-            part = jnp.concatenate([r[t * size : (t + 1) * size, i * width : (i + 1) * width] for r in d_refs], 1)
+            part = jnp.concatenate([r[these, i * width : (i + 1) * width] for r in d_refs], 1)
             grad = grad + mm(reorder(part, seg, n_seg), w_ref[...], NT)
         out_ref[t] = grad.astype(BF16)
 
+    in_loop(slots, 1, slot)
+
 
 def row_parts(stream, chunks, each):
-    if stream == 0:
+    if stream == 1:
         return [(0, each, q, q * each) for q in range(chunks)]
     return [(each, chunks * each, chunks, 0), ((chunks + 1) * each, each, chunks + 1, chunks * each)]
 
@@ -480,10 +521,10 @@
             outs[z & 1][z >> 1, row : row + rows] = total.astype(BF16)
 
 
-def heads_weights_kernel(meta_ref, small_ref, small_m_ref, hid_ref, memory_ref, w_ref, *refs, slots, n_seg):
+def heads_weights_kernel(_, meta_ref, small_ref, small_m_ref, hid_ref, memory_ref, w_ref, *refs, slots, n_seg):
     rows, refs = refs[: slots * n_seg], refs[slots * n_seg :]
     grads, (mem0_ref, mem1_ref, dm0_ref, dm1_ref, keep_ref, send_ref) = refs[:n_seg], refs[n_seg:]
-    seg, core, pair, fresh1 = seg_here(), core_here(), pair_here(), meta_ref[FRESH]
+    seg, core, pair, fresh1 = seg_here(), core_here(), pair_here(), flag(meta_ref, FRESH)
     wide = rows[0].shape[1]
     width = wide // n_seg
     each = keep_ref.shape[2]
@@ -608,12 +649,12 @@
     all_rows = n_seg * size
 
     rows0 = [tokens[0]] + [swap(tokens[0], "seg", m) for m in others]
-    place = jnp.concatenate([new_doc, valid_len])
+    (flags,) = call(flags_kernel, [shape_of(8, 128, dtype=jnp.int32)], ((new_doc, valid_len),), 1)
     w_own, b_own, vecs = call(
         functools.partial(prep_kernel, n_seg=n_seg, chunks=chunks),
         [shape_of(wide, 3 * width), shape_of(1, 3 * width, dtype=F32), shape_of(N_VEC, wide, dtype=F32)],
         (
-            place,
+            (),
             query_proj,
             key_proj,
             value_proj,
@@ -628,25 +669,29 @@
             expand_bias,
         ),
         4,
-        far_in=range(4, 5 + EXP_B),
-        scratch=[pltpu.VMEM((1, hidden_units), F32), pltpu.SemaphoreType.DMA((EXP_B + 1,))],
+        far_in=range(1, 5 + EXP_B),
+        scratch=[
+            pltpu.VMEM((1, hidden_units), F32),
+            pltpu.VMEM((3, wide, wide), BF16),
+            pltpu.SemaphoreType.DMA((EXP_B + 4,)),
+        ],
     )
 
-    second, w_own, *rows0 = lax.optimization_barrier((tokens[1], w_own, *rows0))
+    second, w_own, flags = lax.optimization_barrier((tokens[1], w_own, flags))
     rows = [rows0, [second] + [swap(second, "seg", m) for m in others]]
 
     def project(t):
-        (out,) = call(qkv_kernel, [shape_of(all_rows, 3 * width)], (place, w_own, b_own, *rows[t]), 3)
+        (out,) = call(qkv_kernel, [shape_of(all_rows, 3 * width)], ((), w_own, b_own, *rows[t]), 3)
         return out
 
     def attend(t, qkv, written=()):
         mem_queries = not written
         got = call(
             functools.partial(attn_fwd_kernel, slot=t, blocks=n_seg, heads=heads, mem_queries=mem_queries),
-            [shape_of(size + (mem if mem_queries else 0), width)] * n_seg
+            [shape_of((size + (mem if mem_queries else 0)) // 2, 2 * width)] * n_seg
             + [shape_of(8, all_rows + 128, dtype=F32), shape_of(mem, 3 * width)]
             + [shape_of(mem, wide)] * len(written),
-            (place, qkv, mem_init, w_own, b_own, *written),
+            ((), flags, qkv, mem_init, w_own, b_own, *written),
             8,
         )
         return list(got[:n_seg]), *got[n_seg:]
@@ -655,7 +700,7 @@
         got = call(
             functools.partial(attn_bwd_kernel, slot=t, blocks=n_seg, heads=heads, mem_queries=len(grads) > n_seg),
             [shape_of(size * (2 if more else 1), 3 * width)] * n_seg + [shape_of(mem, 3 * width)],
-            (place, qkv, qkv_mem, lse, *grads, *more),
+            ((), flags, qkv, qkv_mem, lse, *grads, *more),
             8,
         )
         return list(got[:n_seg]), got[n_seg]
@@ -672,7 +717,9 @@
         if len(hidden) > 1:
             left += [shape_of(n_pair, (chunks + 2) * each, mem)] * 2
         got = call(
-            functools.partial(rows_fwd_kernel, n_seg=n_seg, n_pair=n_pair, n_hidden=len(hidden)),
+            functools.partial(
+                rows_fwd_kernel, n_seg=n_seg, n_pair=n_pair, n_hidden=len(hidden), together=1 if len(hidden) > 1 else 4
+            ),
             [
                 shape_of(n_rows, wide, dtype=F32),
                 shape_of(n_rows, 128, dtype=F32),
@@ -681,7 +728,7 @@
                 *result_shapes,
                 *left,
             ],
-            (place, *mixed, *hidden, *weights),
+            ((), *mixed, *hidden, *weights),
             8,
             scratch=[pltpu.VMEM((n_rows, wide), F32)],
         )
@@ -698,7 +745,7 @@
     )
     mixed1, lse1, qkv_mem1, memory1 = attend(1, qkv1, (written,))
     left0_other, left_m_other = swap(left0_send, "doc", 1), swap(left_m_send, "doc", 1)
-    mixed1[0], left0_other, left_m_other = lax.optimization_barrier((mixed1[0], left0_other, left_m_other))
+    mixed1[0], left0_other = lax.optimization_barrier((mixed1[0], left0_other))
     kept1, (layer1,), (left1, left1_send) = rows_forward(trade(mixed1), (tokens[1],), [shape_of(size, wide)])
     left1_other = swap(left1_send, "doc", 1)
     layer_out = jnp.stack([layer0, layer1])
@@ -714,7 +761,7 @@
     got = call(
         functools.partial(token_rows_back_kernel, slots=slots, n_seg=n_seg),
         back_shapes(n_rows) + [shape_of(size, slots * width)] * n_seg,
-        (place, d_out, *kept0, *kept1, *weights),
+        ((), d_out, *kept0, *kept1, *weights),
         10,
         scratch=[pltpu.VMEM((n_rows, wide), F32)],
     )
@@ -726,13 +773,13 @@
     def plain_sum(*parts):
         return sum(p.astype(F32) for p in parts).astype(BF16)
 
-    share = [chunks * each, (chunks + 1) * each]
+    share = [(chunks + 1) * each, chunks * each]
 
     def row_weights(stream, right_other):
         return call(
             functools.partial(rows_weights_kernel, stream=stream, n_seg=n_seg, n_pair=n_pair, each=each),
             [shape_of(n_seg // 2, n_pair // 2, share[stream], wide)] * 4,
-            (place, left0, left1, left0_other, left1_other, right, right_other),
+            ((), left0, left1, left0_other, left1_other, right, right_other),
             2,
         )
 
@@ -757,7 +804,7 @@
     got = call(
         functools.partial(memory_rows_back_kernel, n_seg=n_seg, size=size),
         back_shapes(mem) + [shape_of(mem, wide, dtype=F32), shape_of(mem, width)],
-        (place, *d_mem1_all, key_proj, value_proj, *kept0, *weights),
+        ((), flags, *d_mem1_all, key_proj, value_proj, *kept0, *weights),
         6,
         scratch=[pltpu.VMEM((mem, wide), F32)],
     )
@@ -779,7 +826,7 @@
         keep, send = call(
             functools.partial(quarter_kernel, stream=stream, each=each),
             [shape_of(n_pair // 2, share[stream], wide)] * 2,
-            (place, left_m, left_m_other, right_m, right_m_other, *halves),
+            ((), left_m, left_m_other, right_m, right_m_other, *halves),
             1,
         )
         return keep, send
@@ -792,14 +839,15 @@
     d_qkv, d_mem0 = attend_back(0, qkv0, qkv_mem0, lse0, [*grads, mixed_m], d_qkv1)
 
     came_x, d_mem0 = lax.optimization_barrier((came_x, d_mem0))
-    parts_exp = pair_sum(keep_x, came_x, plain_sum)
+    parts_first = pair_sum(keep_x, came_x, plain_sum)
 
     columns = 3 * width + 2 * N_SMALL
     keep, send = call(
         functools.partial(heads_weights_kernel, slots=slots, n_seg=n_seg),
         [shape_of(n_pair, n_seg, each, columns)] * 2,
         (
-            place,
+            (),
+            flags,
             small,
             small_m,
             hidden_m,
@@ -820,7 +868,7 @@
         return call(
             rows_final_kernel,
             [shape_of(*dims, dtype=F32) for dims in shapes],
-            (place, *parts),
+            ((), *parts),
             1,
             far_out=range(len(shapes)),
         )
@@ -830,25 +878,26 @@
     came_c, came_d, keep = lax.optimization_barrier((came_c, came_d, keep))
     keep_c, send_c, keep_d, send_d = both_sums(keep_c, came_c, keep_d, came_d)
     came_c, came_d = swap(send_c, "seg", 2), swap(send_d, "seg", 1)
-    _, came, parts_exp[1] = lax.optimization_barrier((send_c, came, parts_exp[1]))
+    _, came, parts_first[1] = lax.optimization_barrier((send_c, came, parts_first[1]))
     mine = add(keep, came)
+    mine, *d_qkv = lax.optimization_barrier((mine, *d_qkv))
     came_l = swap(mine[1::2], "doc", 2)
     keep_y, send_y = quarter(1, keep_c, came_c, keep_d, came_d)
-    _, came_l, *d_qkv = lax.optimization_barrier((send_y, came_l, *d_qkv))
+    _, came_l = lax.optimization_barrier((send_y, came_l))
     late = pair_sum(mine[0::2], came_l, add)
-    parts_rest = pair_sum(keep_y, swap(send_y, "doc", 2), plain_sum)
-    (grad_exp,) = rows_final(parts_exp, (each, hidden_units))
+    parts_second = pair_sum(keep_y, swap(send_y, "doc", 2), plain_sum)
+    grad_red, grad_out = rows_final(parts_first, (chunks * each, wide), (each, wide))
 
     back = trade(d_qkv)
     (grad_tokens,) = call(
         functools.partial(tokens_grad_kernel, slots=slots, n_seg=n_seg),
         [shape_of(slots, size, wide)],
-        (place, hidden, query_proj, key_proj, value_proj, *back),
+        ((), hidden, query_proj, key_proj, value_proj, *back),
         3,
         far_out=(0,),
     )
 
-    late[1], grad_exp, layer_out = lax.optimization_barrier((late[1], grad_exp, layer_out))
+    late[1], grad_red, grad_out, layer_out = lax.optimization_barrier((late[1], grad_red, grad_out, layer_out))
     mine = add(*late)
     parts = trade([mine[m] for m in range(n_seg)])
     grad_tokens, *parts = lax.optimization_barrier((grad_tokens, *parts))
@@ -857,11 +906,11 @@
         [shape_of(each, wide, dtype=F32)] * 3
         + [shape_of(1, each, dtype=F32)] * EXP_B
         + [shape_of(1, chunks * each, dtype=F32), shape_of(mem, each, dtype=F32)],
-        (place, *parts),
+        ((), *parts),
         1,
         far_out=range(5 + EXP_B),
     )
-    grad_red, grad_out = rows_final(parts_rest, (chunks * each, wide), (each, wide))
+    (grad_exp,) = rows_final(parts_second, (each, hidden_units))
     grad_q, grad_k, grad_v = got[:3]
     flat = [v.reshape(-1) for v in got[3:-1]]
 

time: 150 us -> 137 us (0.913)
  Pallas kernels: 62.4 us -> 53.9 us
  starting transfers between devices: 48 us -> 44.3 us
  waiting for transfers between devices: 29.7 us -> 32.2 us
  local copies, waits for them, and re-layouts: 5.23 us -> 2.74 us
    pallas_call x20 -> x21, Pallas kernels: 62.4 us -> 53.9 us  [call(): pl.pallas_call(body, out_shape=[o if i in far_out else pltpu.VMEM(o.shape...]
    ppermute x44, starting transfers between devices: 48 us -> 44.3 us  [swap(): lax.ppermute(block, axis, [(i, i ^ mask) for i in range(lax.axis_size(axi...]
    ppermute x44, waiting for transfers between devices: 29.7 us -> 32.2 us  [swap(): lax.ppermute(block, axis, [(i, i ^ mask) for i in range(lax.axis_size(axi...]
    unnamed x22 -> x20, local copies, waits for them, and re-layouts: 3.85 us -> 1.35 us
  transfers between devices with their start and end apart: 44 -> 44, of which waited for: 20 -> 21; matrix products, arithmetic and copies ran while one was open for 2% -> 2% of each run, Pallas kernels for 31% -> 30%
where the time goes in v1:
time: 137 us
  Pallas kernels  53.9 us (39%)
  starting transfers between devices  44.3 us (32%)
  waiting for transfers between devices  32.2 us (24%)
  local copies, waits for them, and re-layouts  2.74 us (2%)
  other arithmetic  2.59 us (2%)
    pallas_call x21, Pallas kernels, call(): pl.pallas_call(body, out_shape=[o if i in far_out else pltpu.VMEM(o.shape...  53.9 us
    ppermute x44, starting transfers between devices, swap(): lax.ppermute(block, axis, [(i, i ^ mask) for i in range(lax.axis_size(axi...  44.3 us
    ppermute x44, waiting for transfers between devices, swap(): lax.ppermute(block, axis, [(i, i ^ mask) for i in range(lax.axis_size(axi...  32.2 us
  transfers between devices with their start and end apart: 44, of which 21 were waited for; matrix products, arithmetic and copies ran while one was open for 2% of the time, Pallas kernels for 30%

profile of v1, /device:TPU:0, one launch (start us, length us, event | category | flops | bytes accessed | tf_op | source)
XLA Modules:
  0.0 136.8 jit_solution(5694034719797389016)
XLA Ops:
  0.7 1.1 slice_bitcast_fusion
  1.8 4.0 %collective-permute-start.2 = (bf16[128,768]{1,0:T(8,128)(2,1)S(1)}, bf16[128,768]{1,0:T(8,128)(2,1)S(1)}, u32[]{:S(2)}, u32[]{:S(2)}) collective-permute-start(bf16[128,768]{1,0:T(8,128)(2,1)S(1)} %get-tuple-element.334.refs_2_.refs_4_.refs_6_), channel_id=1, source_target_pairs={{0,24},{8,16},{16,8},{24,0},{1,25},{9,17},{17,9},{25,1},{2,26},{10... | collective-permute-start | bytes 589832 | tf_op jit(solution)/shard_map/ppermute | solution.py:31
  8.3 4.5 %shard_map.331 = (bf16[768,576]{1,0:T(8,128)(2,1)S(1)}, f32[1,576]{1,0:T(1,128)S(1)}, f32[16,768]{1,0:T(8,128)S(1)}) custom-call(bf16[768,768]{1,0:T(8,128)(2,1)} %refs_1_.5, bf16[768,768]{1,0:T(8,128)(2,1)} %refs_2_.7, bf16[768,768]{1,0:T(8,128)(2,1)} %refs_3_.3, f32[768]{0:T(1024)} %refs_3_.2, f32[768]{0:T(1024)} %refs_4_.1, f32[768]{0:T(1024)} %refs_5_.3, ...), custom_call_target="tpu_custom_call" | custom-call | bytes 12000000 | tf_op jit(solution)/shard_map/pallas_call | solution.py:75
  12.8 2.9 %collective-permute-start.5 = (bf16[128,768]{1,0:T(8,128)(2,1)S(1)}, bf16[128,768]{1,0:T(8,128)(2,1)S(1)}, u32[]{:S(2)}, u32[]{:S(2)}) collective-permute-start(bf16[128,768]{1,0:T(8,128)(2,1)S(1)} %get-tuple-element.170.refs_2_.refs_4_.refs_10_), channel_id=1, source_target_pairs={{0,24},{8,16},{16,8},{24,0},{1,25},{9,17},{17,9},{25,1},{2,26},{10... | collective-permute-start | bytes 589832 | tf_op jit(solution)/shard_map/ppermute | solution.py:31
  16.4 0.8 shard_map.333.refs_1_
  17.2 3.8 %shard_map.334 = (bf16[72,384]{1,0:T(8,128)(2,1)S(1)}, bf16[72,384]{1,0:T(8,128)(2,1)S(1)}, bf16[72,384]{1,0:T(8,128)(2,1)S(1)}, bf16[72,384]{1,0:T(8,128)(2,1)S...) custom-call(s32[8,128]{1,0:T(8,128)S(1)} %shard_map.332.refs_0_, bf16[512,576]{1,0:T(8,128)(2,1)S(1)} %shard_map.333.refs_1_, ...), custom_call_target="tpu_custom_call" | custom-call | bytes 24000000 | tf_op jit(solution)/shard_map/pallas_call | solution.py:75
  21.0 1.9 %collective-permute-start.6 = (bf16[72,384]{1,0:T(8,128)(2,1)S(1)}, bf16[72,384]{1,0:T(8,128)(2,1)S(1)}, u32[]{:S(2)}, u32[]{:S(2)}) collective-permute-start(bf16[72,384]{1,0:T(8,128)(2,1)S(1)} %get-tuple-element.176), channel_id=1, source_target_pairs={{0,8},{8,0},{16,24},{24,16},{1,9},{9,1},{17,25},{25,17},{2,10},{10... | collective-permute-start | bytes 165896 | tf_op jit(solution)/shard_map/ppermute | solution.py:31
  22.9 1.5 %collective-permute-start.7 = (bf16[72,384]{1,0:T(8,128)(2,1)S(1)}, bf16[72,384]{1,0:T(8,128)(2,1)S(1)}, u32[]{:S(2)}, u32[]{:S(2)}) collective-permute-start(bf16[72,384]{1,0:T(8,128)(2,1)S(1)} %get-tuple-element.177), channel_id=1, source_target_pairs={{0,16},{8,24},{16,0},{24,8},{1,17},{9,25},{17,1},{25,9},{2,18},{10... | collective-permute-start | bytes 165896 | tf_op jit(solution)/shard_map/ppermute | solution.py:31
  26.1 1.0 collective-permute-done.7.refs_2_
  27.1 2.4 %collective-permute-done.8.refs_3_ = bf16[72,384]{1,0:T(8,128)(2,1)S(1)} collective-permute-done((bf16[72,384]{1,0:T(8,128)(2,1)S(1)}, bf16[72,384]{1,0:T(8,128)(2,1)S(1)}, u32[]{:S(2)}, u32[]{:S(2)}) %collective-permute-start.8) | collective-permute-done | bytes 55328 | tf_op jit(solution)/shard_map/ppermute | solution.py:31
  29.5 4.6 %shard_map.336 = (f32[144,768]{1,0:T(8,128)S(1)}, f32[144,128]{1,0:T(8,128)S(1)}, f32[144,3072]{1,0:T(8,128)S(1)}, f32[144,768]{1,0:T(8,128)S(1)}, bf16[128,768]...) custom-call(bf16[72,384]{1,0:T(8,128)(2,1)S(1)} %get-tuple-element.1, ...), custom_call_target="tpu_custom_call" | custom-call | bytes 24000000 | tf_op jit(solution)/shard_map/pallas_call | solution.py:75
  34.2 3.1 %shard_map.337 = (bf16[64,384]{1,0:T(8,128)(2,1)S(1)}, bf16[64,384]{1,0:T(8,128)(2,1)S(1)}, bf16[64,384]{1,0:T(8,128)(2,1)S(1)}, bf16[64,384]{1,0:T(8,128)(2,1)S...) custom-call(s32[8,128]{1,0:T(8,128)S(1)} %shard_map.332.refs_0_, ...), custom_call_target="tpu_custom_call" | custom-call | bytes 24000000 | tf_op jit(solution)/shard_map/pallas_call | solution.py:75
  38.0 2.9 %collective-permute-start.12 = (bf16[64,384]{1,0:T(8,128)(2,1)S(1)}, bf16[64,384]{1,0:T(8,128)(2,1)S(1)}, u32[]{:S(2)}, u32[]{:S(2)}) collective-permute-start(bf16[64,384]{1,0:T(8,128)(2,1)S(1)} %get-tuple-element.188), channel_id=1, source_target_pairs={{0,24},{8,16},{16,8},{24,0},{1,25},{9,17},{17,9},{25,1},{2,26},{10... | collective-permute-start | bytes 147464 | tf_op jit(solution)/shard_map/ppermute | solution.py:31
  41.5 1.4 %collective-permute-done.11.refs_2_ = bf16[64,384]{1,0:T(8,128)(2,1)S(1)} collective-permute-done((bf16[64,384]{1,0:T(8,128)(2,1)S(1)}, bf16[64,384]{1,0:T(8,128)(2,1)S(1)}, u32[]{:S(2)}, u32[]{:S(2)}) %collective-permute-start.11) | collective-permute-done | bytes 49184 | tf_op jit(solution)/shard_map/ppermute | solution.py:31
  43.1 3.0 %shard_map.338 = (f32[128,768]{1,0:T(8,128)S(1)}, f32[128,128]{1,0:T(8,128)S(1)}, f32[128,3072]{1,0:T(8,128)S(1)}, f32[128,768]{1,0:T(8,128)S(1)}, bf16[128,768]...) custom-call(bf16[64,384]{1,0:T(8,128)(2,1)S(1)} %get-tuple-element.185.refs_0_, ...), custom_call_target="tpu_custom_call" | custom-call | bytes 24000000 | tf_op jit(solution)/shard_map/pallas_call | solution.py:75
  46.1 4.1 %shard_map.339 = (bf16[256,4608]{1,0:T(8,128)(2,1)S(1)}, f32[256,768]{1,0:T(8,128)S(1)}, f32[16,768]{1,0:T(8,128)S(1)}, bf16[128,384]{1,0:T(8,128)(2,1)S(1)}, bf...) custom-call(bf16[2,128,768]{2,1,0:T(8,128)(2,1)S(1)} %copy-done.6, ...), custom_call_target="tpu_custom_call" | custom-call | bytes 30000000 | tf_op jit(solution)/shard_map/pallas_call | solution.py:75
  50.7 1.8 %collective-permute-start.15 = (bf16[128,384]{1,0:T(8,128)(2,1)S(1)}, bf16[128,384]{1,0:T(8,128)(2,1)S(1)}, u32[]{:S(2)}, u32[]{:S(2)}) collective-permute-start(bf16[128,384]{1,0:T(8,128)(2,1)S(1)} %get-tuple-element.209), channel_id=1, source_target_pairs={{0,8},{8,0},{16,24},{24,16},{1,9},{9,1},{17,25},{25,17},{2,10},{10... | collective-permute-start | bytes 294920 | tf_op jit(solution)/shard_map/ppermute | solution.py:31
  52.6 1.5 %collective-permute-start.16 = (bf16[128,384]{1,0:T(8,128)(2,1)S(1)}, bf16[128,384]{1,0:T(8,128)(2,1)S(1)}, u32[]{:S(2)}, u32[]{:S(2)}) collective-permute-start(bf16[128,384]{1,0:T(8,128)(2,1)S(1)} %get-tuple-element.210), channel_id=1, source_target_pairs={{0,16},{8,24},{16,0},{24,8},{1,17},{9,25},{17,1},{25,9},{2,18},{10... | collective-permute-start | bytes 294920 | tf_op jit(solution)/shard_map/ppermute | solution.py:31
  54.2 1.4 %collective-permute-done.13.refs_3_ = bf16[4,4,144,128]{3,2,1,0:T(8,128)(2,1)S(1)} collective-permute-done((bf16[4,4,144,128]{3,2,1,0:T(8,128)(2,1)S(1)}, bf16[4,4,144,128]{3,2,1,0:T(8,128)(2,1)S(1)}, u32[]{:S(2)}, u32[]{:S(2)}) %collective-permute-start.13) | collective-permute-done | bytes 589856 | tf_op jit(solution)/shard_map/ppermute | solution.py:31
  55.6 1.7 %shard_map.340 = (bf16[2,2,120,768]{3,2,1,0:T(8,128)(2,1)S(1)}, bf16[2,2,120,768]{3,2,1,0:T(8,128)(2,1)S(1)}, bf16[2,2,120,768]{3,2,1,0:T(8,128)(2,1)S(1)}, bf16[2,2,120,768]{3,2,1,0:T(8,128)(2,1)S(1)}) custom-call(bf16[4,4,144,128]{3,2,1,0:T(8,128)(2,1)S(1)} %get-tuple-element.180.refs_0_, bf16[4,4,144,128]{3,2,1,0:T(8,128)(2,1)S(1)} %get-tuple-element.189.refs_1_, ...), custom_call_target="tpu_custom_call" | custom-call | bytes 6000000 | tf_op jit(solution)/shard_map/pallas_call | solution.py:75
  57.4 1.0 collective-permute-done.16.refs_6_
  58.3 1.3 collective-permute-done.17.refs_7_
  59.6 0.8 collective-permute-start.18
  60.4 0.8 collective-permute-start.19
  61.3 5.0 %shard_map.341 = (bf16[128,576]{1,0:T(8,128)(2,1)S(1)}, bf16[128,576]{1,0:T(8,128)(2,1)S(1)}, bf16[128,576]{1,0:T(8,128)(2,1)S(1)}, bf16[128,576]{1,0:T(8,128)(2,1)S(1)}, bf16[16,576]{1,0:T(8,128)(2,1)S(1)}) custom-call(s32[8,128]{1,0:T(8,128)S(1)} %shard_map.332.refs_0_, bf16[512,576]{1,0:T(8,128)(2,1)S(1)} %shard_map.335.refs_1_, ...), custom_call_target="tpu_custom_call" | custom-call | bytes 24000000 | tf_op jit(solution)/shard_map/pallas_call | solution.py:75
  66.3 1.9 %collective-permute-start.22 = (bf16[16,384]{1,0:T(8,128)(2,1)S(1)}, bf16[16,384]{1,0:T(8,128)(2,1)S(1)}, u32[]{:S(2)}, u32[]{:S(2)}) collective-permute-start(bf16[16,384]{1,0:T(8,128)(2,1)S(1)} %slice.159.refs_1_), channel_id=1, source_target_pairs={{0,24},{8,16},{16,8},{24,0},{1,25},{9,17},{17,9},{25,1},{2,26},{10... | collective-permute-start | bytes 36872 | tf_op jit(solution)/shard_map/ppermute | solution.py:31
  68.2 1.2 collective-permute-start.21
  69.8 1.4 %shard_map.342 = (bf16[2,2,96,768]{3,2,1,0:T(8,128)(2,1)S(1)}, bf16[2,2,96,768]{3,2,1,0:T(8,128)(2,1)S(1)}, bf16[2,2,96,768]{3,2,1,0:T(8,128)(2,1)S(1)}, bf16[2,2,96,768]{3,2,1,0:T(8,128)(2,1)S(1)}) custom-call(bf16[4,4,144,128]{3,2,1,0:T(8,128)(2,1)S(1)} %get-tuple-element.180.refs_0_, bf16[4,4,144,128]{3,2,1,0:T(8,128)(2,1)S(1)} %get-tuple-element.189.refs_1_, ...), custom_call_target="tpu_custom_call" | custom-call | bytes 6000000 | tf_op jit(solution)/shard_map/pallas_call | solution.py:75
  71.2 6.6 %collective-permute-done.22.refs_4_ = bf16[16,384]{1,0:T(8,128)(2,1)S(1)} collective-permute-done((bf16[16,384]{1,0:T(8,128)(2,1)S(1)}, bf16[16,384]{1,0:T(8,128)(2,1)S(1)}, u32[]{:S(2)}, u32[]{:S(2)}) %collective-permute-start.22) | collective-permute-done | bytes 12320 | tf_op jit(solution)/shard_map/ppermute | solution.py:31
  78.7 1.3 collective-permute-start.23
  80.6 4.8 %shard_map.343 = (bf16[16,4608]{1,0:T(8,128)(2,1)S(1)}, f32[16,768]{1,0:T(8,128)S(1)}, f32[16,768]{1,0:T(8,128)S(1)}, f32[16,768]{1,0:T(8,128)S(1)}, bf16[16,192]{1,0:T(8,128)(2,1)S(1)}) custom-call(s32[8,128]{1,0:T(8,128)S(1)} %shard_map.332.refs_0_, bf16[16,384]{1,0:T(8,128)(2,1)S(1)} %slice.159.refs_1_, ...), custom_call_target="tpu_custom_call" | custom-call | bytes 18000000 | tf_op jit(solution)/shard_map/pallas_call | solution.py:75
  86.0 1.3 collective-permute-done.23.refs_5_
  87.2 1.4 %collective-permute-done.24.refs_7_ = bf16[2,120,768]{2,1,0:T(8,128)(2,1)S(1)} collective-permute-done((bf16[2,120,768]{2,1,0:T(8,128)(2,1)S(1)}, bf16[2,120,768]{2,1,0:T(8,128)(2,1)S(1)}, u32[]{:S(2)}, u32[]{:S(2)}) %collective-permute-start.24) | collective-permute-done | bytes 368672 | tf_op jit(solution)/shard_map/ppermute | solution.py:31
  89.1 1.6 %collective-permute-start.29 = (bf16[2,120,768]{2,1,0:T(8,128)(2,1)S(1)}, bf16[2,120,768]{2,1,0:T(8,128)(2,1)S(1)}, u32[]{:S(2)}, u32[]{:S(2)}) collective-permute-start(bf16[2,120,768]{2,1,0:T(8,128)(2,1)S(1)} %get-tuple-element.261), channel_id=1, source_target_pairs={{0,2},{1,3},{2,0},{3,1},{4,6},{5,7},{6,4},{7,5},{8,10},{9,11},{10,... | collective-permute-start | bytes 1105928 | tf_op jit(solution)/shard_map/ppermute | solution.py:31
  91.4 0.9 collective-permute-start.26
  92.3 5.9 %shard_map.345 = (bf16[256,576]{1,0:T(8,128)(2,1)S(1)}, bf16[256,576]{1,0:T(8,128)(2,1)S(1)}, bf16[256,576]{1,0:T(8,128)(2,1)S(1)}, bf16[256,576]{1,0:T(8,128)(2,1)S(1)}, bf16[16,576]{1,0:T(8,128)(2,1)S(1)}) custom-call(s32[8,128]{1,0:T(8,128)S(1)} %shard_map.332.refs_0_, bf16[512,576]{1,0:T(8,128)(2,1)S(1)} %shard_map.333.refs_1_, ...), custom_call_target="tpu_custom_call" | custom-call | bytes 24000000 | tf_op jit(solution)/shard_map/pallas_call | solution.py:75
  98.5 2.7 %collective-permute-start.31 = (bf16[1,120,768]{2,1,0:T(8,128)(2,1)S(1)}, bf16[1,120,768]{2,1,0:T(8,128)(2,1)S(1)}, u32[]{:S(2)}, u32[]{:S(2)}) collective-permute-start(bf16[1,120,768]{2,1,0:T(8,128)(2,1)S(1)} %get-tuple-element.327), channel_id=1, source_target_pairs={{0,4},{1,5},{2,6},{3,7},{4,0},{5,1},{6,2},{7,3},{8,12},{9,13},{10,... | collective-permute-start | bytes 552968 | tf_op jit(solution)/shard_map/ppermute | solution.py:31
  101.1 2.9 %shard_map.346 = (bf16[4,4,24,640]{3,2,1,0:T(8,128)(2,1)S(1)}, bf16[4,4,24,640]{3,2,1,0:T(8,128)(2,1)S(1)}) custom-call(s32[8,128]{1,0:T(8,128)S(1)} %shard_map.332.refs_0_, f32[16,768]{1,0:T(8,128)S(1)} %get-tuple-element.238.refs_1_, f32[16,768]{1,0:T(8,128)S(1)} %get-tuple-element.239.refs_2_, f32[16,768]{1,0:T(8,128)S(1)} %get-tuple-element.240.refs_3_, ...), custom_call_target="tpu_custom_call" | custom-call | bytes 18000000 | tf_op jit(solution)/shard_map/pallas_call | solution.py:75
  104.4 1.2 collective-permute-done.26
  106.5 1.1 collective-permute-start.32
  109.9 2.2 %collective-permute-start.36 = (bf16[256,576]{1,0:T(8,128)(2,1)S(1)}, bf16[256,576]{1,0:T(8,128)(2,1)S(1)}, u32[]{:S(2)}, u32[]{:S(2)}) collective-permute-start(bf16[256,576]{1,0:T(8,128)(2,1)S(1)} %get-tuple-element.285.refs_15_), channel_id=1, source_target_pairs={{0,8},{8,0},{16,24},{24,16},{1,9},{9,1},{17,25},{25,17},{2,10},{10... | collective-permute-start | bytes 884744 | tf_op jit(solution)/shard_map/ppermute | solution.py:31
  113.5 1.5 %collective-permute-done.33.refs_7_ = bf16[2,96,768]{2,1,0:T(8,128)(2,1)S(1)} collective-permute-done((bf16[2,96,768]{2,1,0:T(8,128)(2,1)S(1)}, bf16[2,96,768]{2,1,0:T(8,128)(2,1)S(1)}, u32[]{:S(2)}, u32[]{:S(2)}) %collective-permute-start.33) | collective-permute-done | bytes 294944 | tf_op jit(solution)/shard_map/ppermute | solution.py:31
  115.1 1.8 %collective-permute-start.38 = (bf16[256,576]{1,0:T(8,128)(2,1)S(1)}, bf16[256,576]{1,0:T(8,128)(2,1)S(1)}, u32[]{:S(2)}, u32[]{:S(2)}) collective-permute-start(bf16[256,576]{1,0:T(8,128)(2,1)S(1)} %get-tuple-element.287.refs_17_), channel_id=1, source_target_pairs={{0,24},{8,16},{16,8},{24,0},{1,25},{9,17},{17,9},{25,1},{2,26},{10... | collective-permute-start | bytes 884744 | tf_op jit(solution)/shard_map/ppermute | solution.py:31
  118.9 8.5 %collective-permute-done.42 = bf16[2,96,768]{2,1,0:T(8,128)(2,1)S(1)} collective-permute-done((bf16[2,96,768]{2,1,0:T(8,128)(2,1)S(1)}, bf16[2,96,768]{2,1,0:T(8,128)(2,1)S(1)}, u32[]{:S(2)}, u32[]{:S(2)}) %collective-permute-start.42) | collective-permute-done | bytes 294944 | tf_op jit(solution)/shard_map/ppermute | solution.py:31
  127.9 1.6 %collective-permute-start.41 = (bf16[24,640]{1,0:T(8,128)(2,1)S(1)}, bf16[24,640]{1,0:T(8,128)(2,1)S(1)}, u32[]{:S(2)}, u32[]{:S(2)}) collective-permute-start(bf16[24,640]{1,0:T(8,128)(2,1)S(1)} %get-tuple-element.336), channel_id=1, source_target_pairs={{0,24},{8,16},{16,8},{24,0},{1,25},{9,17},{17,9},{25,1},{2,26},{10... | collective-permute-start | bytes 92168 | tf_op jit(solution)/shard_map/ppermute | solution.py:31
  129.5 1.6 %collective-permute-start.40 = (bf16[24,640]{1,0:T(8,128)(2,1)S(1)}, bf16[24,640]{1,0:T(8,128)(2,1)S(1)}, u32[]{:S(2)}, u32[]{:S(2)}) collective-permute-start(bf16[24,640]{1,0:T(8,128)(2,1)S(1)} %get-tuple-element.337), channel_id=1, source_target_pairs={{0,16},{8,24},{16,0},{24,8},{1,17},{9,25},{17,1},{25,9},{2,18},{10... | collective-permute-start | bytes 92168 | tf_op jit(solution)/shard_map/ppermute | solution.py:31
  131.5 3.5 %shard_map.349 = bf16[2,128,768]{2,1,0:T(8,128)(2,1)} custom-call(f32[256,768]{1,0:T(8,128)S(1)} %get-tuple-element.283.refs_0_, bf16[768,768]{1,0:T(8,128)(2,1)S(1)} %copy-done.5, bf16[768,768]{1,0:T(8,128)(2,1)S(1)} %copy-done.3, bf16[768,768]{1,0:T(8,128)(2,1)S(1)} %copy-done.4, bf16[256,576]{1,0:T(8,128)(2,1)S(1)} %get-tuple-element.284.refs_14_.refs_4_, ...), custom_call_target="tpu_custom_call" | custom-call | bytes 9000000 | tf_op jit(solution)/shard_map/pallas_call | solution.py:75
  135.0 1.0 shard_map.350
  (105 shorter events, 19.4 us)
Async XLA Ops:
  0.7 28.9 %copy-start.2 = (bf16[768,768]{1,0:T(8,128)(2,1)S(1)}, bf16[768,768]{1,0:T(8,128)(2,1)}, u32[]{:S(2)}) copy-start(bf16[768,768]{1,0:T(8,128)(2,1)} %refs_12_.3) | copy-start | bytes 3538948
  1.8 14.4 %collective-permute-start.2 = (bf16[128,768]{1,0:T(8,128)(2,1)S(1)}, bf16[128,768]{1,0:T(8,128)(2,1)S(1)}, u32[]{:S(2)}, u32[]{:S(2)}) collective-permute-start(bf16[128,768]{1,0:T(8,128)(2,1)S(1)} %get-tuple-element.334.refs_2_.refs_4_.refs_6_), channel_id=1, source_target_pairs={{0,24},{8,16},{16,8},{24,0},{1,25},{9,17},{17,9},{25,1},{2,26},{10... | collective-permute-start | bytes 589832 | tf_op jit(solution)/shard_map/ppermute | solution.py:31
  5.8 10.6 %collective-permute-start.1 = (bf16[128,768]{1,0:T(8,128)(2,1)S(1)}, bf16[128,768]{1,0:T(8,128)(2,1)S(1)}, u32[]{:S(2)}, u32[]{:S(2)}) collective-permute-start(bf16[128,768]{1,0:T(8,128)(2,1)S(1)} %get-tuple-element.334.refs_2_.refs_4_.refs_6_), channel_id=1, source_target_pairs={{0,16},{8,24},{16,0},{24,8},{1,17},{9,25},{17,1},{25,9},{2,18},{10... | collective-permute-start | bytes 589832 | tf_op jit(solution)/shard_map/ppermute | solution.py:31
  6.3 10.1 %collective-permute-start = (bf16[128,768]{1,0:T(8,128)(2,1)S(1)}, bf16[128,768]{1,0:T(8,128)(2,1)S(1)}, u32[]{:S(2)}, u32[]{:S(2)}) collective-permute-start(bf16[128,768]{1,0:T(8,128)(2,1)S(1)} %get-tuple-element.334.refs_2_.refs_4_.refs_6_), channel_id=1, source_target_pairs={{0,8},{8,0},{16,24},{24,16},{1,9},{9,1},{17,25},{25,17},{2,10},{10... | collective-permute-start | bytes 589832 | tf_op jit(solution)/shard_map/ppermute | solution.py:31
  8.3 21.2 %copy-start.1 = (bf16[3072,768]{1,0:T(8,128)(2,1)S(1)}, bf16[3072,768]{1,0:T(8,128)(2,1)}, u32[]{:S(2)}) copy-start(bf16[3072,768]{1,0:T(8,128)(2,1)} %refs_14_.1) | copy-start | bytes 14155780
  12.8 11.6 %collective-permute-start.5 = (bf16[128,768]{1,0:T(8,128)(2,1)S(1)}, bf16[128,768]{1,0:T(8,128)(2,1)S(1)}, u32[]{:S(2)}, u32[]{:S(2)}) collective-permute-start(bf16[128,768]{1,0:T(8,128)(2,1)S(1)} %get-tuple-element.170.refs_2_.refs_4_.refs_10_), channel_id=1, source_target_pairs={{0,24},{8,16},{16,8},{24,0},{1,25},{9,17},{17,9},{25,1},{2,26},{10... | collective-permute-start | bytes 589832 | tf_op jit(solution)/shard_map/ppermute | solution.py:31
  15.7 8.8 %collective-permute-start.4 = (bf16[128,768]{1,0:T(8,128)(2,1)S(1)}, bf16[128,768]{1,0:T(8,128)(2,1)S(1)}, u32[]{:S(2)}, u32[]{:S(2)}) collective-permute-start(bf16[128,768]{1,0:T(8,128)(2,1)S(1)} %get-tuple-element.170.refs_2_.refs_4_.refs_10_), channel_id=1, source_target_pairs={{0,16},{8,24},{16,0},{24,8},{1,17},{9,25},{17,1},{25,9},{2,18},{10... | collective-permute-start | bytes 589832 | tf_op jit(solution)/shard_map/ppermute | solution.py:31
  16.3 8.7 %collective-permute-start.3 = (bf16[128,768]{1,0:T(8,128)(2,1)S(1)}, bf16[128,768]{1,0:T(8,128)(2,1)S(1)}, u32[]{:S(2)}, u32[]{:S(2)}) collective-permute-start(bf16[128,768]{1,0:T(8,128)(2,1)S(1)} %get-tuple-element.170.refs_2_.refs_4_.refs_10_), channel_id=1, source_target_pairs={{0,8},{8,0},{16,24},{24,16},{1,9},{9,1},{17,25},{25,17},{2,10},{10... | collective-permute-start | bytes 589832 | tf_op jit(solution)/shard_map/ppermute | solution.py:31
  16.4 13.1 %copy-start = (bf16[768,3072]{1,0:T(8,128)(2,1)S(1)}, bf16[768,3072]{1,0:T(8,128)(2,1)}, u32[]{:S(2)}) copy-start(bf16[768,3072]{1,0:T(8,128)(2,1)} %refs_13_.1) | copy-start | bytes 14155780
  21.0 5.0 %collective-permute-start.6 = (bf16[72,384]{1,0:T(8,128)(2,1)S(1)}, bf16[72,384]{1,0:T(8,128)(2,1)S(1)}, u32[]{:S(2)}, u32[]{:S(2)}) collective-permute-start(bf16[72,384]{1,0:T(8,128)(2,1)S(1)} %get-tuple-element.176), channel_id=1, source_target_pairs={{0,8},{8,0},{16,24},{24,16},{1,9},{9,1},{17,25},{25,17},{2,10},{10... | collective-permute-start | bytes 165896 | tf_op jit(solution)/shard_map/ppermute | solution.py:31
  22.9 4.2 %collective-permute-start.7 = (bf16[72,384]{1,0:T(8,128)(2,1)S(1)}, bf16[72,384]{1,0:T(8,128)(2,1)S(1)}, u32[]{:S(2)}, u32[]{:S(2)}) collective-permute-start(bf16[72,384]{1,0:T(8,128)(2,1)S(1)} %get-tuple-element.177), channel_id=1, source_target_pairs={{0,16},{8,24},{16,0},{24,8},{1,17},{9,25},{17,1},{25,9},{2,18},{10... | collective-permute-start | bytes 165896 | tf_op jit(solution)/shard_map/ppermute | solution.py:31
  24.5 5.1 %collective-permute-start.8 = (bf16[72,384]{1,0:T(8,128)(2,1)S(1)}, bf16[72,384]{1,0:T(8,128)(2,1)S(1)}, u32[]{:S(2)}, u32[]{:S(2)}) collective-permute-start(bf16[72,384]{1,0:T(8,128)(2,1)S(1)} %get-tuple-element.178), channel_id=1, source_target_pairs={{0,24},{8,16},{16,8},{24,0},{1,25},{9,17},{17,9},{25,1},{2,26},{10... | collective-permute-start | bytes 165896 | tf_op jit(solution)/shard_map/ppermute | solution.py:31
  34.2 6.7 %collective-permute-start.9 = (bf16[4,4,144,128]{3,2,1,0:T(8,128)(2,1)S(1)}, bf16[4,4,144,128]{3,2,1,0:T(8,128)(2,1)S(1)}, u32[]{:S(2)}, u32[]{:S(2)}) collective-permute-start(bf16[4,4,144,128]{3,2,1,0:T(8,128)(2,1)S(1)} %get-tuple-element.184), channel_id=1, source_target_pairs={{0,1},{1,0},{2,3},{3,2},{4,5},{5,4},{6,7},{7,6},{8,9},{9,8},{10,11... | collective-permute-start | bytes 1769480 | tf_op jit(solution)/shard_map/ppermute | solution.py:31
  37.3 4.2 %collective-permute-start.10 = (bf16[64,384]{1,0:T(8,128)(2,1)S(1)}, bf16[64,384]{1,0:T(8,128)(2,1)S(1)}, u32[]{:S(2)}, u32[]{:S(2)}) collective-permute-start(bf16[64,384]{1,0:T(8,128)(2,1)S(1)} %get-tuple-element.186), channel_id=1, source_target_pairs={{0,8},{8,0},{16,24},{24,16},{1,9},{9,1},{17,25},{25,17},{2,10},{10... | collective-permute-start | bytes 147464 | tf_op jit(solution)/shard_map/ppermute | solution.py:31
  37.9 5.0 %collective-permute-start.11 = (bf16[64,384]{1,0:T(8,128)(2,1)S(1)}, bf16[64,384]{1,0:T(8,128)(2,1)S(1)}, u32[]{:S(2)}, u32[]{:S(2)}) collective-permute-start(bf16[64,384]{1,0:T(8,128)(2,1)S(1)} %get-tuple-element.187), channel_id=1, source_target_pairs={{0,16},{8,24},{16,0},{24,8},{1,17},{9,25},{17,1},{25,9},{2,18},{10... | collective-permute-start | bytes 147464 | tf_op jit(solution)/shard_map/ppermute | solution.py:31
  38.0 5.0 %collective-permute-start.12 = (bf16[64,384]{1,0:T(8,128)(2,1)S(1)}, bf16[64,384]{1,0:T(8,128)(2,1)S(1)}, u32[]{:S(2)}, u32[]{:S(2)}) collective-permute-start(bf16[64,384]{1,0:T(8,128)(2,1)S(1)} %get-tuple-element.188), channel_id=1, source_target_pairs={{0,24},{8,16},{16,8},{24,0},{1,25},{9,17},{17,9},{25,1},{2,26},{10... | collective-permute-start | bytes 147464 | tf_op jit(solution)/shard_map/ppermute | solution.py:31
  50.2 5.4 %collective-permute-start.14 = (bf16[256,4608]{1,0:T(8,128)(2,1)S(1)}, bf16[256,4608]{1,0:T(8,128)(2,1)S(1)}, u32[]{:S(2)}, u32[]{:S(2)}) collective-permute-start(bf16[256,4608]{1,0:T(8,128)(2,1)S(1)} %get-tuple-element.202.refs_4_), channel_id=1, source_target_pairs={{0,1},{1,0},{2,3},{3,2},{4,5},{5,4},{6,7},{7,6},{8,9},{9,8},{10,11... | collective-permute-start | bytes 7077896 | tf_op jit(solution)/shard_map/ppermute | solution.py:31
  50.2 5.4 %collective-permute-start.13 = (bf16[4,4,144,128]{3,2,1,0:T(8,128)(2,1)S(1)}, bf16[4,4,144,128]{3,2,1,0:T(8,128)(2,1)S(1)}, u32[]{:S(2)}, u32[]{:S(2)}) collective-permute-start(bf16[4,4,144,128]{3,2,1,0:T(8,128)(2,1)S(1)} %get-tuple-element.200), channel_id=1, source_target_pairs={{0,1},{1,0},{2,3},{3,2},{4,5},{5,4},{6,7},{7,6},{8,9},{9,8},{10,11... | collective-permute-start | bytes 1769480 | tf_op jit(solution)/shard_map/ppermute | solution.py:31
  50.7 6.6 %collective-permute-start.15 = (bf16[128,384]{1,0:T(8,128)(2,1)S(1)}, bf16[128,384]{1,0:T(8,128)(2,1)S(1)}, u32[]{:S(2)}, u32[]{:S(2)}) collective-permute-start(bf16[128,384]{1,0:T(8,128)(2,1)S(1)} %get-tuple-element.209), channel_id=1, source_target_pairs={{0,8},{8,0},{16,24},{24,16},{1,9},{9,1},{17,25},{25,17},{2,10},{10... | collective-permute-start | bytes 294920 | tf_op jit(solution)/shard_map/ppermute | solution.py:31
  52.6 5.7 %collective-permute-start.16 = (bf16[128,384]{1,0:T(8,128)(2,1)S(1)}, bf16[128,384]{1,0:T(8,128)(2,1)S(1)}, u32[]{:S(2)}, u32[]{:S(2)}) collective-permute-start(bf16[128,384]{1,0:T(8,128)(2,1)S(1)} %get-tuple-element.210), channel_id=1, source_target_pairs={{0,16},{8,24},{16,0},{24,8},{1,17},{9,25},{17,1},{25,9},{2,18},{10... | collective-permute-start | bytes 294920 | tf_op jit(solution)/shard_map/ppermute | solution.py:31
  54.1 5.5 %collective-permute-start.17 = (bf16[128,384]{1,0:T(8,128)(2,1)S(1)}, bf16[128,384]{1,0:T(8,128)(2,1)S(1)}, u32[]{:S(2)}, u32[]{:S(2)}) collective-permute-start(bf16[128,384]{1,0:T(8,128)(2,1)S(1)} %get-tuple-element.211), channel_id=1, source_target_pairs={{0,24},{8,16},{16,8},{24,0},{1,25},{9,17},{17,9},{25,1},{2,26},{10... | collective-permute-start | bytes 294920 | tf_op jit(solution)/shard_map/ppermute | solution.py:31
  59.6 18.7 %collective-permute-start.18 = (bf16[2,2,120,768]{3,2,1,0:T(8,128)(2,1)S(1)}, bf16[2,2,120,768]{3,2,1,0:T(8,128)(2,1)S(1)}, u32[]{:S(2)}, u32[]{:S(2)}) collective-permute-start(bf16[2,2,120,768]{3,2,1,0:T(8,128)(2,1)S(1)} %get-tuple-element.220), channel_id=1, source_target_pairs={{0,8},{8,0},{16,24},{24,16},{1,9},{9,1},{17,25},{25,17},{2,10},{10... | collective-permute-start | bytes 2211848 | tf_op jit(solution)/shard_map/ppermute | solution.py:31
  60.4 17.9 %collective-permute-start.19 = (bf16[2,2,120,768]{3,2,1,0:T(8,128)(2,1)S(1)}, bf16[2,2,120,768]{3,2,1,0:T(8,128)(2,1)S(1)}, u32[]{:S(2)}, u32[]{:S(2)}) collective-permute-start(bf16[2,2,120,768]{3,2,1,0:T(8,128)(2,1)S(1)} %get-tuple-element.221), channel_id=1, source_target_pairs={{0,16},{8,24},{16,0},{24,8},{1,17},{9,25},{17,1},{25,9},{2,18},{10... | collective-permute-start | bytes 2211848 | tf_op jit(solution)/shard_map/ppermute | solution.py:31
  66.3 11.5 %collective-permute-start.22 = (bf16[16,384]{1,0:T(8,128)(2,1)S(1)}, bf16[16,384]{1,0:T(8,128)(2,1)S(1)}, u32[]{:S(2)}, u32[]{:S(2)}) collective-permute-start(bf16[16,384]{1,0:T(8,128)(2,1)S(1)} %slice.159.refs_1_), channel_id=1, source_target_pairs={{0,24},{8,16},{16,8},{24,0},{1,25},{9,17},{17,9},{25,1},{2,26},{10... | collective-permute-start | bytes 36872 | tf_op jit(solution)/shard_map/ppermute | solution.py:31
  68.2 10.2 %collective-permute-start.21 = (bf16[16,384]{1,0:T(8,128)(2,1)S(1)}, bf16[16,384]{1,0:T(8,128)(2,1)S(1)}, u32[]{:S(2)}, u32[]{:S(2)}) collective-permute-start(bf16[16,384]{1,0:T(8,128)(2,1)S(1)} %slice.159.refs_1_), channel_id=1, source_target_pairs={{0,16},{8,24},{16,0},{24,8},{1,17},{9,25},{17,1},{25,9},{2,18},{10... | collective-permute-start | bytes 36872 | tf_op jit(solution)/shard_map/ppermute | solution.py:31
  69.3 9.0 %collective-permute-start.20 = (bf16[16,384]{1,0:T(8,128)(2,1)S(1)}, bf16[16,384]{1,0:T(8,128)(2,1)S(1)}, u32[]{:S(2)}, u32[]{:S(2)}) collective-permute-start(bf16[16,384]{1,0:T(8,128)(2,1)S(1)} %slice.159.refs_1_), channel_id=1, source_target_pairs={{0,8},{8,0},{16,24},{24,16},{1,9},{9,1},{17,25},{25,17},{2,10},{10... | collective-permute-start | bytes 36872 | tf_op jit(solution)/shard_map/ppermute | solution.py:31
  78.7 8.5 %collective-permute-start.23 = (bf16[2,120,768]{2,1,0:T(8,128)(2,1)S(1)}, bf16[2,120,768]{2,1,0:T(8,128)(2,1)S(1)}, u32[]{:S(2)}, u32[]{:S(2)}) collective-permute-start(bf16[2,120,768]{2,1,0:T(8,128)(2,1)S(1)} %get-tuple-element.232), channel_id=1, source_target_pairs={{0,16},{8,24},{16,0},{24,8},{1,17},{9,25},{17,1},{25,9},{2,18},{10... | collective-permute-start | bytes 1105928 | tf_op jit(solution)/shard_map/ppermute | solution.py:31
  80.1 8.6 %collective-permute-start.24 = (bf16[2,120,768]{2,1,0:T(8,128)(2,1)S(1)}, bf16[2,120,768]{2,1,0:T(8,128)(2,1)S(1)}, u32[]{:S(2)}, u32[]{:S(2)}) collective-permute-start(bf16[2,120,768]{2,1,0:T(8,128)(2,1)S(1)} %get-tuple-element.233), channel_id=1, source_target_pairs={{0,8},{8,0},{16,24},{24,16},{1,9},{9,1},{17,25},{25,17},{2,10},{10... | collective-permute-start | bytes 1105928 | tf_op jit(solution)/shard_map/ppermute | solution.py:31
  85.4 3.2 %collective-permute-start.28 = (bf16[16,4608]{1,0:T(8,128)(2,1)S(1)}, bf16[16,4608]{1,0:T(8,128)(2,1)S(1)}, u32[]{:S(2)}, u32[]{:S(2)}) collective-permute-start(bf16[16,4608]{1,0:T(8,128)(2,1)S(1)} %get-tuple-element.246.refs_2_), channel_id=1, source_target_pairs={{0,1},{1,0},{2,3},{3,2},{4,5},{5,4},{6,7},{7,6},{8,9},{9,8},{10,11... | collective-permute-start | bytes 442376 | tf_op jit(solution)/shard_map/ppermute | solution.py:31
  85.5 3.2 %collective-permute-start.27 = (bf16[4,144,16]{2,1,0:T(8,128)(2,1)S(1)}, bf16[4,144,16]{2,1,0:T(8,128)(2,1)S(1)}, u32[]{:S(2)}, u32[]{:S(2)}) collective-permute-start(bf16[4,144,16]{2,1,0:T(8,128)(2,1)S(1)} %get-tuple-element.245), channel_id=1, source_target_pairs={{0,1},{1,0},{2,3},{3,2},{4,5},{5,4},{6,7},{7,6},{8,9},{9,8},{10,11... | collective-permute-start | bytes 55304 | tf_op jit(solution)/shard_map/ppermute | solution.py:31
  89.1 9.3 %collective-permute-start.29 = (bf16[2,120,768]{2,1,0:T(8,128)(2,1)S(1)}, bf16[2,120,768]{2,1,0:T(8,128)(2,1)S(1)}, u32[]{:S(2)}, u32[]{:S(2)}) collective-permute-start(bf16[2,120,768]{2,1,0:T(8,128)(2,1)S(1)} %get-tuple-element.261), channel_id=1, source_target_pairs={{0,2},{1,3},{2,0},{3,1},{4,6},{5,7},{6,4},{7,5},{8,10},{9,11},{10,... | collective-permute-start | bytes 1105928 | tf_op jit(solution)/shard_map/ppermute | solution.py:31
  90.7 13.7 %collective-permute-start.25 = (bf16[2,2,96,768]{3,2,1,0:T(8,128)(2,1)S(1)}, bf16[2,2,96,768]{3,2,1,0:T(8,128)(2,1)S(1)}, u32[]{:S(2)}, u32[]{:S(2)}) collective-permute-start(bf16[2,2,96,768]{3,2,1,0:T(8,128)(2,1)S(1)} %get-tuple-element.236), channel_id=1, source_target_pairs={{0,8},{8,0},{16,24},{24,16},{1,9},{9,1},{17,25},{25,17},{2,10},{10... | collective-permute-start | bytes 1769480 | tf_op jit(solution)/shard_map/ppermute | solution.py:31
  91.4 14.2 %collective-permute-start.26 = (bf16[2,2,96,768]{3,2,1,0:T(8,128)(2,1)S(1)}, bf16[2,2,96,768]{3,2,1,0:T(8,128)(2,1)S(1)}, u32[]{:S(2)}, u32[]{:S(2)}) collective-permute-start(bf16[2,2,96,768]{3,2,1,0:T(8,128)(2,1)S(1)} %get-tuple-element.237), channel_id=1, source_target_pairs={{0,16},{8,24},{16,0},{24,8},{1,17},{9,25},{17,1},{25,9},{2,18},{10... | collective-permute-start | bytes 1769480 | tf_op jit(solution)/shard_map/ppermute | solution.py:31
  98.5 9.9 %collective-permute-start.31 = (bf16[1,120,768]{2,1,0:T(8,128)(2,1)S(1)}, bf16[1,120,768]{2,1,0:T(8,128)(2,1)S(1)}, u32[]{:S(2)}, u32[]{:S(2)}) collective-permute-start(bf16[1,120,768]{2,1,0:T(8,128)(2,1)S(1)} %get-tuple-element.327), channel_id=1, source_target_pairs={{0,4},{1,5},{2,6},{3,7},{4,0},{5,1},{6,2},{7,3},{8,12},{9,13},{10,... | collective-permute-start | bytes 552968 | tf_op jit(solution)/shard_map/ppermute | solution.py:31
  104.1 4.3 %collective-permute-start.30 = (bf16[4,4,24,640]{3,2,1,0:T(8,128)(2,1)S(1)}, bf16[4,4,24,640]{3,2,1,0:T(8,128)(2,1)S(1)}, u32[]{:S(2)}, u32[]{:S(2)}) collective-permute-start(bf16[4,4,24,640]{3,2,1,0:T(8,128)(2,1)S(1)} %get-tuple-element.268), channel_id=1, source_target_pairs={{0,1},{1,0},{2,3},{3,2},{4,5},{5,4},{6,7},{7,6},{8,9},{9,8},{10,11... | collective-permute-start | bytes 1474568 | tf_op jit(solution)/shard_map/ppermute | solution.py:31
  105.8 9.3 %collective-permute-start.33 = (bf16[2,96,768]{2,1,0:T(8,128)(2,1)S(1)}, bf16[2,96,768]{2,1,0:T(8,128)(2,1)S(1)}, u32[]{:S(2)}, u32[]{:S(2)}) collective-permute-start(bf16[2,96,768]{2,1,0:T(8,128)(2,1)S(1)} %get-tuple-element.322), channel_id=1, source_target_pairs={{0,8},{8,0},{16,24},{24,16},{1,9},{9,1},{17,25},{25,17},{2,10},{10... | collective-permute-start | bytes 884744 | tf_op jit(solution)/shard_map/ppermute | solution.py:31
  106.5 10.3 %collective-permute-start.32 = (bf16[2,96,768]{2,1,0:T(8,128)(2,1)S(1)}, bf16[2,96,768]{2,1,0:T(8,128)(2,1)S(1)}, u32[]{:S(2)}, u32[]{:S(2)}) collective-permute-start(bf16[2,96,768]{2,1,0:T(8,128)(2,1)S(1)} %get-tuple-element.325), channel_id=1, source_target_pairs={{0,16},{8,24},{16,0},{24,8},{1,17},{9,25},{17,1},{25,9},{2,18},{10... | collective-permute-start | bytes 884744 | tf_op jit(solution)/shard_map/ppermute | solution.py:31
  108.9 9.1 %collective-permute-start.34 = (bf16[2,4,24,640]{3,2,1,0:T(8,128)(2,1)S(1)}, bf16[2,4,24,640]{3,2,1,0:T(8,128)(2,1)S(1)}, u32[]{:S(2)}, u32[]{:S(2)}) collective-permute-start(bf16[2,4,24,640]{3,2,1,0:T(8,128)(2,1)S(1)} %get-tuple-element.332), channel_id=1, source_target_pairs={{0,2},{1,3},{2,0},{3,1},{4,6},{5,7},{6,4},{7,5},{8,10},{9,11},{10,... | collective-permute-start | bytes 737288 | tf_op jit(solution)/shard_map/ppermute | solution.py:31
  109.9 19.6 %collective-permute-start.36 = (bf16[256,576]{1,0:T(8,128)(2,1)S(1)}, bf16[256,576]{1,0:T(8,128)(2,1)S(1)}, u32[]{:S(2)}, u32[]{:S(2)}) collective-permute-start(bf16[256,576]{1,0:T(8,128)(2,1)S(1)} %get-tuple-element.285.refs_15_), channel_id=1, source_target_pairs={{0,8},{8,0},{16,24},{24,16},{1,9},{9,1},{17,25},{25,17},{2,10},{10... | collective-permute-start | bytes 884744 | tf_op jit(solution)/shard_map/ppermute | solution.py:31
  112.1 19.0 %collective-permute-start.37 = (bf16[256,576]{1,0:T(8,128)(2,1)S(1)}, bf16[256,576]{1,0:T(8,128)(2,1)S(1)}, u32[]{:S(2)}, u32[]{:S(2)}) collective-permute-start(bf16[256,576]{1,0:T(8,128)(2,1)S(1)} %get-tuple-element.286.refs_16_), channel_id=1, source_target_pairs={{0,16},{8,24},{16,0},{24,8},{1,17},{9,25},{17,1},{25,9},{2,18},{10... | collective-permute-start | bytes 884744 | tf_op jit(solution)/shard_map/ppermute | solution.py:31
  115.1 16.4 %collective-permute-start.38 = (bf16[256,576]{1,0:T(8,128)(2,1)S(1)}, bf16[256,576]{1,0:T(8,128)(2,1)S(1)}, u32[]{:S(2)}, u32[]{:S(2)}) collective-permute-start(bf16[256,576]{1,0:T(8,128)(2,1)S(1)} %get-tuple-element.287.refs_17_), channel_id=1, source_target_pairs={{0,24},{8,16},{16,8},{24,0},{1,25},{9,17},{17,9},{25,1},{2,26},{10... | collective-permute-start | bytes 884744 | tf_op jit(solution)/shard_map/ppermute | solution.py:31
  117.2 10.2 %collective-permute-start.42 = (bf16[2,96,768]{2,1,0:T(8,128)(2,1)S(1)}, bf16[2,96,768]{2,1,0:T(8,128)(2,1)S(1)}, u32[]{:S(2)}, u32[]{:S(2)}) collective-permute-start(bf16[2,96,768]{2,1,0:T(8,128)(2,1)S(1)} %get-tuple-element.275), channel_id=1, source_target_pairs={{0,2},{1,3},{2,0},{3,1},{4,6},{5,7},{6,4},{7,5},{8,10},{9,11},{10,... | collective-permute-start | bytes 884744 | tf_op jit(solution)/shard_map/ppermute | solution.py:31
  118.1 13.4 %copy-start.5 = (bf16[768,768]{1,0:T(8,128)(2,1)S(1)}, bf16[768,768]{1,0:T(8,128)(2,1)}, u32[]{:S(2)}) copy-start(bf16[768,768]{1,0:T(8,128)(2,1)} %refs_1_.5) | copy-start | bytes 3538948
  118.3 9.2 %collective-permute-start.35 = (bf16[1,4,24,640]{3,2,1,0:T(8,128)(2,1)S(1)}, bf16[1,4,24,640]{3,2,1,0:T(8,128)(2,1)S(1)}, u32[]{:S(2)}, u32[]{:S(2)}) collective-permute-start(bf16[1,4,24,640]{3,2,1,0:T(8,128)(2,1)S(1)} %pad_maximum_fusion.2), channel_id=1, source_target_pairs={{0,4},{1,5},{2,6},{3,7},{4,0},{5,1},{6,2},{7,3},{8,12},{9,13},{10,... | collective-permute-start | bytes 368648 | tf_op jit(solution)/shard_map/ppermute | solution.py:31
  127.5 8.6 %collective-permute-start.43 = (bf16[1,96,768]{2,1,0:T(8,128)(2,1)S(1)}, bf16[1,96,768]{2,1,0:T(8,128)(2,1)S(1)}, u32[]{:S(2)}, u32[]{:S(2)}) collective-permute-start(bf16[1,96,768]{2,1,0:T(8,128)(2,1)S(1)} %get-tuple-element.328), channel_id=1, source_target_pairs={{0,4},{1,5},{2,6},{3,7},{4,0},{5,1},{6,2},{7,3},{8,12},{9,13},{10,... | collective-permute-start | bytes 442376 | tf_op jit(solution)/shard_map/ppermute | solution.py:31
  127.9 7.1 %collective-permute-start.41 = (bf16[24,640]{1,0:T(8,128)(2,1)S(1)}, bf16[24,640]{1,0:T(8,128)(2,1)S(1)}, u32[]{:S(2)}, u32[]{:S(2)}) collective-permute-start(bf16[24,640]{1,0:T(8,128)(2,1)S(1)} %get-tuple-element.336), channel_id=1, source_target_pairs={{0,24},{8,16},{16,8},{24,0},{1,25},{9,17},{17,9},{25,1},{2,26},{10... | collective-permute-start | bytes 92168 | tf_op jit(solution)/shard_map/ppermute | solution.py:31
  129.5 5.5 %collective-permute-start.40 = (bf16[24,640]{1,0:T(8,128)(2,1)S(1)}, bf16[24,640]{1,0:T(8,128)(2,1)S(1)}, u32[]{:S(2)}, u32[]{:S(2)}) collective-permute-start(bf16[24,640]{1,0:T(8,128)(2,1)S(1)} %get-tuple-element.337), channel_id=1, source_target_pairs={{0,16},{8,24},{16,0},{24,8},{1,17},{9,25},{17,1},{25,9},{2,18},{10... | collective-permute-start | bytes 92168 | tf_op jit(solution)/shard_map/ppermute | solution.py:31
  131.1 3.9 %collective-permute-start.39 = (bf16[24,640]{1,0:T(8,128)(2,1)S(1)}, bf16[24,640]{1,0:T(8,128)(2,1)S(1)}, u32[]{:S(2)}, u32[]{:S(2)}) collective-permute-start(bf16[24,640]{1,0:T(8,128)(2,1)S(1)} %get-tuple-element.338), channel_id=1, source_target_pairs={{0,8},{8,0},{16,24},{24,16},{1,9},{9,1},{17,25},{25,17},{2,10},{10... | collective-permute-start | bytes 92168 | tf_op jit(solution)/shard_map/ppermute | solution.py:31
  (6 other events, 15.4 us)

commit v2 on v1

--- a/solution.py
+++ b/solution.py
@@ -124,12 +124,19 @@
         c.start()
     seg = seg_here()
     rows = w_ref.shape[0] // 8
+    width = w_ref.shape[1] // 3
     for c in weights:
         c.wait()
 
     def some_rows(i):
         these = pl.ds(pl.multiple_of(i * rows, rows), rows)
-        w_ref[these] = jnp.concatenate([own_columns(near_ref[k, these], seg, n_seg) for k in range(3)], axis=1)
+        for b in range(n_seg):
+
+            @pl.when(seg == b)
+            def _():
+                cols = slice(b * width, (b + 1) * width)
+                w_ref[these] = jnp.concatenate([near_ref[k, these, cols] for k in range(3)], axis=1)
+
 
     in_loop(8, 1, some_rows)
     for c in copies:

time: 137 us -> 136 us (level)
  starting transfers between devices: 44.3 us -> 47 us
  waiting for transfers between devices: 32.2 us -> 30.2 us
  Pallas kernels: 53.9 us -> 52.5 us
    ppermute x44, starting transfers between devices: 44.3 us -> 47 us  [swap(): lax.ppermute(block, axis, [(i, i ^ mask) for i in range(lax.axis_size(axi...]
    ppermute x44, waiting for transfers between devices: 32.2 us -> 30.2 us  [swap(): lax.ppermute(block, axis, [(i, i ^ mask) for i in range(lax.axis_size(axi...]
    pallas_call x21, Pallas kernels: 53.9 us -> 52.5 us  [call(): pl.pallas_call(body, out_shape=[o if i in far_out else pltpu.VMEM(o.shape...]
  transfers between devices with their start and end apart: 44 -> 44, of which waited for: 21 -> 22; matrix products, arithmetic and copies ran while one was open for 2% -> 2% of each run, Pallas kernels for 30% -> 29%
where the time goes in v2:
time: 136 us
  Pallas kernels  52.5 us (39%)
  starting transfers between devices  47 us (35%)
  waiting for transfers between devices  30.2 us (22%)
  local copies, waits for them, and re-layouts  2.74 us (2%)
  other arithmetic  2.59 us (2%)
    pallas_call x21, Pallas kernels, call(): pl.pallas_call(body, out_shape=[o if i in far_out else pltpu.VMEM(o.shape...  52.5 us
    ppermute x44, starting transfers between devices, swap(): lax.ppermute(block, axis, [(i, i ^ mask) for i in range(lax.axis_size(axi...  47 us
    ppermute x44, waiting for transfers between devices, swap(): lax.ppermute(block, axis, [(i, i ^ mask) for i in range(lax.axis_size(axi...  30.2 us
  transfers between devices with their start and end apart: 44, of which 22 were waited for; matrix products, arithmetic and copies ran while one was open for 2% of the time, Pallas kernels for 29%

profile of v2, /device:TPU:0, one launch (start us, length us, event | category | flops | bytes accessed | tf_op | source)
XLA Modules:
  0.0 136.1 jit_solution(805553288222789800)
XLA Ops:
  0.7 1.1 slice_bitcast_fusion
  1.8 4.0 %collective-permute-start.2 = (bf16[128,768]{1,0:T(8,128)(2,1)S(1)}, bf16[128,768]{1,0:T(8,128)(2,1)S(1)}, u32[]{:S(2)}, u32[]{:S(2)}) collective-permute-start(bf16[128,768]{1,0:T(8,128)(2,1)S(1)} %get-tuple-element.334.refs_2_.refs_4_.refs_6_), channel_id=1, source_target_pairs={{0,24},{8,16},{16,8},{24,0},{1,25},{9,17},{17,9},{25,1},{2,26},{10... | collective-permute-start | bytes 589832 | tf_op jit(solution)/shard_map/ppermute | solution.py:31
  8.3 3.1 %shard_map.331 = (bf16[768,576]{1,0:T(8,128)(2,1)S(1)}, f32[1,576]{1,0:T(1,128)S(1)}, f32[16,768]{1,0:T(8,128)S(1)}) custom-call(bf16[768,768]{1,0:T(8,128)(2,1)} %refs_1_.5, bf16[768,768]{1,0:T(8,128)(2,1)} %refs_2_.7, bf16[768,768]{1,0:T(8,128)(2,1)} %refs_3_.3, f32[768]{0:T(1024)} %refs_3_.2, f32[768]{0:T(1024)} %refs_4_.1, f32[768]{0:T(1024)} %refs_5_.3, ...), custom_call_target="tpu_custom_call" | custom-call | bytes 12000000 | tf_op jit(solution)/shard_map/pallas_call | solution.py:75
  11.5 3.0 %collective-permute-start.5 = (bf16[128,768]{1,0:T(8,128)(2,1)S(1)}, bf16[128,768]{1,0:T(8,128)(2,1)S(1)}, u32[]{:S(2)}, u32[]{:S(2)}) collective-permute-start(bf16[128,768]{1,0:T(8,128)(2,1)S(1)} %get-tuple-element.170.refs_2_.refs_4_.refs_10_), channel_id=1, source_target_pairs={{0,24},{8,16},{16,8},{24,0},{1,25},{9,17},{17,9},{25,1},{2,26},{10... | collective-permute-start | bytes 589832 | tf_op jit(solution)/shard_map/ppermute | solution.py:31
  16.6 3.8 %shard_map.334 = (bf16[72,384]{1,0:T(8,128)(2,1)S(1)}, bf16[72,384]{1,0:T(8,128)(2,1)S(1)}, bf16[72,384]{1,0:T(8,128)(2,1)S(1)}, bf16[72,384]{1,0:T(8,128)(2,1)S...) custom-call(s32[8,128]{1,0:T(8,128)S(1)} %shard_map.332.refs_0_, bf16[512,576]{1,0:T(8,128)(2,1)S(1)} %shard_map.333.refs_1_, ...), custom_call_target="tpu_custom_call" | custom-call | bytes 24000000 | tf_op jit(solution)/shard_map/pallas_call | solution.py:75
  20.5 1.4 %collective-permute-start.6 = (bf16[72,384]{1,0:T(8,128)(2,1)S(1)}, bf16[72,384]{1,0:T(8,128)(2,1)S(1)}, u32[]{:S(2)}, u32[]{:S(2)}) collective-permute-start(bf16[72,384]{1,0:T(8,128)(2,1)S(1)} %get-tuple-element.176), channel_id=1, source_target_pairs={{0,8},{8,0},{16,24},{24,16},{1,9},{9,1},{17,25},{25,17},{2,10},{10... | collective-permute-start | bytes 165896 | tf_op jit(solution)/shard_map/ppermute | solution.py:31
  21.9 1.2 collective-permute-start.7
  25.0 1.4 %collective-permute-done.7.refs_2_ = bf16[72,384]{1,0:T(8,128)(2,1)S(1)} collective-permute-done((bf16[72,384]{1,0:T(8,128)(2,1)S(1)}, bf16[72,384]{1,0:T(8,128)(2,1)S(1)}, u32[]{:S(2)}, u32[]{:S(2)}) %collective-permute-start.7) | collective-permute-done | bytes 55328 | tf_op jit(solution)/shard_map/ppermute | solution.py:31
  26.4 1.8 %collective-permute-done.8.refs_3_ = bf16[72,384]{1,0:T(8,128)(2,1)S(1)} collective-permute-done((bf16[72,384]{1,0:T(8,128)(2,1)S(1)}, bf16[72,384]{1,0:T(8,128)(2,1)S(1)}, u32[]{:S(2)}, u32[]{:S(2)}) %collective-permute-start.8) | collective-permute-done | bytes 55328 | tf_op jit(solution)/shard_map/ppermute | solution.py:31
  28.2 4.6 %shard_map.336 = (f32[144,768]{1,0:T(8,128)S(1)}, f32[144,128]{1,0:T(8,128)S(1)}, f32[144,3072]{1,0:T(8,128)S(1)}, f32[144,768]{1,0:T(8,128)S(1)}, bf16[128,768]...) custom-call(bf16[72,384]{1,0:T(8,128)(2,1)S(1)} %get-tuple-element.1, ...), custom_call_target="tpu_custom_call" | custom-call | bytes 24000000 | tf_op jit(solution)/shard_map/pallas_call | solution.py:75
  32.9 3.1 %shard_map.337 = (bf16[64,384]{1,0:T(8,128)(2,1)S(1)}, bf16[64,384]{1,0:T(8,128)(2,1)S(1)}, bf16[64,384]{1,0:T(8,128)(2,1)S(1)}, bf16[64,384]{1,0:T(8,128)(2,1)S...) custom-call(s32[8,128]{1,0:T(8,128)S(1)} %shard_map.332.refs_0_, ...), custom_call_target="tpu_custom_call" | custom-call | bytes 24000000 | tf_op jit(solution)/shard_map/pallas_call | solution.py:75
  36.0 0.9 collective-permute-start.10
  37.4 2.1 %collective-permute-start.12 = (bf16[64,384]{1,0:T(8,128)(2,1)S(1)}, bf16[64,384]{1,0:T(8,128)(2,1)S(1)}, u32[]{:S(2)}, u32[]{:S(2)}) collective-permute-start(bf16[64,384]{1,0:T(8,128)(2,1)S(1)} %get-tuple-element.188), channel_id=1, source_target_pairs={{0,24},{8,16},{16,8},{24,0},{1,25},{9,17},{17,9},{25,1},{2,26},{10... | collective-permute-start | bytes 147464 | tf_op jit(solution)/shard_map/ppermute | solution.py:31
  40.2 1.4 %collective-permute-done.11.refs_2_ = bf16[64,384]{1,0:T(8,128)(2,1)S(1)} collective-permute-done((bf16[64,384]{1,0:T(8,128)(2,1)S(1)}, bf16[64,384]{1,0:T(8,128)(2,1)S(1)}, u32[]{:S(2)}, u32[]{:S(2)}) %collective-permute-start.11) | collective-permute-done | bytes 49184 | tf_op jit(solution)/shard_map/ppermute | solution.py:31
  42.4 3.0 %shard_map.338 = (f32[128,768]{1,0:T(8,128)S(1)}, f32[128,128]{1,0:T(8,128)S(1)}, f32[128,3072]{1,0:T(8,128)S(1)}, f32[128,768]{1,0:T(8,128)S(1)}, bf16[128,768]...) custom-call(bf16[64,384]{1,0:T(8,128)(2,1)S(1)} %get-tuple-element.185.refs_0_, ...), custom_call_target="tpu_custom_call" | custom-call | bytes 24000000 | tf_op jit(solution)/shard_map/pallas_call | solution.py:75
  45.5 4.1 %shard_map.339 = (bf16[256,4608]{1,0:T(8,128)(2,1)S(1)}, f32[256,768]{1,0:T(8,128)S(1)}, f32[16,768]{1,0:T(8,128)S(1)}, bf16[128,384]{1,0:T(8,128)(2,1)S(1)}, bf...) custom-call(bf16[2,128,768]{2,1,0:T(8,128)(2,1)S(1)} %copy-done.6, ...), custom_call_target="tpu_custom_call" | custom-call | bytes 30000000 | tf_op jit(solution)/shard_map/pallas_call | solution.py:75
  50.1 1.4 %collective-permute-start.15 = (bf16[128,384]{1,0:T(8,128)(2,1)S(1)}, bf16[128,384]{1,0:T(8,128)(2,1)S(1)}, u32[]{:S(2)}, u32[]{:S(2)}) collective-permute-start(bf16[128,384]{1,0:T(8,128)(2,1)S(1)} %get-tuple-element.209), channel_id=1, source_target_pairs={{0,8},{8,0},{16,24},{24,16},{1,9},{9,1},{17,25},{25,17},{2,10},{10... | collective-permute-start | bytes 294920 | tf_op jit(solution)/shard_map/ppermute | solution.py:31
  51.6 1.2 collective-permute-start.16
  53.6 1.4 %collective-permute-done.13.refs_3_ = bf16[4,4,144,128]{3,2,1,0:T(8,128)(2,1)S(1)} collective-permute-done((bf16[4,4,144,128]{3,2,1,0:T(8,128)(2,1)S(1)}, bf16[4,4,144,128]{3,2,1,0:T(8,128)(2,1)S(1)}, u32[]{:S(2)}, u32[]{:S(2)}) %collective-permute-start.13) | collective-permute-done | bytes 589856 | tf_op jit(solution)/shard_map/ppermute | solution.py:31
  55.0 1.7 %shard_map.340 = (bf16[2,2,120,768]{3,2,1,0:T(8,128)(2,1)S(1)}, bf16[2,2,120,768]{3,2,1,0:T(8,128)(2,1)S(1)}, bf16[2,2,120,768]{3,2,1,0:T(8,128)(2,1)S(1)}, bf16[2,2,120,768]{3,2,1,0:T(8,128)(2,1)S(1)}) custom-call(bf16[4,4,144,128]{3,2,1,0:T(8,128)(2,1)S(1)} %get-tuple-element.180.refs_0_, bf16[4,4,144,128]{3,2,1,0:T(8,128)(2,1)S(1)} %get-tuple-element.189.refs_1_, ...), custom_call_target="tpu_custom_call" | custom-call | bytes 6000000 | tf_op jit(solution)/shard_map/pallas_call | solution.py:75
  57.2 1.1 collective-permute-done.17.refs_7_
  59.2 1.2 collective-permute-start.19
  60.4 5.0 %shard_map.341 = (bf16[128,576]{1,0:T(8,128)(2,1)S(1)}, bf16[128,576]{1,0:T(8,128)(2,1)S(1)}, bf16[128,576]{1,0:T(8,128)(2,1)S(1)}, bf16[128,576]{1,0:T(8,128)(2,1)S(1)}, bf16[16,576]{1,0:T(8,128)(2,1)S(1)}) custom-call(s32[8,128]{1,0:T(8,128)S(1)} %shard_map.332.refs_0_, bf16[512,576]{1,0:T(8,128)(2,1)S(1)} %shard_map.335.refs_1_, ...), custom_call_target="tpu_custom_call" | custom-call | bytes 24000000 | tf_op jit(solution)/shard_map/pallas_call | solution.py:75
  65.4 1.4 %collective-permute-start.22 = (bf16[16,384]{1,0:T(8,128)(2,1)S(1)}, bf16[16,384]{1,0:T(8,128)(2,1)S(1)}, u32[]{:S(2)}, u32[]{:S(2)}) collective-permute-start(bf16[16,384]{1,0:T(8,128)(2,1)S(1)} %slice.159.refs_1_), channel_id=1, source_target_pairs={{0,24},{8,16},{16,8},{24,0},{1,25},{9,17},{17,9},{25,1},{2,26},{10... | collective-permute-start | bytes 36872 | tf_op jit(solution)/shard_map/ppermute | solution.py:31
  66.9 1.2 collective-permute-start.21
  68.9 1.4 %shard_map.342 = (bf16[2,2,96,768]{3,2,1,0:T(8,128)(2,1)S(1)}, bf16[2,2,96,768]{3,2,1,0:T(8,128)(2,1)S(1)}, bf16[2,2,96,768]{3,2,1,0:T(8,128)(2,1)S(1)}, bf16[2,2,96,768]{3,2,1,0:T(8,128)(2,1)S(1)}) custom-call(bf16[4,4,144,128]{3,2,1,0:T(8,128)(2,1)S(1)} %get-tuple-element.180.refs_0_, bf16[4,4,144,128]{3,2,1,0:T(8,128)(2,1)S(1)} %get-tuple-element.189.refs_1_, ...), custom_call_target="tpu_custom_call" | custom-call | bytes 6000000 | tf_op jit(solution)/shard_map/pallas_call | solution.py:75
  70.3 6.5 %collective-permute-done.22.refs_4_ = bf16[16,384]{1,0:T(8,128)(2,1)S(1)} collective-permute-done((bf16[16,384]{1,0:T(8,128)(2,1)S(1)}, bf16[16,384]{1,0:T(8,128)(2,1)S(1)}, u32[]{:S(2)}, u32[]{:S(2)}) %collective-permute-start.22) | collective-permute-done | bytes 12320 | tf_op jit(solution)/shard_map/ppermute | solution.py:31
  77.4 1.3 collective-permute-start.23
  79.6 4.8 %shard_map.343 = (bf16[16,4608]{1,0:T(8,128)(2,1)S(1)}, f32[16,768]{1,0:T(8,128)S(1)}, f32[16,768]{1,0:T(8,128)S(1)}, f32[16,768]{1,0:T(8,128)S(1)}, bf16[16,192]{1,0:T(8,128)(2,1)S(1)}) custom-call(s32[8,128]{1,0:T(8,128)S(1)} %shard_map.332.refs_0_, bf16[16,384]{1,0:T(8,128)(2,1)S(1)} %slice.159.refs_1_, ...), custom_call_target="tpu_custom_call" | custom-call | bytes 18000000 | tf_op jit(solution)/shard_map/pallas_call | solution.py:75
  85.9 1.1 collective-permute-done.24.refs_7_
  87.4 1.6 %collective-permute-start.29 = (bf16[2,120,768]{2,1,0:T(8,128)(2,1)S(1)}, bf16[2,120,768]{2,1,0:T(8,128)(2,1)S(1)}, u32[]{:S(2)}, u32[]{:S(2)}) collective-permute-start(bf16[2,120,768]{2,1,0:T(8,128)(2,1)S(1)} %get-tuple-element.261), channel_id=1, source_target_pairs={{0,2},{1,3},{2,0},{3,1},{4,6},{5,7},{6,4},{7,5},{8,10},{9,11},{10,... | collective-permute-start | bytes 1105928 | tf_op jit(solution)/shard_map/ppermute | solution.py:31
  89.7 0.9 collective-permute-start.26
  90.6 5.9 %shard_map.345 = (bf16[256,576]{1,0:T(8,128)(2,1)S(1)}, bf16[256,576]{1,0:T(8,128)(2,1)S(1)}, bf16[256,576]{1,0:T(8,128)(2,1)S(1)}, bf16[256,576]{1,0:T(8,128)(2,1)S(1)}, bf16[16,576]{1,0:T(8,128)(2,1)S(1)}) custom-call(s32[8,128]{1,0:T(8,128)S(1)} %shard_map.332.refs_0_, bf16[512,576]{1,0:T(8,128)(2,1)S(1)} %shard_map.333.refs_1_, ...), custom_call_target="tpu_custom_call" | custom-call | bytes 24000000 | tf_op jit(solution)/shard_map/pallas_call | solution.py:75
  97.5 2.7 %collective-permute-start.31 = (bf16[1,120,768]{2,1,0:T(8,128)(2,1)S(1)}, bf16[1,120,768]{2,1,0:T(8,128)(2,1)S(1)}, u32[]{:S(2)}, u32[]{:S(2)}) collective-permute-start(bf16[1,120,768]{2,1,0:T(8,128)(2,1)S(1)} %get-tuple-element.327), channel_id=1, source_target_pairs={{0,4},{1,5},{2,6},{3,7},{4,0},{5,1},{6,2},{7,3},{8,12},{9,13},{10,... | collective-permute-start | bytes 552968 | tf_op jit(solution)/shard_map/ppermute | solution.py:31
  100.2 2.9 %shard_map.346 = (bf16[4,4,24,640]{3,2,1,0:T(8,128)(2,1)S(1)}, bf16[4,4,24,640]{3,2,1,0:T(8,128)(2,1)S(1)}) custom-call(s32[8,128]{1,0:T(8,128)S(1)} %shard_map.332.refs_0_, f32[16,768]{1,0:T(8,128)S(1)} %get-tuple-element.238.refs_1_, f32[16,768]{1,0:T(8,128)S(1)} %get-tuple-element.239.refs_2_, f32[16,768]{1,0:T(8,128)S(1)} %get-tuple-element.240.refs_3_, ...), custom_call_target="tpu_custom_call" | custom-call | bytes 18000000 | tf_op jit(solution)/shard_map/pallas_call | solution.py:75
  104.5 0.9 collective-permute-start.33
  106.4 1.1 collective-permute-done.31
  109.6 1.7 %collective-permute-start.36 = (bf16[256,576]{1,0:T(8,128)(2,1)S(1)}, bf16[256,576]{1,0:T(8,128)(2,1)S(1)}, u32[]{:S(2)}, u32[]{:S(2)}) collective-permute-start(bf16[256,576]{1,0:T(8,128)(2,1)S(1)} %get-tuple-element.285.refs_15_), channel_id=1, source_target_pairs={{0,8},{8,0},{16,24},{24,16},{1,9},{9,1},{17,25},{25,17},{2,10},{10... | collective-permute-start | bytes 884744 | tf_op jit(solution)/shard_map/ppermute | solution.py:31
  112.6 1.2 collective-permute-done.33.refs_7_
  113.8 1.0 collective-permute-start.38
  115.2 1.5 %collective-permute-start.42 = (bf16[2,96,768]{2,1,0:T(8,128)(2,1)S(1)}, bf16[2,96,768]{2,1,0:T(8,128)(2,1)S(1)}, u32[]{:S(2)}, u32[]{:S(2)}) collective-permute-start(bf16[2,96,768]{2,1,0:T(8,128)(2,1)S(1)} %get-tuple-element.275), channel_id=1, source_target_pairs={{0,2},{1,3},{2,0},{3,1},{4,6},{5,7},{6,4},{7,5},{8,10},{9,11},{10,... | collective-permute-start | bytes 884744 | tf_op jit(solution)/shard_map/ppermute | solution.py:31
  117.0 1.2 collective-permute-start.35
  118.3 7.1 %collective-permute-done.42 = bf16[2,96,768]{2,1,0:T(8,128)(2,1)S(1)} collective-permute-done((bf16[2,96,768]{2,1,0:T(8,128)(2,1)S(1)}, bf16[2,96,768]{2,1,0:T(8,128)(2,1)S(1)}, u32[]{:S(2)}, u32[]{:S(2)}) %collective-permute-start.42) | collective-permute-done | bytes 294944 | tf_op jit(solution)/shard_map/ppermute | solution.py:31
  125.6 1.3 collective-permute-start.43
  127.2 1.8 %collective-permute-start.41 = (bf16[24,640]{1,0:T(8,128)(2,1)S(1)}, bf16[24,640]{1,0:T(8,128)(2,1)S(1)}, u32[]{:S(2)}, u32[]{:S(2)}) collective-permute-start(bf16[24,640]{1,0:T(8,128)(2,1)S(1)} %get-tuple-element.336), channel_id=1, source_target_pairs={{0,24},{8,16},{16,8},{24,0},{1,25},{9,17},{17,9},{25,1},{2,26},{10... | collective-permute-start | bytes 92168 | tf_op jit(solution)/shard_map/ppermute | solution.py:31
  129.0 1.5 %collective-permute-start.40 = (bf16[24,640]{1,0:T(8,128)(2,1)S(1)}, bf16[24,640]{1,0:T(8,128)(2,1)S(1)}, u32[]{:S(2)}, u32[]{:S(2)}) collective-permute-start(bf16[24,640]{1,0:T(8,128)(2,1)S(1)} %get-tuple-element.337), channel_id=1, source_target_pairs={{0,16},{8,24},{16,0},{24,8},{1,17},{9,25},{17,1},{25,9},{2,18},{10... | collective-permute-start | bytes 92168 | tf_op jit(solution)/shard_map/ppermute | solution.py:31
  130.8 3.5 %shard_map.349 = bf16[2,128,768]{2,1,0:T(8,128)(2,1)} custom-call(f32[256,768]{1,0:T(8,128)S(1)} %get-tuple-element.283.refs_0_, bf16[768,768]{1,0:T(8,128)(2,1)S(1)} %copy-done.5, bf16[768,768]{1,0:T(8,128)(2,1)S(1)} %copy-done.3, bf16[768,768]{1,0:T(8,128)(2,1)S(1)} %copy-done.4, bf16[256,576]{1,0:T(8,128)(2,1)S(1)} %get-tuple-element.284.refs_14_.refs_4_, ...), custom_call_target="tpu_custom_call" | custom-call | bytes 9000000 | tf_op jit(solution)/shard_map/pallas_call | solution.py:75
  134.4 1.0 shard_map.350
  (105 shorter events, 25.2 us)
Async XLA Ops:
  0.7 27.6 %copy-start.2 = (bf16[768,768]{1,0:T(8,128)(2,1)S(1)}, bf16[768,768]{1,0:T(8,128)(2,1)}, u32[]{:S(2)}) copy-start(bf16[768,768]{1,0:T(8,128)(2,1)} %refs_12_.3) | copy-start | bytes 3538948
  1.8 13.1 %collective-permute-start.2 = (bf16[128,768]{1,0:T(8,128)(2,1)S(1)}, bf16[128,768]{1,0:T(8,128)(2,1)S(1)}, u32[]{:S(2)}, u32[]{:S(2)}) collective-permute-start(bf16[128,768]{1,0:T(8,128)(2,1)S(1)} %get-tuple-element.334.refs_2_.refs_4_.refs_6_), channel_id=1, source_target_pairs={{0,24},{8,16},{16,8},{24,0},{1,25},{9,17},{17,9},{25,1},{2,26},{10... | collective-permute-start | bytes 589832 | tf_op jit(solution)/shard_map/ppermute | solution.py:31
  5.8 9.6 %collective-permute-start.1 = (bf16[128,768]{1,0:T(8,128)(2,1)S(1)}, bf16[128,768]{1,0:T(8,128)(2,1)S(1)}, u32[]{:S(2)}, u32[]{:S(2)}) collective-permute-start(bf16[128,768]{1,0:T(8,128)(2,1)S(1)} %get-tuple-element.334.refs_2_.refs_4_.refs_6_), channel_id=1, source_target_pairs={{0,16},{8,24},{16,0},{24,8},{1,17},{9,25},{17,1},{25,9},{2,18},{10... | collective-permute-start | bytes 589832 | tf_op jit(solution)/shard_map/ppermute | solution.py:31
  6.3 9.6 %collective-permute-start = (bf16[128,768]{1,0:T(8,128)(2,1)S(1)}, bf16[128,768]{1,0:T(8,128)(2,1)S(1)}, u32[]{:S(2)}, u32[]{:S(2)}) collective-permute-start(bf16[128,768]{1,0:T(8,128)(2,1)S(1)} %get-tuple-element.334.refs_2_.refs_4_.refs_6_), channel_id=1, source_target_pairs={{0,8},{8,0},{16,24},{24,16},{1,9},{9,1},{17,25},{25,17},{2,10},{10... | collective-permute-start | bytes 589832 | tf_op jit(solution)/shard_map/ppermute | solution.py:31
  8.3 19.9 %copy-start.1 = (bf16[3072,768]{1,0:T(8,128)(2,1)S(1)}, bf16[3072,768]{1,0:T(8,128)(2,1)}, u32[]{:S(2)}) copy-start(bf16[3072,768]{1,0:T(8,128)(2,1)} %refs_14_.1) | copy-start | bytes 14155780
  11.5 11.7 %collective-permute-start.5 = (bf16[128,768]{1,0:T(8,128)(2,1)S(1)}, bf16[128,768]{1,0:T(8,128)(2,1)S(1)}, u32[]{:S(2)}, u32[]{:S(2)}) collective-permute-start(bf16[128,768]{1,0:T(8,128)(2,1)S(1)} %get-tuple-element.170.refs_2_.refs_4_.refs_10_), channel_id=1, source_target_pairs={{0,24},{8,16},{16,8},{24,0},{1,25},{9,17},{17,9},{25,1},{2,26},{10... | collective-permute-start | bytes 589832 | tf_op jit(solution)/shard_map/ppermute | solution.py:31
  14.4 9.6 %collective-permute-start.4 = (bf16[128,768]{1,0:T(8,128)(2,1)S(1)}, bf16[128,768]{1,0:T(8,128)(2,1)S(1)}, u32[]{:S(2)}, u32[]{:S(2)}) collective-permute-start(bf16[128,768]{1,0:T(8,128)(2,1)S(1)} %get-tuple-element.170.refs_2_.refs_4_.refs_10_), channel_id=1, source_target_pairs={{0,16},{8,24},{16,0},{24,8},{1,17},{9,25},{17,1},{25,9},{2,18},{10... | collective-permute-start | bytes 589832 | tf_op jit(solution)/shard_map/ppermute | solution.py:31
  14.9 9.3 %collective-permute-start.3 = (bf16[128,768]{1,0:T(8,128)(2,1)S(1)}, bf16[128,768]{1,0:T(8,128)(2,1)S(1)}, u32[]{:S(2)}, u32[]{:S(2)}) collective-permute-start(bf16[128,768]{1,0:T(8,128)(2,1)S(1)} %get-tuple-element.170.refs_2_.refs_4_.refs_10_), channel_id=1, source_target_pairs={{0,8},{8,0},{16,24},{24,16},{1,9},{9,1},{17,25},{25,17},{2,10},{10... | collective-permute-start | bytes 589832 | tf_op jit(solution)/shard_map/ppermute | solution.py:31
  15.8 12.4 %copy-start = (bf16[768,3072]{1,0:T(8,128)(2,1)S(1)}, bf16[768,3072]{1,0:T(8,128)(2,1)}, u32[]{:S(2)}) copy-start(bf16[768,3072]{1,0:T(8,128)(2,1)} %refs_13_.1) | copy-start | bytes 14155780
  20.5 4.6 %collective-permute-start.6 = (bf16[72,384]{1,0:T(8,128)(2,1)S(1)}, bf16[72,384]{1,0:T(8,128)(2,1)S(1)}, u32[]{:S(2)}, u32[]{:S(2)}) collective-permute-start(bf16[72,384]{1,0:T(8,128)(2,1)S(1)} %get-tuple-element.176), channel_id=1, source_target_pairs={{0,8},{8,0},{16,24},{24,16},{1,9},{9,1},{17,25},{25,17},{2,10},{10... | collective-permute-start | bytes 165896 | tf_op jit(solution)/shard_map/ppermute | solution.py:31
  21.9 4.5 %collective-permute-start.7 = (bf16[72,384]{1,0:T(8,128)(2,1)S(1)}, bf16[72,384]{1,0:T(8,128)(2,1)S(1)}, u32[]{:S(2)}, u32[]{:S(2)}) collective-permute-start(bf16[72,384]{1,0:T(8,128)(2,1)S(1)} %get-tuple-element.177), channel_id=1, source_target_pairs={{0,16},{8,24},{16,0},{24,8},{1,17},{9,25},{17,1},{25,9},{2,18},{10... | collective-permute-start | bytes 165896 | tf_op jit(solution)/shard_map/ppermute | solution.py:31
  23.2 5.1 %collective-permute-start.8 = (bf16[72,384]{1,0:T(8,128)(2,1)S(1)}, bf16[72,384]{1,0:T(8,128)(2,1)S(1)}, u32[]{:S(2)}, u32[]{:S(2)}) collective-permute-start(bf16[72,384]{1,0:T(8,128)(2,1)S(1)} %get-tuple-element.178), channel_id=1, source_target_pairs={{0,24},{8,16},{16,8},{24,0},{1,25},{9,17},{17,9},{25,1},{2,26},{10... | collective-permute-start | bytes 165896 | tf_op jit(solution)/shard_map/ppermute | solution.py:31
  32.8 6.7 %collective-permute-start.9 = (bf16[4,4,144,128]{3,2,1,0:T(8,128)(2,1)S(1)}, bf16[4,4,144,128]{3,2,1,0:T(8,128)(2,1)S(1)}, u32[]{:S(2)}, u32[]{:S(2)}) collective-permute-start(bf16[4,4,144,128]{3,2,1,0:T(8,128)(2,1)S(1)} %get-tuple-element.184), channel_id=1, source_target_pairs={{0,1},{1,0},{2,3},{3,2},{4,5},{5,4},{6,7},{7,6},{8,9},{9,8},{10,11... | collective-permute-start | bytes 1769480 | tf_op jit(solution)/shard_map/ppermute | solution.py:31
  36.0 4.2 %collective-permute-start.10 = (bf16[64,384]{1,0:T(8,128)(2,1)S(1)}, bf16[64,384]{1,0:T(8,128)(2,1)S(1)}, u32[]{:S(2)}, u32[]{:S(2)}) collective-permute-start(bf16[64,384]{1,0:T(8,128)(2,1)S(1)} %get-tuple-element.186), channel_id=1, source_target_pairs={{0,8},{8,0},{16,24},{24,16},{1,9},{9,1},{17,25},{25,17},{2,10},{10... | collective-permute-start | bytes 147464 | tf_op jit(solution)/shard_map/ppermute | solution.py:31
  37.0 4.6 %collective-permute-start.11 = (bf16[64,384]{1,0:T(8,128)(2,1)S(1)}, bf16[64,384]{1,0:T(8,128)(2,1)S(1)}, u32[]{:S(2)}, u32[]{:S(2)}) collective-permute-start(bf16[64,384]{1,0:T(8,128)(2,1)S(1)} %get-tuple-element.187), channel_id=1, source_target_pairs={{0,16},{8,24},{16,0},{24,8},{1,17},{9,25},{17,1},{25,9},{2,18},{10... | collective-permute-start | bytes 147464 | tf_op jit(solution)/shard_map/ppermute | solution.py:31
  37.4 5.0 %collective-permute-start.12 = (bf16[64,384]{1,0:T(8,128)(2,1)S(1)}, bf16[64,384]{1,0:T(8,128)(2,1)S(1)}, u32[]{:S(2)}, u32[]{:S(2)}) collective-permute-start(bf16[64,384]{1,0:T(8,128)(2,1)S(1)} %get-tuple-element.188), channel_id=1, source_target_pairs={{0,24},{8,16},{16,8},{24,0},{1,25},{9,17},{17,9},{25,1},{2,26},{10... | collective-permute-start | bytes 147464 | tf_op jit(solution)/shard_map/ppermute | solution.py:31
  49.6 5.4 %collective-permute-start.14 = (bf16[256,4608]{1,0:T(8,128)(2,1)S(1)}, bf16[256,4608]{1,0:T(8,128)(2,1)S(1)}, u32[]{:S(2)}, u32[]{:S(2)}) collective-permute-start(bf16[256,4608]{1,0:T(8,128)(2,1)S(1)} %get-tuple-element.202.refs_4_), channel_id=1, source_target_pairs={{0,1},{1,0},{2,3},{3,2},{4,5},{5,4},{6,7},{7,6},{8,9},{9,8},{10,11... | collective-permute-start | bytes 7077896 | tf_op jit(solution)/shard_map/ppermute | solution.py:31
  49.6 5.4 %collective-permute-start.13 = (bf16[4,4,144,128]{3,2,1,0:T(8,128)(2,1)S(1)}, bf16[4,4,144,128]{3,2,1,0:T(8,128)(2,1)S(1)}, u32[]{:S(2)}, u32[]{:S(2)}) collective-permute-start(bf16[4,4,144,128]{3,2,1,0:T(8,128)(2,1)S(1)} %get-tuple-element.200), channel_id=1, source_target_pairs={{0,1},{1,0},{2,3},{3,2},{4,5},{5,4},{6,7},{7,6},{8,9},{9,8},{10,11... | collective-permute-start | bytes 1769480 | tf_op jit(solution)/shard_map/ppermute | solution.py:31
  50.1 6.6 %collective-permute-start.15 = (bf16[128,384]{1,0:T(8,128)(2,1)S(1)}, bf16[128,384]{1,0:T(8,128)(2,1)S(1)}, u32[]{:S(2)}, u32[]{:S(2)}) collective-permute-start(bf16[128,384]{1,0:T(8,128)(2,1)S(1)} %get-tuple-element.209), channel_id=1, source_target_pairs={{0,8},{8,0},{16,24},{24,16},{1,9},{9,1},{17,25},{25,17},{2,10},{10... | collective-permute-start | bytes 294920 | tf_op jit(solution)/shard_map/ppermute | solution.py:31
  51.6 5.7 %collective-permute-start.16 = (bf16[128,384]{1,0:T(8,128)(2,1)S(1)}, bf16[128,384]{1,0:T(8,128)(2,1)S(1)}, u32[]{:S(2)}, u32[]{:S(2)}) collective-permute-start(bf16[128,384]{1,0:T(8,128)(2,1)S(1)} %get-tuple-element.210), channel_id=1, source_target_pairs={{0,16},{8,24},{16,0},{24,8},{1,17},{9,25},{17,1},{25,9},{2,18},{10... | collective-permute-start | bytes 294920 | tf_op jit(solution)/shard_map/ppermute | solution.py:31
  52.8 5.5 %collective-permute-start.17 = (bf16[128,384]{1,0:T(8,128)(2,1)S(1)}, bf16[128,384]{1,0:T(8,128)(2,1)S(1)}, u32[]{:S(2)}, u32[]{:S(2)}) collective-permute-start(bf16[128,384]{1,0:T(8,128)(2,1)S(1)} %get-tuple-element.211), channel_id=1, source_target_pairs={{0,24},{8,16},{16,8},{24,0},{1,25},{9,17},{17,9},{25,1},{2,26},{10... | collective-permute-start | bytes 294920 | tf_op jit(solution)/shard_map/ppermute | solution.py:31
  58.3 18.7 %collective-permute-start.18 = (bf16[2,2,120,768]{3,2,1,0:T(8,128)(2,1)S(1)}, bf16[2,2,120,768]{3,2,1,0:T(8,128)(2,1)S(1)}, u32[]{:S(2)}, u32[]{:S(2)}) collective-permute-start(bf16[2,2,120,768]{3,2,1,0:T(8,128)(2,1)S(1)} %get-tuple-element.220), channel_id=1, source_target_pairs={{0,8},{8,0},{16,24},{24,16},{1,9},{9,1},{17,25},{25,17},{2,10},{10... | collective-permute-start | bytes 2211848 | tf_op jit(solution)/shard_map/ppermute | solution.py:31
  59.2 17.9 %collective-permute-start.19 = (bf16[2,2,120,768]{3,2,1,0:T(8,128)(2,1)S(1)}, bf16[2,2,120,768]{3,2,1,0:T(8,128)(2,1)S(1)}, u32[]{:S(2)}, u32[]{:S(2)}) collective-permute-start(bf16[2,2,120,768]{3,2,1,0:T(8,128)(2,1)S(1)} %get-tuple-element.221), channel_id=1, source_target_pairs={{0,16},{8,24},{16,0},{24,8},{1,17},{9,25},{17,1},{25,9},{2,18},{10... | collective-permute-start | bytes 2211848 | tf_op jit(solution)/shard_map/ppermute | solution.py:31
  65.4 11.4 %collective-permute-start.22 = (bf16[16,384]{1,0:T(8,128)(2,1)S(1)}, bf16[16,384]{1,0:T(8,128)(2,1)S(1)}, u32[]{:S(2)}, u32[]{:S(2)}) collective-permute-start(bf16[16,384]{1,0:T(8,128)(2,1)S(1)} %slice.159.refs_1_), channel_id=1, source_target_pairs={{0,24},{8,16},{16,8},{24,0},{1,25},{9,17},{17,9},{25,1},{2,26},{10... | collective-permute-start | bytes 36872 | tf_op jit(solution)/shard_map/ppermute | solution.py:31
  66.9 10.2 %collective-permute-start.21 = (bf16[16,384]{1,0:T(8,128)(2,1)S(1)}, bf16[16,384]{1,0:T(8,128)(2,1)S(1)}, u32[]{:S(2)}, u32[]{:S(2)}) collective-permute-start(bf16[16,384]{1,0:T(8,128)(2,1)S(1)} %slice.159.refs_1_), channel_id=1, source_target_pairs={{0,16},{8,24},{16,0},{24,8},{1,17},{9,25},{17,1},{25,9},{2,18},{10... | collective-permute-start | bytes 36872 | tf_op jit(solution)/shard_map/ppermute | solution.py:31
  68.1 9.0 %collective-permute-start.20 = (bf16[16,384]{1,0:T(8,128)(2,1)S(1)}, bf16[16,384]{1,0:T(8,128)(2,1)S(1)}, u32[]{:S(2)}, u32[]{:S(2)}) collective-permute-start(bf16[16,384]{1,0:T(8,128)(2,1)S(1)} %slice.159.refs_1_), channel_id=1, source_target_pairs={{0,8},{8,0},{16,24},{24,16},{1,9},{9,1},{17,25},{25,17},{2,10},{10... | collective-permute-start | bytes 36872 | tf_op jit(solution)/shard_map/ppermute | solution.py:31
  77.4 8.4 %collective-permute-start.23 = (bf16[2,120,768]{2,1,0:T(8,128)(2,1)S(1)}, bf16[2,120,768]{2,1,0:T(8,128)(2,1)S(1)}, u32[]{:S(2)}, u32[]{:S(2)}) collective-permute-start(bf16[2,120,768]{2,1,0:T(8,128)(2,1)S(1)} %get-tuple-element.232), channel_id=1, source_target_pairs={{0,16},{8,24},{16,0},{24,8},{1,17},{9,25},{17,1},{25,9},{2,18},{10... | collective-permute-start | bytes 1105928 | tf_op jit(solution)/shard_map/ppermute | solution.py:31
  78.8 8.2 %collective-permute-start.24 = (bf16[2,120,768]{2,1,0:T(8,128)(2,1)S(1)}, bf16[2,120,768]{2,1,0:T(8,128)(2,1)S(1)}, u32[]{:S(2)}, u32[]{:S(2)}) collective-permute-start(bf16[2,120,768]{2,1,0:T(8,128)(2,1)S(1)} %get-tuple-element.233), channel_id=1, source_target_pairs={{0,8},{8,0},{16,24},{24,16},{1,9},{9,1},{17,25},{25,17},{2,10},{10... | collective-permute-start | bytes 1105928 | tf_op jit(solution)/shard_map/ppermute | solution.py:31
  84.5 2.5 %collective-permute-start.28 = (bf16[16,4608]{1,0:T(8,128)(2,1)S(1)}, bf16[16,4608]{1,0:T(8,128)(2,1)S(1)}, u32[]{:S(2)}, u32[]{:S(2)}) collective-permute-start(bf16[16,4608]{1,0:T(8,128)(2,1)S(1)} %get-tuple-element.246.refs_2_), channel_id=1, source_target_pairs={{0,1},{1,0},{2,3},{3,2},{4,5},{5,4},{6,7},{7,6},{8,9},{9,8},{10,11... | collective-permute-start | bytes 442376 | tf_op jit(solution)/shard_map/ppermute | solution.py:31
  84.5 2.4 %collective-permute-start.27 = (bf16[4,144,16]{2,1,0:T(8,128)(2,1)S(1)}, bf16[4,144,16]{2,1,0:T(8,128)(2,1)S(1)}, u32[]{:S(2)}, u32[]{:S(2)}) collective-permute-start(bf16[4,144,16]{2,1,0:T(8,128)(2,1)S(1)} %get-tuple-element.245), channel_id=1, source_target_pairs={{0,1},{1,0},{2,3},{3,2},{4,5},{5,4},{6,7},{7,6},{8,9},{9,8},{10,11... | collective-permute-start | bytes 55304 | tf_op jit(solution)/shard_map/ppermute | solution.py:31
  87.4 10.0 %collective-permute-start.29 = (bf16[2,120,768]{2,1,0:T(8,128)(2,1)S(1)}, bf16[2,120,768]{2,1,0:T(8,128)(2,1)S(1)}, u32[]{:S(2)}, u32[]{:S(2)}) collective-permute-start(bf16[2,120,768]{2,1,0:T(8,128)(2,1)S(1)} %get-tuple-element.261), channel_id=1, source_target_pairs={{0,2},{1,3},{2,0},{3,1},{4,6},{5,7},{6,4},{7,5},{8,10},{9,11},{10,... | collective-permute-start | bytes 1105928 | tf_op jit(solution)/shard_map/ppermute | solution.py:31
  89.0 14.4 %collective-permute-start.25 = (bf16[2,2,96,768]{3,2,1,0:T(8,128)(2,1)S(1)}, bf16[2,2,96,768]{3,2,1,0:T(8,128)(2,1)S(1)}, u32[]{:S(2)}, u32[]{:S(2)}) collective-permute-start(bf16[2,2,96,768]{3,2,1,0:T(8,128)(2,1)S(1)} %get-tuple-element.236), channel_id=1, source_target_pairs={{0,8},{8,0},{16,24},{24,16},{1,9},{9,1},{17,25},{25,17},{2,10},{10... | collective-permute-start | bytes 1769480 | tf_op jit(solution)/shard_map/ppermute | solution.py:31
  89.7 14.6 %collective-permute-start.26 = (bf16[2,2,96,768]{3,2,1,0:T(8,128)(2,1)S(1)}, bf16[2,2,96,768]{3,2,1,0:T(8,128)(2,1)S(1)}, u32[]{:S(2)}, u32[]{:S(2)}) collective-permute-start(bf16[2,2,96,768]{3,2,1,0:T(8,128)(2,1)S(1)} %get-tuple-element.237), channel_id=1, source_target_pairs={{0,16},{8,24},{16,0},{24,8},{1,17},{9,25},{17,1},{25,9},{2,18},{10... | collective-permute-start | bytes 1769480 | tf_op jit(solution)/shard_map/ppermute | solution.py:31
  97.5 10.0 %collective-permute-start.31 = (bf16[1,120,768]{2,1,0:T(8,128)(2,1)S(1)}, bf16[1,120,768]{2,1,0:T(8,128)(2,1)S(1)}, u32[]{:S(2)}, u32[]{:S(2)}) collective-permute-start(bf16[1,120,768]{2,1,0:T(8,128)(2,1)S(1)} %get-tuple-element.327), channel_id=1, source_target_pairs={{0,4},{1,5},{2,6},{3,7},{4,0},{5,1},{6,2},{7,3},{8,12},{9,13},{10,... | collective-permute-start | bytes 552968 | tf_op jit(solution)/shard_map/ppermute | solution.py:31
  103.1 4.4 %collective-permute-start.30 = (bf16[4,4,24,640]{3,2,1,0:T(8,128)(2,1)S(1)}, bf16[4,4,24,640]{3,2,1,0:T(8,128)(2,1)S(1)}, u32[]{:S(2)}, u32[]{:S(2)}) collective-permute-start(bf16[4,4,24,640]{3,2,1,0:T(8,128)(2,1)S(1)} %get-tuple-element.268), channel_id=1, source_target_pairs={{0,1},{1,0},{2,3},{3,2},{4,5},{5,4},{6,7},{7,6},{8,9},{9,8},{10,11... | collective-permute-start | bytes 1474568 | tf_op jit(solution)/shard_map/ppermute | solution.py:31
  104.5 9.3 %collective-permute-start.33 = (bf16[2,96,768]{2,1,0:T(8,128)(2,1)S(1)}, bf16[2,96,768]{2,1,0:T(8,128)(2,1)S(1)}, u32[]{:S(2)}, u32[]{:S(2)}) collective-permute-start(bf16[2,96,768]{2,1,0:T(8,128)(2,1)S(1)} %get-tuple-element.322), channel_id=1, source_target_pairs={{0,8},{8,0},{16,24},{24,16},{1,9},{9,1},{17,25},{25,17},{2,10},{10... | collective-permute-start | bytes 884744 | tf_op jit(solution)/shard_map/ppermute | solution.py:31
  105.6 9.2 %collective-permute-start.32 = (bf16[2,96,768]{2,1,0:T(8,128)(2,1)S(1)}, bf16[2,96,768]{2,1,0:T(8,128)(2,1)S(1)}, u32[]{:S(2)}, u32[]{:S(2)}) collective-permute-start(bf16[2,96,768]{2,1,0:T(8,128)(2,1)S(1)} %get-tuple-element.325), channel_id=1, source_target_pairs={{0,16},{8,24},{16,0},{24,8},{1,17},{9,25},{17,1},{25,9},{2,18},{10... | collective-permute-start | bytes 884744 | tf_op jit(solution)/shard_map/ppermute | solution.py:31
  108.0 8.7 %collective-permute-start.34 = (bf16[2,4,24,640]{3,2,1,0:T(8,128)(2,1)S(1)}, bf16[2,4,24,640]{3,2,1,0:T(8,128)(2,1)S(1)}, u32[]{:S(2)}, u32[]{:S(2)}) collective-permute-start(bf16[2,4,24,640]{3,2,1,0:T(8,128)(2,1)S(1)} %get-tuple-element.332), channel_id=1, source_target_pairs={{0,2},{1,3},{2,0},{3,1},{4,6},{5,7},{6,4},{7,5},{8,10},{9,11},{10,... | collective-permute-start | bytes 737288 | tf_op jit(solution)/shard_map/ppermute | solution.py:31
  109.6 19.5 %collective-permute-start.36 = (bf16[256,576]{1,0:T(8,128)(2,1)S(1)}, bf16[256,576]{1,0:T(8,128)(2,1)S(1)}, u32[]{:S(2)}, u32[]{:S(2)}) collective-permute-start(bf16[256,576]{1,0:T(8,128)(2,1)S(1)} %get-tuple-element.285.refs_15_), channel_id=1, source_target_pairs={{0,8},{8,0},{16,24},{24,16},{1,9},{9,1},{17,25},{25,17},{2,10},{10... | collective-permute-start | bytes 884744 | tf_op jit(solution)/shard_map/ppermute | solution.py:31
  111.2 19.3 %collective-permute-start.37 = (bf16[256,576]{1,0:T(8,128)(2,1)S(1)}, bf16[256,576]{1,0:T(8,128)(2,1)S(1)}, u32[]{:S(2)}, u32[]{:S(2)}) collective-permute-start(bf16[256,576]{1,0:T(8,128)(2,1)S(1)} %get-tuple-element.286.refs_16_), channel_id=1, source_target_pairs={{0,16},{8,24},{16,0},{24,8},{1,17},{9,25},{17,1},{25,9},{2,18},{10... | collective-permute-start | bytes 884744 | tf_op jit(solution)/shard_map/ppermute | solution.py:31
  113.8 17.0 %collective-permute-start.38 = (bf16[256,576]{1,0:T(8,128)(2,1)S(1)}, bf16[256,576]{1,0:T(8,128)(2,1)S(1)}, u32[]{:S(2)}, u32[]{:S(2)}) collective-permute-start(bf16[256,576]{1,0:T(8,128)(2,1)S(1)} %get-tuple-element.287.refs_17_), channel_id=1, source_target_pairs={{0,24},{8,16},{16,8},{24,0},{1,25},{9,17},{17,9},{25,1},{2,26},{10... | collective-permute-start | bytes 884744 | tf_op jit(solution)/shard_map/ppermute | solution.py:31
  115.2 10.3 %collective-permute-start.42 = (bf16[2,96,768]{2,1,0:T(8,128)(2,1)S(1)}, bf16[2,96,768]{2,1,0:T(8,128)(2,1)S(1)}, u32[]{:S(2)}, u32[]{:S(2)}) collective-permute-start(bf16[2,96,768]{2,1,0:T(8,128)(2,1)S(1)} %get-tuple-element.275), channel_id=1, source_target_pairs={{0,2},{1,3},{2,0},{3,1},{4,6},{5,7},{6,4},{7,5},{8,10},{9,11},{10,... | collective-permute-start | bytes 884744 | tf_op jit(solution)/shard_map/ppermute | solution.py:31
  116.8 14.0 %copy-start.5 = (bf16[768,768]{1,0:T(8,128)(2,1)S(1)}, bf16[768,768]{1,0:T(8,128)(2,1)}, u32[]{:S(2)}) copy-start(bf16[768,768]{1,0:T(8,128)(2,1)} %refs_1_.5) | copy-start | bytes 3538948
  117.0 9.9 %collective-permute-start.35 = (bf16[1,4,24,640]{3,2,1,0:T(8,128)(2,1)S(1)}, bf16[1,4,24,640]{3,2,1,0:T(8,128)(2,1)S(1)}, u32[]{:S(2)}, u32[]{:S(2)}) collective-permute-start(bf16[1,4,24,640]{3,2,1,0:T(8,128)(2,1)S(1)} %pad_maximum_fusion.2), channel_id=1, source_target_pairs={{0,4},{1,5},{2,6},{3,7},{4,0},{5,1},{6,2},{7,3},{8,12},{9,13},{10,... | collective-permute-start | bytes 368648 | tf_op jit(solution)/shard_map/ppermute | solution.py:31
  125.6 9.8 %collective-permute-start.43 = (bf16[1,96,768]{2,1,0:T(8,128)(2,1)S(1)}, bf16[1,96,768]{2,1,0:T(8,128)(2,1)S(1)}, u32[]{:S(2)}, u32[]{:S(2)}) collective-permute-start(bf16[1,96,768]{2,1,0:T(8,128)(2,1)S(1)} %get-tuple-element.328), channel_id=1, source_target_pairs={{0,4},{1,5},{2,6},{3,7},{4,0},{5,1},{6,2},{7,3},{8,12},{9,13},{10,... | collective-permute-start | bytes 442376 | tf_op jit(solution)/shard_map/ppermute | solution.py:31
  127.2 7.1 %collective-permute-start.41 = (bf16[24,640]{1,0:T(8,128)(2,1)S(1)}, bf16[24,640]{1,0:T(8,128)(2,1)S(1)}, u32[]{:S(2)}, u32[]{:S(2)}) collective-permute-start(bf16[24,640]{1,0:T(8,128)(2,1)S(1)} %get-tuple-element.336), channel_id=1, source_target_pairs={{0,24},{8,16},{16,8},{24,0},{1,25},{9,17},{17,9},{25,1},{2,26},{10... | collective-permute-start | bytes 92168 | tf_op jit(solution)/shard_map/ppermute | solution.py:31
  129.0 5.3 %collective-permute-start.40 = (bf16[24,640]{1,0:T(8,128)(2,1)S(1)}, bf16[24,640]{1,0:T(8,128)(2,1)S(1)}, u32[]{:S(2)}, u32[]{:S(2)}) collective-permute-start(bf16[24,640]{1,0:T(8,128)(2,1)S(1)} %get-tuple-element.337), channel_id=1, source_target_pairs={{0,16},{8,24},{16,0},{24,8},{1,17},{9,25},{17,1},{25,9},{2,18},{10... | collective-permute-start | bytes 92168 | tf_op jit(solution)/shard_map/ppermute | solution.py:31
  130.5 3.9 %collective-permute-start.39 = (bf16[24,640]{1,0:T(8,128)(2,1)S(1)}, bf16[24,640]{1,0:T(8,128)(2,1)S(1)}, u32[]{:S(2)}, u32[]{:S(2)}) collective-permute-start(bf16[24,640]{1,0:T(8,128)(2,1)S(1)} %get-tuple-element.338), channel_id=1, source_target_pairs={{0,8},{8,0},{16,24},{24,16},{1,9},{9,1},{17,25},{25,17},{2,10},{10... | collective-permute-start | bytes 92168 | tf_op jit(solution)/shard_map/ppermute | solution.py:31
  (6 other events, 17.6 us)

commit v3 on v2

--- a/solution.py
+++ b/solution.py
@@ -713,7 +713,8 @@
         return list(got[:n_seg]), got[n_seg]
 
     def trade(blocks):
-        return [blocks[0]] + [swap(blocks[m], "seg", m) for m in others]
+        came = {m: swap(blocks[m], "seg", m) for m in reversed(others)}
+        return [blocks[0]] + [came[m] for m in others]
 
     weights = (vecs, output_proj, expand_proj, reduce_proj)
     each = wide // (n_seg * n_doc)

time: 136 us -> 136 us (level)
  no operation moved by 1% of the time
where the time goes in v3:
time: 136 us
  Pallas kernels  52.5 us (39%)
  starting transfers between devices  47 us (35%)
  waiting for transfers between devices  30.2 us (22%)
  local copies, waits for them, and re-layouts  2.74 us (2%)
  other arithmetic  2.59 us (2%)
    pallas_call x21, Pallas kernels, call(): pl.pallas_call(body, out_shape=[o if i in far_out else pltpu.VMEM(o.shape...  52.5 us
    ppermute x44, starting transfers between devices, swap(): lax.ppermute(block, axis, [(i, i ^ mask) for i in range(lax.axis_size(axi...  47 us
    ppermute x44, waiting for transfers between devices, swap(): lax.ppermute(block, axis, [(i, i ^ mask) for i in range(lax.axis_size(axi...  30.2 us
  transfers between devices with their start and end apart: 44, of which 22 were waited for; matrix products, arithmetic and copies ran while one was open for 2% of the time, Pallas kernels for 29%

profile of v3, /device:TPU:0, one launch (start us, length us, event | category | flops | bytes accessed | tf_op | source)
XLA Modules:
  0.0 136.1 jit_solution(805553288222789800)
XLA Ops:
  0.7 1.1 slice_bitcast_fusion
  1.8 4.0 %collective-permute-start.2 = (bf16[128,768]{1,0:T(8,128)(2,1)S(1)}, bf16[128,768]{1,0:T(8,128)(2,1)S(1)}, u32[]{:S(2)}, u32[]{:S(2)}) collective-permute-start(bf16[128,768]{1,0:T(8,128)(2,1)S(1)} %get-tuple-element.334.refs_2_.refs_4_.refs_6_), channel_id=1, source_target_pairs={{0,24},{8,16},{16,8},{24,0},{1,25},{9,17},{17,9},{25,1},{2,26},{10... | collective-permute-start | bytes 589832 | tf_op jit(solution)/shard_map/ppermute | solution.py:31
  8.3 3.1 %shard_map.331 = (bf16[768,576]{1,0:T(8,128)(2,1)S(1)}, f32[1,576]{1,0:T(1,128)S(1)}, f32[16,768]{1,0:T(8,128)S(1)}) custom-call(bf16[768,768]{1,0:T(8,128)(2,1)} %refs_1_.5, bf16[768,768]{1,0:T(8,128)(2,1)} %refs_2_.7, bf16[768,768]{1,0:T(8,128)(2,1)} %refs_3_.3, f32[768]{0:T(1024)} %refs_3_.2, f32[768]{0:T(1024)} %refs_4_.1, f32[768]{0:T(1024)} %refs_5_.3, ...), custom_call_target="tpu_custom_call" | custom-call | bytes 12000000 | tf_op jit(solution)/shard_map/pallas_call | solution.py:75
  11.5 3.0 %collective-permute-start.5 = (bf16[128,768]{1,0:T(8,128)(2,1)S(1)}, bf16[128,768]{1,0:T(8,128)(2,1)S(1)}, u32[]{:S(2)}, u32[]{:S(2)}) collective-permute-start(bf16[128,768]{1,0:T(8,128)(2,1)S(1)} %get-tuple-element.170.refs_2_.refs_4_.refs_10_), channel_id=1, source_target_pairs={{0,24},{8,16},{16,8},{24,0},{1,25},{9,17},{17,9},{25,1},{2,26},{10... | collective-permute-start | bytes 589832 | tf_op jit(solution)/shard_map/ppermute | solution.py:31
  16.6 3.8 %shard_map.334 = (bf16[72,384]{1,0:T(8,128)(2,1)S(1)}, bf16[72,384]{1,0:T(8,128)(2,1)S(1)}, bf16[72,384]{1,0:T(8,128)(2,1)S(1)}, bf16[72,384]{1,0:T(8,128)(2,1)S...) custom-call(s32[8,128]{1,0:T(8,128)S(1)} %shard_map.332.refs_0_, bf16[512,576]{1,0:T(8,128)(2,1)S(1)} %shard_map.333.refs_1_, ...), custom_call_target="tpu_custom_call" | custom-call | bytes 24000000 | tf_op jit(solution)/shard_map/pallas_call | solution.py:75
  20.5 1.4 %collective-permute-start.6 = (bf16[72,384]{1,0:T(8,128)(2,1)S(1)}, bf16[72,384]{1,0:T(8,128)(2,1)S(1)}, u32[]{:S(2)}, u32[]{:S(2)}) collective-permute-start(bf16[72,384]{1,0:T(8,128)(2,1)S(1)} %get-tuple-element.176), channel_id=1, source_target_pairs={{0,8},{8,0},{16,24},{24,16},{1,9},{9,1},{17,25},{25,17},{2,10},{10... | collective-permute-start | bytes 165896 | tf_op jit(solution)/shard_map/ppermute | solution.py:31
  21.9 1.2 collective-permute-start.7
  25.0 1.4 %collective-permute-done.7.refs_2_ = bf16[72,384]{1,0:T(8,128)(2,1)S(1)} collective-permute-done((bf16[72,384]{1,0:T(8,128)(2,1)S(1)}, bf16[72,384]{1,0:T(8,128)(2,1)S(1)}, u32[]{:S(2)}, u32[]{:S(2)}) %collective-permute-start.7) | collective-permute-done | bytes 55328 | tf_op jit(solution)/shard_map/ppermute | solution.py:31
  26.4 1.8 %collective-permute-done.8.refs_3_ = bf16[72,384]{1,0:T(8,128)(2,1)S(1)} collective-permute-done((bf16[72,384]{1,0:T(8,128)(2,1)S(1)}, bf16[72,384]{1,0:T(8,128)(2,1)S(1)}, u32[]{:S(2)}, u32[]{:S(2)}) %collective-permute-start.8) | collective-permute-done | bytes 55328 | tf_op jit(solution)/shard_map/ppermute | solution.py:31
  28.2 4.6 %shard_map.336 = (f32[144,768]{1,0:T(8,128)S(1)}, f32[144,128]{1,0:T(8,128)S(1)}, f32[144,3072]{1,0:T(8,128)S(1)}, f32[144,768]{1,0:T(8,128)S(1)}, bf16[128,768]...) custom-call(bf16[72,384]{1,0:T(8,128)(2,1)S(1)} %get-tuple-element.1, ...), custom_call_target="tpu_custom_call" | custom-call | bytes 24000000 | tf_op jit(solution)/shard_map/pallas_call | solution.py:75
  32.9 3.1 %shard_map.337 = (bf16[64,384]{1,0:T(8,128)(2,1)S(1)}, bf16[64,384]{1,0:T(8,128)(2,1)S(1)}, bf16[64,384]{1,0:T(8,128)(2,1)S(1)}, bf16[64,384]{1,0:T(8,128)(2,1)S...) custom-call(s32[8,128]{1,0:T(8,128)S(1)} %shard_map.332.refs_0_, ...), custom_call_target="tpu_custom_call" | custom-call | bytes 24000000 | tf_op jit(solution)/shard_map/pallas_call | solution.py:75
  36.0 0.9 collective-permute-start.10
  37.4 2.1 %collective-permute-start.12 = (bf16[64,384]{1,0:T(8,128)(2,1)S(1)}, bf16[64,384]{1,0:T(8,128)(2,1)S(1)}, u32[]{:S(2)}, u32[]{:S(2)}) collective-permute-start(bf16[64,384]{1,0:T(8,128)(2,1)S(1)} %get-tuple-element.188), channel_id=1, source_target_pairs={{0,24},{8,16},{16,8},{24,0},{1,25},{9,17},{17,9},{25,1},{2,26},{10... | collective-permute-start | bytes 147464 | tf_op jit(solution)/shard_map/ppermute | solution.py:31
  40.2 1.4 %collective-permute-done.11.refs_2_ = bf16[64,384]{1,0:T(8,128)(2,1)S(1)} collective-permute-done((bf16[64,384]{1,0:T(8,128)(2,1)S(1)}, bf16[64,384]{1,0:T(8,128)(2,1)S(1)}, u32[]{:S(2)}, u32[]{:S(2)}) %collective-permute-start.11) | collective-permute-done | bytes 49184 | tf_op jit(solution)/shard_map/ppermute | solution.py:31
  42.4 3.0 %shard_map.338 = (f32[128,768]{1,0:T(8,128)S(1)}, f32[128,128]{1,0:T(8,128)S(1)}, f32[128,3072]{1,0:T(8,128)S(1)}, f32[128,768]{1,0:T(8,128)S(1)}, bf16[128,768]...) custom-call(bf16[64,384]{1,0:T(8,128)(2,1)S(1)} %get-tuple-element.185.refs_0_, ...), custom_call_target="tpu_custom_call" | custom-call | bytes 24000000 | tf_op jit(solution)/shard_map/pallas_call | solution.py:75
  45.5 4.1 %shard_map.339 = (bf16[256,4608]{1,0:T(8,128)(2,1)S(1)}, f32[256,768]{1,0:T(8,128)S(1)}, f32[16,768]{1,0:T(8,128)S(1)}, bf16[128,384]{1,0:T(8,128)(2,1)S(1)}, bf...) custom-call(bf16[2,128,768]{2,1,0:T(8,128)(2,1)S(1)} %copy-done.6, ...), custom_call_target="tpu_custom_call" | custom-call | bytes 30000000 | tf_op jit(solution)/shard_map/pallas_call | solution.py:75
  50.1 1.4 %collective-permute-start.15 = (bf16[128,384]{1,0:T(8,128)(2,1)S(1)}, bf16[128,384]{1,0:T(8,128)(2,1)S(1)}, u32[]{:S(2)}, u32[]{:S(2)}) collective-permute-start(bf16[128,384]{1,0:T(8,128)(2,1)S(1)} %get-tuple-element.209), channel_id=1, source_target_pairs={{0,8},{8,0},{16,24},{24,16},{1,9},{9,1},{17,25},{25,17},{2,10},{10... | collective-permute-start | bytes 294920 | tf_op jit(solution)/shard_map/ppermute | solution.py:31
  51.6 1.2 collective-permute-start.16
  53.6 1.4 %collective-permute-done.13.refs_3_ = bf16[4,4,144,128]{3,2,1,0:T(8,128)(2,1)S(1)} collective-permute-done((bf16[4,4,144,128]{3,2,1,0:T(8,128)(2,1)S(1)}, bf16[4,4,144,128]{3,2,1,0:T(8,128)(2,1)S(1)}, u32[]{:S(2)}, u32[]{:S(2)}) %collective-permute-start.13) | collective-permute-done | bytes 589856 | tf_op jit(solution)/shard_map/ppermute | solution.py:31
  55.0 1.7 %shard_map.340 = (bf16[2,2,120,768]{3,2,1,0:T(8,128)(2,1)S(1)}, bf16[2,2,120,768]{3,2,1,0:T(8,128)(2,1)S(1)}, bf16[2,2,120,768]{3,2,1,0:T(8,128)(2,1)S(1)}, bf16[2,2,120,768]{3,2,1,0:T(8,128)(2,1)S(1)}) custom-call(bf16[4,4,144,128]{3,2,1,0:T(8,128)(2,1)S(1)} %get-tuple-element.180.refs_0_, bf16[4,4,144,128]{3,2,1,0:T(8,128)(2,1)S(1)} %get-tuple-element.189.refs_1_, ...), custom_call_target="tpu_custom_call" | custom-call | bytes 6000000 | tf_op jit(solution)/shard_map/pallas_call | solution.py:75
  57.2 1.1 collective-permute-done.17.refs_7_
  59.2 1.2 collective-permute-start.19
  60.4 5.0 %shard_map.341 = (bf16[128,576]{1,0:T(8,128)(2,1)S(1)}, bf16[128,576]{1,0:T(8,128)(2,1)S(1)}, bf16[128,576]{1,0:T(8,128)(2,1)S(1)}, bf16[128,576]{1,0:T(8,128)(2,1)S(1)}, bf16[16,576]{1,0:T(8,128)(2,1)S(1)}) custom-call(s32[8,128]{1,0:T(8,128)S(1)} %shard_map.332.refs_0_, bf16[512,576]{1,0:T(8,128)(2,1)S(1)} %shard_map.335.refs_1_, ...), custom_call_target="tpu_custom_call" | custom-call | bytes 24000000 | tf_op jit(solution)/shard_map/pallas_call | solution.py:75
  65.4 1.4 %collective-permute-start.22 = (bf16[16,384]{1,0:T(8,128)(2,1)S(1)}, bf16[16,384]{1,0:T(8,128)(2,1)S(1)}, u32[]{:S(2)}, u32[]{:S(2)}) collective-permute-start(bf16[16,384]{1,0:T(8,128)(2,1)S(1)} %slice.159.refs_1_), channel_id=1, source_target_pairs={{0,24},{8,16},{16,8},{24,0},{1,25},{9,17},{17,9},{25,1},{2,26},{10... | collective-permute-start | bytes 36872 | tf_op jit(solution)/shard_map/ppermute | solution.py:31
  66.9 1.2 collective-permute-start.21
  68.9 1.4 %shard_map.342 = (bf16[2,2,96,768]{3,2,1,0:T(8,128)(2,1)S(1)}, bf16[2,2,96,768]{3,2,1,0:T(8,128)(2,1)S(1)}, bf16[2,2,96,768]{3,2,1,0:T(8,128)(2,1)S(1)}, bf16[2,2,96,768]{3,2,1,0:T(8,128)(2,1)S(1)}) custom-call(bf16[4,4,144,128]{3,2,1,0:T(8,128)(2,1)S(1)} %get-tuple-element.180.refs_0_, bf16[4,4,144,128]{3,2,1,0:T(8,128)(2,1)S(1)} %get-tuple-element.189.refs_1_, ...), custom_call_target="tpu_custom_call" | custom-call | bytes 6000000 | tf_op jit(solution)/shard_map/pallas_call | solution.py:75
  70.3 6.5 %collective-permute-done.22.refs_4_ = bf16[16,384]{1,0:T(8,128)(2,1)S(1)} collective-permute-done((bf16[16,384]{1,0:T(8,128)(2,1)S(1)}, bf16[16,384]{1,0:T(8,128)(2,1)S(1)}, u32[]{:S(2)}, u32[]{:S(2)}) %collective-permute-start.22) | collective-permute-done | bytes 12320 | tf_op jit(solution)/shard_map/ppermute | solution.py:31
  77.4 1.3 collective-permute-start.23
  79.6 4.8 %shard_map.343 = (bf16[16,4608]{1,0:T(8,128)(2,1)S(1)}, f32[16,768]{1,0:T(8,128)S(1)}, f32[16,768]{1,0:T(8,128)S(1)}, f32[16,768]{1,0:T(8,128)S(1)}, bf16[16,192]{1,0:T(8,128)(2,1)S(1)}) custom-call(s32[8,128]{1,0:T(8,128)S(1)} %shard_map.332.refs_0_, bf16[16,384]{1,0:T(8,128)(2,1)S(1)} %slice.159.refs_1_, ...), custom_call_target="tpu_custom_call" | custom-call | bytes 18000000 | tf_op jit(solution)/shard_map/pallas_call | solution.py:75
  85.9 1.1 collective-permute-done.24.refs_7_
  87.4 1.6 %collective-permute-start.29 = (bf16[2,120,768]{2,1,0:T(8,128)(2,1)S(1)}, bf16[2,120,768]{2,1,0:T(8,128)(2,1)S(1)}, u32[]{:S(2)}, u32[]{:S(2)}) collective-permute-start(bf16[2,120,768]{2,1,0:T(8,128)(2,1)S(1)} %get-tuple-element.261), channel_id=1, source_target_pairs={{0,2},{1,3},{2,0},{3,1},{4,6},{5,7},{6,4},{7,5},{8,10},{9,11},{10,... | collective-permute-start | bytes 1105928 | tf_op jit(solution)/shard_map/ppermute | solution.py:31
  89.7 0.9 collective-permute-start.26
  90.6 5.9 %shard_map.345 = (bf16[256,576]{1,0:T(8,128)(2,1)S(1)}, bf16[256,576]{1,0:T(8,128)(2,1)S(1)}, bf16[256,576]{1,0:T(8,128)(2,1)S(1)}, bf16[256,576]{1,0:T(8,128)(2,1)S(1)}, bf16[16,576]{1,0:T(8,128)(2,1)S(1)}) custom-call(s32[8,128]{1,0:T(8,128)S(1)} %shard_map.332.refs_0_, bf16[512,576]{1,0:T(8,128)(2,1)S(1)} %shard_map.333.refs_1_, ...), custom_call_target="tpu_custom_call" | custom-call | bytes 24000000 | tf_op jit(solution)/shard_map/pallas_call | solution.py:75
  97.5 2.7 %collective-permute-start.31 = (bf16[1,120,768]{2,1,0:T(8,128)(2,1)S(1)}, bf16[1,120,768]{2,1,0:T(8,128)(2,1)S(1)}, u32[]{:S(2)}, u32[]{:S(2)}) collective-permute-start(bf16[1,120,768]{2,1,0:T(8,128)(2,1)S(1)} %get-tuple-element.327), channel_id=1, source_target_pairs={{0,4},{1,5},{2,6},{3,7},{4,0},{5,1},{6,2},{7,3},{8,12},{9,13},{10,... | collective-permute-start | bytes 552968 | tf_op jit(solution)/shard_map/ppermute | solution.py:31
  100.2 2.9 %shard_map.346 = (bf16[4,4,24,640]{3,2,1,0:T(8,128)(2,1)S(1)}, bf16[4,4,24,640]{3,2,1,0:T(8,128)(2,1)S(1)}) custom-call(s32[8,128]{1,0:T(8,128)S(1)} %shard_map.332.refs_0_, f32[16,768]{1,0:T(8,128)S(1)} %get-tuple-element.238.refs_1_, f32[16,768]{1,0:T(8,128)S(1)} %get-tuple-element.239.refs_2_, f32[16,768]{1,0:T(8,128)S(1)} %get-tuple-element.240.refs_3_, ...), custom_call_target="tpu_custom_call" | custom-call | bytes 18000000 | tf_op jit(solution)/shard_map/pallas_call | solution.py:75
  104.5 0.9 collective-permute-start.33
  106.4 1.1 collective-permute-done.31
  109.6 1.7 %collective-permute-start.36 = (bf16[256,576]{1,0:T(8,128)(2,1)S(1)}, bf16[256,576]{1,0:T(8,128)(2,1)S(1)}, u32[]{:S(2)}, u32[]{:S(2)}) collective-permute-start(bf16[256,576]{1,0:T(8,128)(2,1)S(1)} %get-tuple-element.285.refs_15_), channel_id=1, source_target_pairs={{0,8},{8,0},{16,24},{24,16},{1,9},{9,1},{17,25},{25,17},{2,10},{10... | collective-permute-start | bytes 884744 | tf_op jit(solution)/shard_map/ppermute | solution.py:31
  112.6 1.2 collective-permute-done.33.refs_7_
  113.8 1.0 collective-permute-start.38
  115.2 1.5 %collective-permute-start.42 = (bf16[2,96,768]{2,1,0:T(8,128)(2,1)S(1)}, bf16[2,96,768]{2,1,0:T(8,128)(2,1)S(1)}, u32[]{:S(2)}, u32[]{:S(2)}) collective-permute-start(bf16[2,96,768]{2,1,0:T(8,128)(2,1)S(1)} %get-tuple-element.275), channel_id=1, source_target_pairs={{0,2},{1,3},{2,0},{3,1},{4,6},{5,7},{6,4},{7,5},{8,10},{9,11},{10,... | collective-permute-start | bytes 884744 | tf_op jit(solution)/shard_map/ppermute | solution.py:31
  117.0 1.2 collective-permute-start.35
  118.3 7.1 %collective-permute-done.42 = bf16[2,96,768]{2,1,0:T(8,128)(2,1)S(1)} collective-permute-done((bf16[2,96,768]{2,1,0:T(8,128)(2,1)S(1)}, bf16[2,96,768]{2,1,0:T(8,128)(2,1)S(1)}, u32[]{:S(2)}, u32[]{:S(2)}) %collective-permute-start.42) | collective-permute-done | bytes 294944 | tf_op jit(solution)/shard_map/ppermute | solution.py:31
  125.6 1.3 collective-permute-start.43
  127.2 1.8 %collective-permute-start.41 = (bf16[24,640]{1,0:T(8,128)(2,1)S(1)}, bf16[24,640]{1,0:T(8,128)(2,1)S(1)}, u32[]{:S(2)}, u32[]{:S(2)}) collective-permute-start(bf16[24,640]{1,0:T(8,128)(2,1)S(1)} %get-tuple-element.336), channel_id=1, source_target_pairs={{0,24},{8,16},{16,8},{24,0},{1,25},{9,17},{17,9},{25,1},{2,26},{10... | collective-permute-start | bytes 92168 | tf_op jit(solution)/shard_map/ppermute | solution.py:31
  129.0 1.5 %collective-permute-start.40 = (bf16[24,640]{1,0:T(8,128)(2,1)S(1)}, bf16[24,640]{1,0:T(8,128)(2,1)S(1)}, u32[]{:S(2)}, u32[]{:S(2)}) collective-permute-start(bf16[24,640]{1,0:T(8,128)(2,1)S(1)} %get-tuple-element.337), channel_id=1, source_target_pairs={{0,16},{8,24},{16,0},{24,8},{1,17},{9,25},{17,1},{25,9},{2,18},{10... | collective-permute-start | bytes 92168 | tf_op jit(solution)/shard_map/ppermute | solution.py:31
  130.8 3.5 %shard_map.349 = bf16[2,128,768]{2,1,0:T(8,128)(2,1)} custom-call(f32[256,768]{1,0:T(8,128)S(1)} %get-tuple-element.283.refs_0_, bf16[768,768]{1,0:T(8,128)(2,1)S(1)} %copy-done.5, bf16[768,768]{1,0:T(8,128)(2,1)S(1)} %copy-done.3, bf16[768,768]{1,0:T(8,128)(2,1)S(1)} %copy-done.4, bf16[256,576]{1,0:T(8,128)(2,1)S(1)} %get-tuple-element.284.refs_14_.refs_4_, ...), custom_call_target="tpu_custom_call" | custom-call | bytes 9000000 | tf_op jit(solution)/shard_map/pallas_call | solution.py:75
  134.4 1.0 shard_map.350
  (105 shorter events, 25.2 us)
Async XLA Ops:
  0.7 27.6 %copy-start.2 = (bf16[768,768]{1,0:T(8,128)(2,1)S(1)}, bf16[768,768]{1,0:T(8,128)(2,1)}, u32[]{:S(2)}) copy-start(bf16[768,768]{1,0:T(8,128)(2,1)} %refs_12_.3) | copy-start | bytes 3538948
  1.8 13.1 %collective-permute-start.2 = (bf16[128,768]{1,0:T(8,128)(2,1)S(1)}, bf16[128,768]{1,0:T(8,128)(2,1)S(1)}, u32[]{:S(2)}, u32[]{:S(2)}) collective-permute-start(bf16[128,768]{1,0:T(8,128)(2,1)S(1)} %get-tuple-element.334.refs_2_.refs_4_.refs_6_), channel_id=1, source_target_pairs={{0,24},{8,16},{16,8},{24,0},{1,25},{9,17},{17,9},{25,1},{2,26},{10... | collective-permute-start | bytes 589832 | tf_op jit(solution)/shard_map/ppermute | solution.py:31
  5.8 9.6 %collective-permute-start.1 = (bf16[128,768]{1,0:T(8,128)(2,1)S(1)}, bf16[128,768]{1,0:T(8,128)(2,1)S(1)}, u32[]{:S(2)}, u32[]{:S(2)}) collective-permute-start(bf16[128,768]{1,0:T(8,128)(2,1)S(1)} %get-tuple-element.334.refs_2_.refs_4_.refs_6_), channel_id=1, source_target_pairs={{0,16},{8,24},{16,0},{24,8},{1,17},{9,25},{17,1},{25,9},{2,18},{10... | collective-permute-start | bytes 589832 | tf_op jit(solution)/shard_map/ppermute | solution.py:31
  6.3 9.6 %collective-permute-start = (bf16[128,768]{1,0:T(8,128)(2,1)S(1)}, bf16[128,768]{1,0:T(8,128)(2,1)S(1)}, u32[]{:S(2)}, u32[]{:S(2)}) collective-permute-start(bf16[128,768]{1,0:T(8,128)(2,1)S(1)} %get-tuple-element.334.refs_2_.refs_4_.refs_6_), channel_id=1, source_target_pairs={{0,8},{8,0},{16,24},{24,16},{1,9},{9,1},{17,25},{25,17},{2,10},{10... | collective-permute-start | bytes 589832 | tf_op jit(solution)/shard_map/ppermute | solution.py:31
  8.3 19.9 %copy-start.1 = (bf16[3072,768]{1,0:T(8,128)(2,1)S(1)}, bf16[3072,768]{1,0:T(8,128)(2,1)}, u32[]{:S(2)}) copy-start(bf16[3072,768]{1,0:T(8,128)(2,1)} %refs_14_.1) | copy-start | bytes 14155780
  11.5 11.7 %collective-permute-start.5 = (bf16[128,768]{1,0:T(8,128)(2,1)S(1)}, bf16[128,768]{1,0:T(8,128)(2,1)S(1)}, u32[]{:S(2)}, u32[]{:S(2)}) collective-permute-start(bf16[128,768]{1,0:T(8,128)(2,1)S(1)} %get-tuple-element.170.refs_2_.refs_4_.refs_10_), channel_id=1, source_target_pairs={{0,24},{8,16},{16,8},{24,0},{1,25},{9,17},{17,9},{25,1},{2,26},{10... | collective-permute-start | bytes 589832 | tf_op jit(solution)/shard_map/ppermute | solution.py:31
  14.4 9.6 %collective-permute-start.4 = (bf16[128,768]{1,0:T(8,128)(2,1)S(1)}, bf16[128,768]{1,0:T(8,128)(2,1)S(1)}, u32[]{:S(2)}, u32[]{:S(2)}) collective-permute-start(bf16[128,768]{1,0:T(8,128)(2,1)S(1)} %get-tuple-element.170.refs_2_.refs_4_.refs_10_), channel_id=1, source_target_pairs={{0,16},{8,24},{16,0},{24,8},{1,17},{9,25},{17,1},{25,9},{2,18},{10... | collective-permute-start | bytes 589832 | tf_op jit(solution)/shard_map/ppermute | solution.py:31
  14.9 9.3 %collective-permute-start.3 = (bf16[128,768]{1,0:T(8,128)(2,1)S(1)}, bf16[128,768]{1,0:T(8,128)(2,1)S(1)}, u32[]{:S(2)}, u32[]{:S(2)}) collective-permute-start(bf16[128,768]{1,0:T(8,128)(2,1)S(1)} %get-tuple-element.170.refs_2_.refs_4_.refs_10_), channel_id=1, source_target_pairs={{0,8},{8,0},{16,24},{24,16},{1,9},{9,1},{17,25},{25,17},{2,10},{10... | collective-permute-start | bytes 589832 | tf_op jit(solution)/shard_map/ppermute | solution.py:31
  15.8 12.4 %copy-start = (bf16[768,3072]{1,0:T(8,128)(2,1)S(1)}, bf16[768,3072]{1,0:T(8,128)(2,1)}, u32[]{:S(2)}) copy-start(bf16[768,3072]{1,0:T(8,128)(2,1)} %refs_13_.1) | copy-start | bytes 14155780
  20.5 4.6 %collective-permute-start.6 = (bf16[72,384]{1,0:T(8,128)(2,1)S(1)}, bf16[72,384]{1,0:T(8,128)(2,1)S(1)}, u32[]{:S(2)}, u32[]{:S(2)}) collective-permute-start(bf16[72,384]{1,0:T(8,128)(2,1)S(1)} %get-tuple-element.176), channel_id=1, source_target_pairs={{0,8},{8,0},{16,24},{24,16},{1,9},{9,1},{17,25},{25,17},{2,10},{10... | collective-permute-start | bytes 165896 | tf_op jit(solution)/shard_map/ppermute | solution.py:31
  21.9 4.5 %collective-permute-start.7 = (bf16[72,384]{1,0:T(8,128)(2,1)S(1)}, bf16[72,384]{1,0:T(8,128)(2,1)S(1)}, u32[]{:S(2)}, u32[]{:S(2)}) collective-permute-start(bf16[72,384]{1,0:T(8,128)(2,1)S(1)} %get-tuple-element.177), channel_id=1, source_target_pairs={{0,16},{8,24},{16,0},{24,8},{1,17},{9,25},{17,1},{25,9},{2,18},{10... | collective-permute-start | bytes 165896 | tf_op jit(solution)/shard_map/ppermute | solution.py:31
  23.2 5.1 %collective-permute-start.8 = (bf16[72,384]{1,0:T(8,128)(2,1)S(1)}, bf16[72,384]{1,0:T(8,128)(2,1)S(1)}, u32[]{:S(2)}, u32[]{:S(2)}) collective-permute-start(bf16[72,384]{1,0:T(8,128)(2,1)S(1)} %get-tuple-element.178), channel_id=1, source_target_pairs={{0,24},{8,16},{16,8},{24,0},{1,25},{9,17},{17,9},{25,1},{2,26},{10... | collective-permute-start | bytes 165896 | tf_op jit(solution)/shard_map/ppermute | solution.py:31
  32.8 6.7 %collective-permute-start.9 = (bf16[4,4,144,128]{3,2,1,0:T(8,128)(2,1)S(1)}, bf16[4,4,144,128]{3,2,1,0:T(8,128)(2,1)S(1)}, u32[]{:S(2)}, u32[]{:S(2)}) collective-permute-start(bf16[4,4,144,128]{3,2,1,0:T(8,128)(2,1)S(1)} %get-tuple-element.184), channel_id=1, source_target_pairs={{0,1},{1,0},{2,3},{3,2},{4,5},{5,4},{6,7},{7,6},{8,9},{9,8},{10,11... | collective-permute-start | bytes 1769480 | tf_op jit(solution)/shard_map/ppermute | solution.py:31
  36.0 4.2 %collective-permute-start.10 = (bf16[64,384]{1,0:T(8,128)(2,1)S(1)}, bf16[64,384]{1,0:T(8,128)(2,1)S(1)}, u32[]{:S(2)}, u32[]{:S(2)}) collective-permute-start(bf16[64,384]{1,0:T(8,128)(2,1)S(1)} %get-tuple-element.186), channel_id=1, source_target_pairs={{0,8},{8,0},{16,24},{24,16},{1,9},{9,1},{17,25},{25,17},{2,10},{10... | collective-permute-start | bytes 147464 | tf_op jit(solution)/shard_map/ppermute | solution.py:31
  37.0 4.6 %collective-permute-start.11 = (bf16[64,384]{1,0:T(8,128)(2,1)S(1)}, bf16[64,384]{1,0:T(8,128)(2,1)S(1)}, u32[]{:S(2)}, u32[]{:S(2)}) collective-permute-start(bf16[64,384]{1,0:T(8,128)(2,1)S(1)} %get-tuple-element.187), channel_id=1, source_target_pairs={{0,16},{8,24},{16,0},{24,8},{1,17},{9,25},{17,1},{25,9},{2,18},{10... | collective-permute-start | bytes 147464 | tf_op jit(solution)/shard_map/ppermute | solution.py:31
  37.4 5.0 %collective-permute-start.12 = (bf16[64,384]{1,0:T(8,128)(2,1)S(1)}, bf16[64,384]{1,0:T(8,128)(2,1)S(1)}, u32[]{:S(2)}, u32[]{:S(2)}) collective-permute-start(bf16[64,384]{1,0:T(8,128)(2,1)S(1)} %get-tuple-element.188), channel_id=1, source_target_pairs={{0,24},{8,16},{16,8},{24,0},{1,25},{9,17},{17,9},{25,1},{2,26},{10... | collective-permute-start | bytes 147464 | tf_op jit(solution)/shard_map/ppermute | solution.py:31
  49.6 5.4 %collective-permute-start.14 = (bf16[256,4608]{1,0:T(8,128)(2,1)S(1)}, bf16[256,4608]{1,0:T(8,128)(2,1)S(1)}, u32[]{:S(2)}, u32[]{:S(2)}) collective-permute-start(bf16[256,4608]{1,0:T(8,128)(2,1)S(1)} %get-tuple-element.202.refs_4_), channel_id=1, source_target_pairs={{0,1},{1,0},{2,3},{3,2},{4,5},{5,4},{6,7},{7,6},{8,9},{9,8},{10,11... | collective-permute-start | bytes 7077896 | tf_op jit(solution)/shard_map/ppermute | solution.py:31
  49.6 5.4 %collective-permute-start.13 = (bf16[4,4,144,128]{3,2,1,0:T(8,128)(2,1)S(1)}, bf16[4,4,144,128]{3,2,1,0:T(8,128)(2,1)S(1)}, u32[]{:S(2)}, u32[]{:S(2)}) collective-permute-start(bf16[4,4,144,128]{3,2,1,0:T(8,128)(2,1)S(1)} %get-tuple-element.200), channel_id=1, source_target_pairs={{0,1},{1,0},{2,3},{3,2},{4,5},{5,4},{6,7},{7,6},{8,9},{9,8},{10,11... | collective-permute-start | bytes 1769480 | tf_op jit(solution)/shard_map/ppermute | solution.py:31
  50.1 6.6 %collective-permute-start.15 = (bf16[128,384]{1,0:T(8,128)(2,1)S(1)}, bf16[128,384]{1,0:T(8,128)(2,1)S(1)}, u32[]{:S(2)}, u32[]{:S(2)}) collective-permute-start(bf16[128,384]{1,0:T(8,128)(2,1)S(1)} %get-tuple-element.209), channel_id=1, source_target_pairs={{0,8},{8,0},{16,24},{24,16},{1,9},{9,1},{17,25},{25,17},{2,10},{10... | collective-permute-start | bytes 294920 | tf_op jit(solution)/shard_map/ppermute | solution.py:31
  51.6 5.7 %collective-permute-start.16 = (bf16[128,384]{1,0:T(8,128)(2,1)S(1)}, bf16[128,384]{1,0:T(8,128)(2,1)S(1)}, u32[]{:S(2)}, u32[]{:S(2)}) collective-permute-start(bf16[128,384]{1,0:T(8,128)(2,1)S(1)} %get-tuple-element.210), channel_id=1, source_target_pairs={{0,16},{8,24},{16,0},{24,8},{1,17},{9,25},{17,1},{25,9},{2,18},{10... | collective-permute-start | bytes 294920 | tf_op jit(solution)/shard_map/ppermute | solution.py:31
  52.8 5.5 %collective-permute-start.17 = (bf16[128,384]{1,0:T(8,128)(2,1)S(1)}, bf16[128,384]{1,0:T(8,128)(2,1)S(1)}, u32[]{:S(2)}, u32[]{:S(2)}) collective-permute-start(bf16[128,384]{1,0:T(8,128)(2,1)S(1)} %get-tuple-element.211), channel_id=1, source_target_pairs={{0,24},{8,16},{16,8},{24,0},{1,25},{9,17},{17,9},{25,1},{2,26},{10... | collective-permute-start | bytes 294920 | tf_op jit(solution)/shard_map/ppermute | solution.py:31
  58.3 18.7 %collective-permute-start.18 = (bf16[2,2,120,768]{3,2,1,0:T(8,128)(2,1)S(1)}, bf16[2,2,120,768]{3,2,1,0:T(8,128)(2,1)S(1)}, u32[]{:S(2)}, u32[]{:S(2)}) collective-permute-start(bf16[2,2,120,768]{3,2,1,0:T(8,128)(2,1)S(1)} %get-tuple-element.220), channel_id=1, source_target_pairs={{0,8},{8,0},{16,24},{24,16},{1,9},{9,1},{17,25},{25,17},{2,10},{10... | collective-permute-start | bytes 2211848 | tf_op jit(solution)/shard_map/ppermute | solution.py:31
  59.2 17.9 %collective-permute-start.19 = (bf16[2,2,120,768]{3,2,1,0:T(8,128)(2,1)S(1)}, bf16[2,2,120,768]{3,2,1,0:T(8,128)(2,1)S(1)}, u32[]{:S(2)}, u32[]{:S(2)}) collective-permute-start(bf16[2,2,120,768]{3,2,1,0:T(8,128)(2,1)S(1)} %get-tuple-element.221), channel_id=1, source_target_pairs={{0,16},{8,24},{16,0},{24,8},{1,17},{9,25},{17,1},{25,9},{2,18},{10... | collective-permute-start | bytes 2211848 | tf_op jit(solution)/shard_map/ppermute | solution.py:31
  65.4 11.4 %collective-permute-start.22 = (bf16[16,384]{1,0:T(8,128)(2,1)S(1)}, bf16[16,384]{1,0:T(8,128)(2,1)S(1)}, u32[]{:S(2)}, u32[]{:S(2)}) collective-permute-start(bf16[16,384]{1,0:T(8,128)(2,1)S(1)} %slice.159.refs_1_), channel_id=1, source_target_pairs={{0,24},{8,16},{16,8},{24,0},{1,25},{9,17},{17,9},{25,1},{2,26},{10... | collective-permute-start | bytes 36872 | tf_op jit(solution)/shard_map/ppermute | solution.py:31
  66.9 10.2 %collective-permute-start.21 = (bf16[16,384]{1,0:T(8,128)(2,1)S(1)}, bf16[16,384]{1,0:T(8,128)(2,1)S(1)}, u32[]{:S(2)}, u32[]{:S(2)}) collective-permute-start(bf16[16,384]{1,0:T(8,128)(2,1)S(1)} %slice.159.refs_1_), channel_id=1, source_target_pairs={{0,16},{8,24},{16,0},{24,8},{1,17},{9,25},{17,1},{25,9},{2,18},{10... | collective-permute-start | bytes 36872 | tf_op jit(solution)/shard_map/ppermute | solution.py:31
  68.1 9.0 %collective-permute-start.20 = (bf16[16,384]{1,0:T(8,128)(2,1)S(1)}, bf16[16,384]{1,0:T(8,128)(2,1)S(1)}, u32[]{:S(2)}, u32[]{:S(2)}) collective-permute-start(bf16[16,384]{1,0:T(8,128)(2,1)S(1)} %slice.159.refs_1_), channel_id=1, source_target_pairs={{0,8},{8,0},{16,24},{24,16},{1,9},{9,1},{17,25},{25,17},{2,10},{10... | collective-permute-start | bytes 36872 | tf_op jit(solution)/shard_map/ppermute | solution.py:31
  77.4 8.4 %collective-permute-start.23 = (bf16[2,120,768]{2,1,0:T(8,128)(2,1)S(1)}, bf16[2,120,768]{2,1,0:T(8,128)(2,1)S(1)}, u32[]{:S(2)}, u32[]{:S(2)}) collective-permute-start(bf16[2,120,768]{2,1,0:T(8,128)(2,1)S(1)} %get-tuple-element.232), channel_id=1, source_target_pairs={{0,16},{8,24},{16,0},{24,8},{1,17},{9,25},{17,1},{25,9},{2,18},{10... | collective-permute-start | bytes 1105928 | tf_op jit(solution)/shard_map/ppermute | solution.py:31
  78.8 8.2 %collective-permute-start.24 = (bf16[2,120,768]{2,1,0:T(8,128)(2,1)S(1)}, bf16[2,120,768]{2,1,0:T(8,128)(2,1)S(1)}, u32[]{:S(2)}, u32[]{:S(2)}) collective-permute-start(bf16[2,120,768]{2,1,0:T(8,128)(2,1)S(1)} %get-tuple-element.233), channel_id=1, source_target_pairs={{0,8},{8,0},{16,24},{24,16},{1,9},{9,1},{17,25},{25,17},{2,10},{10... | collective-permute-start | bytes 1105928 | tf_op jit(solution)/shard_map/ppermute | solution.py:31
  84.5 2.5 %collective-permute-start.28 = (bf16[16,4608]{1,0:T(8,128)(2,1)S(1)}, bf16[16,4608]{1,0:T(8,128)(2,1)S(1)}, u32[]{:S(2)}, u32[]{:S(2)}) collective-permute-start(bf16[16,4608]{1,0:T(8,128)(2,1)S(1)} %get-tuple-element.246.refs_2_), channel_id=1, source_target_pairs={{0,1},{1,0},{2,3},{3,2},{4,5},{5,4},{6,7},{7,6},{8,9},{9,8},{10,11... | collective-permute-start | bytes 442376 | tf_op jit(solution)/shard_map/ppermute | solution.py:31
  84.5 2.4 %collective-permute-start.27 = (bf16[4,144,16]{2,1,0:T(8,128)(2,1)S(1)}, bf16[4,144,16]{2,1,0:T(8,128)(2,1)S(1)}, u32[]{:S(2)}, u32[]{:S(2)}) collective-permute-start(bf16[4,144,16]{2,1,0:T(8,128)(2,1)S(1)} %get-tuple-element.245), channel_id=1, source_target_pairs={{0,1},{1,0},{2,3},{3,2},{4,5},{5,4},{6,7},{7,6},{8,9},{9,8},{10,11... | collective-permute-start | bytes 55304 | tf_op jit(solution)/shard_map/ppermute | solution.py:31
  87.4 10.0 %collective-permute-start.29 = (bf16[2,120,768]{2,1,0:T(8,128)(2,1)S(1)}, bf16[2,120,768]{2,1,0:T(8,128)(2,1)S(1)}, u32[]{:S(2)}, u32[]{:S(2)}) collective-permute-start(bf16[2,120,768]{2,1,0:T(8,128)(2,1)S(1)} %get-tuple-element.261), channel_id=1, source_target_pairs={{0,2},{1,3},{2,0},{3,1},{4,6},{5,7},{6,4},{7,5},{8,10},{9,11},{10,... | collective-permute-start | bytes 1105928 | tf_op jit(solution)/shard_map/ppermute | solution.py:31
  89.0 14.4 %collective-permute-start.25 = (bf16[2,2,96,768]{3,2,1,0:T(8,128)(2,1)S(1)}, bf16[2,2,96,768]{3,2,1,0:T(8,128)(2,1)S(1)}, u32[]{:S(2)}, u32[]{:S(2)}) collective-permute-start(bf16[2,2,96,768]{3,2,1,0:T(8,128)(2,1)S(1)} %get-tuple-element.236), channel_id=1, source_target_pairs={{0,8},{8,0},{16,24},{24,16},{1,9},{9,1},{17,25},{25,17},{2,10},{10... | collective-permute-start | bytes 1769480 | tf_op jit(solution)/shard_map/ppermute | solution.py:31
  89.7 14.6 %collective-permute-start.26 = (bf16[2,2,96,768]{3,2,1,0:T(8,128)(2,1)S(1)}, bf16[2,2,96,768]{3,2,1,0:T(8,128)(2,1)S(1)}, u32[]{:S(2)}, u32[]{:S(2)}) collective-permute-start(bf16[2,2,96,768]{3,2,1,0:T(8,128)(2,1)S(1)} %get-tuple-element.237), channel_id=1, source_target_pairs={{0,16},{8,24},{16,0},{24,8},{1,17},{9,25},{17,1},{25,9},{2,18},{10... | collective-permute-start | bytes 1769480 | tf_op jit(solution)/shard_map/ppermute | solution.py:31
  97.5 10.0 %collective-permute-start.31 = (bf16[1,120,768]{2,1,0:T(8,128)(2,1)S(1)}, bf16[1,120,768]{2,1,0:T(8,128)(2,1)S(1)}, u32[]{:S(2)}, u32[]{:S(2)}) collective-permute-start(bf16[1,120,768]{2,1,0:T(8,128)(2,1)S(1)} %get-tuple-element.327), channel_id=1, source_target_pairs={{0,4},{1,5},{2,6},{3,7},{4,0},{5,1},{6,2},{7,3},{8,12},{9,13},{10,... | collective-permute-start | bytes 552968 | tf_op jit(solution)/shard_map/ppermute | solution.py:31
  103.1 4.4 %collective-permute-start.30 = (bf16[4,4,24,640]{3,2,1,0:T(8,128)(2,1)S(1)}, bf16[4,4,24,640]{3,2,1,0:T(8,128)(2,1)S(1)}, u32[]{:S(2)}, u32[]{:S(2)}) collective-permute-start(bf16[4,4,24,640]{3,2,1,0:T(8,128)(2,1)S(1)} %get-tuple-element.268), channel_id=1, source_target_pairs={{0,1},{1,0},{2,3},{3,2},{4,5},{5,4},{6,7},{7,6},{8,9},{9,8},{10,11... | collective-permute-start | bytes 1474568 | tf_op jit(solution)/shard_map/ppermute | solution.py:31
  104.5 9.3 %collective-permute-start.33 = (bf16[2,96,768]{2,1,0:T(8,128)(2,1)S(1)}, bf16[2,96,768]{2,1,0:T(8,128)(2,1)S(1)}, u32[]{:S(2)}, u32[]{:S(2)}) collective-permute-start(bf16[2,96,768]{2,1,0:T(8,128)(2,1)S(1)} %get-tuple-element.322), channel_id=1, source_target_pairs={{0,8},{8,0},{16,24},{24,16},{1,9},{9,1},{17,25},{25,17},{2,10},{10... | collective-permute-start | bytes 884744 | tf_op jit(solution)/shard_map/ppermute | solution.py:31
  105.6 9.2 %collective-permute-start.32 = (bf16[2,96,768]{2,1,0:T(8,128)(2,1)S(1)}, bf16[2,96,768]{2,1,0:T(8,128)(2,1)S(1)}, u32[]{:S(2)}, u32[]{:S(2)}) collective-permute-start(bf16[2,96,768]{2,1,0:T(8,128)(2,1)S(1)} %get-tuple-element.325), channel_id=1, source_target_pairs={{0,16},{8,24},{16,0},{24,8},{1,17},{9,25},{17,1},{25,9},{2,18},{10... | collective-permute-start | bytes 884744 | tf_op jit(solution)/shard_map/ppermute | solution.py:31
  108.0 8.7 %collective-permute-start.34 = (bf16[2,4,24,640]{3,2,1,0:T(8,128)(2,1)S(1)}, bf16[2,4,24,640]{3,2,1,0:T(8,128)(2,1)S(1)}, u32[]{:S(2)}, u32[]{:S(2)}) collective-permute-start(bf16[2,4,24,640]{3,2,1,0:T(8,128)(2,1)S(1)} %get-tuple-element.332), channel_id=1, source_target_pairs={{0,2},{1,3},{2,0},{3,1},{4,6},{5,7},{6,4},{7,5},{8,10},{9,11},{10,... | collective-permute-start | bytes 737288 | tf_op jit(solution)/shard_map/ppermute | solution.py:31
  109.6 19.5 %collective-permute-start.36 = (bf16[256,576]{1,0:T(8,128)(2,1)S(1)}, bf16[256,576]{1,0:T(8,128)(2,1)S(1)}, u32[]{:S(2)}, u32[]{:S(2)}) collective-permute-start(bf16[256,576]{1,0:T(8,128)(2,1)S(1)} %get-tuple-element.285.refs_15_), channel_id=1, source_target_pairs={{0,8},{8,0},{16,24},{24,16},{1,9},{9,1},{17,25},{25,17},{2,10},{10... | collective-permute-start | bytes 884744 | tf_op jit(solution)/shard_map/ppermute | solution.py:31
  111.2 19.3 %collective-permute-start.37 = (bf16[256,576]{1,0:T(8,128)(2,1)S(1)}, bf16[256,576]{1,0:T(8,128)(2,1)S(1)}, u32[]{:S(2)}, u32[]{:S(2)}) collective-permute-start(bf16[256,576]{1,0:T(8,128)(2,1)S(1)} %get-tuple-element.286.refs_16_), channel_id=1, source_target_pairs={{0,16},{8,24},{16,0},{24,8},{1,17},{9,25},{17,1},{25,9},{2,18},{10... | collective-permute-start | bytes 884744 | tf_op jit(solution)/shard_map/ppermute | solution.py:31
  113.8 17.0 %collective-permute-start.38 = (bf16[256,576]{1,0:T(8,128)(2,1)S(1)}, bf16[256,576]{1,0:T(8,128)(2,1)S(1)}, u32[]{:S(2)}, u32[]{:S(2)}) collective-permute-start(bf16[256,576]{1,0:T(8,128)(2,1)S(1)} %get-tuple-element.287.refs_17_), channel_id=1, source_target_pairs={{0,24},{8,16},{16,8},{24,0},{1,25},{9,17},{17,9},{25,1},{2,26},{10... | collective-permute-start | bytes 884744 | tf_op jit(solution)/shard_map/ppermute | solution.py:31
  115.2 10.3 %collective-permute-start.42 = (bf16[2,96,768]{2,1,0:T(8,128)(2,1)S(1)}, bf16[2,96,768]{2,1,0:T(8,128)(2,1)S(1)}, u32[]{:S(2)}, u32[]{:S(2)}) collective-permute-start(bf16[2,96,768]{2,1,0:T(8,128)(2,1)S(1)} %get-tuple-element.275), channel_id=1, source_target_pairs={{0,2},{1,3},{2,0},{3,1},{4,6},{5,7},{6,4},{7,5},{8,10},{9,11},{10,... | collective-permute-start | bytes 884744 | tf_op jit(solution)/shard_map/ppermute | solution.py:31
  116.8 14.0 %copy-start.5 = (bf16[768,768]{1,0:T(8,128)(2,1)S(1)}, bf16[768,768]{1,0:T(8,128)(2,1)}, u32[]{:S(2)}) copy-start(bf16[768,768]{1,0:T(8,128)(2,1)} %refs_1_.5) | copy-start | bytes 3538948
  117.0 9.9 %collective-permute-start.35 = (bf16[1,4,24,640]{3,2,1,0:T(8,128)(2,1)S(1)}, bf16[1,4,24,640]{3,2,1,0:T(8,128)(2,1)S(1)}, u32[]{:S(2)}, u32[]{:S(2)}) collective-permute-start(bf16[1,4,24,640]{3,2,1,0:T(8,128)(2,1)S(1)} %pad_maximum_fusion.2), channel_id=1, source_target_pairs={{0,4},{1,5},{2,6},{3,7},{4,0},{5,1},{6,2},{7,3},{8,12},{9,13},{10,... | collective-permute-start | bytes 368648 | tf_op jit(solution)/shard_map/ppermute | solution.py:31
  125.6 9.8 %collective-permute-start.43 = (bf16[1,96,768]{2,1,0:T(8,128)(2,1)S(1)}, bf16[1,96,768]{2,1,0:T(8,128)(2,1)S(1)}, u32[]{:S(2)}, u32[]{:S(2)}) collective-permute-start(bf16[1,96,768]{2,1,0:T(8,128)(2,1)S(1)} %get-tuple-element.328), channel_id=1, source_target_pairs={{0,4},{1,5},{2,6},{3,7},{4,0},{5,1},{6,2},{7,3},{8,12},{9,13},{10,... | collective-permute-start | bytes 442376 | tf_op jit(solution)/shard_map/ppermute | solution.py:31
  127.2 7.1 %collective-permute-start.41 = (bf16[24,640]{1,0:T(8,128)(2,1)S(1)}, bf16[24,640]{1,0:T(8,128)(2,1)S(1)}, u32[]{:S(2)}, u32[]{:S(2)}) collective-permute-start(bf16[24,640]{1,0:T(8,128)(2,1)S(1)} %get-tuple-element.336), channel_id=1, source_target_pairs={{0,24},{8,16},{16,8},{24,0},{1,25},{9,17},{17,9},{25,1},{2,26},{10... | collective-permute-start | bytes 92168 | tf_op jit(solution)/shard_map/ppermute | solution.py:31
  129.0 5.3 %collective-permute-start.40 = (bf16[24,640]{1,0:T(8,128)(2,1)S(1)}, bf16[24,640]{1,0:T(8,128)(2,1)S(1)}, u32[]{:S(2)}, u32[]{:S(2)}) collective-permute-start(bf16[24,640]{1,0:T(8,128)(2,1)S(1)} %get-tuple-element.337), channel_id=1, source_target_pairs={{0,16},{8,24},{16,0},{24,8},{1,17},{9,25},{17,1},{25,9},{2,18},{10... | collective-permute-start | bytes 92168 | tf_op jit(solution)/shard_map/ppermute | solution.py:31
  130.5 3.9 %collective-permute-start.39 = (bf16[24,640]{1,0:T(8,128)(2,1)S(1)}, bf16[24,640]{1,0:T(8,128)(2,1)S(1)}, u32[]{:S(2)}, u32[]{:S(2)}) collective-permute-start(bf16[24,640]{1,0:T(8,128)(2,1)S(1)} %get-tuple-element.338), channel_id=1, source_target_pairs={{0,8},{8,0},{16,24},{24,16},{1,9},{9,1},{17,25},{25,17},{2,10},{10... | collective-permute-start | bytes 92168 | tf_op jit(solution)/shard_map/ppermute | solution.py:31
  (6 other events, 17.6 us)
